TPU v7x, 512 devices: a whole 4x4x16 slice. The times are simulated.
512 devices in a mesh: grp: 16 (over y, x), tp: 32 (over z, core).
Axes of the slice: x: 4, y: 4, z: 16, core: 2. Of those that a mesh axis runs over, the one named last changes fastest.
Arguments:
- tokens: bfloat16 [6144, 5120], P('grp'), may hold values from -36 to 36
- trainer_panels: bfloat16 [64, 5120, 128], P('tp', 'grp'), may hold values from -0.078125 to 0.078125
- panel_home: int32 [48], replicated, may hold values from 0 to 63, as said below
- lengths: int32 [16, 4], P('grp'), may hold values from 1 to 192, 384 in all within a row
Outputs:
- context: float32 [6144, 4096], P(('grp', 'tp'))
Inputs may be any that keep to these rules, and one draw needn't show every extreme that they name: `panel_home`: entries are distinct; entry p is 2 times the tp index of the trainer device that holds panel p, plus the panel's slot on that device. Panels 0 to 31 are query heads, the next 8 key heads, the last 8 value heads. Some trainer device holds 2 panels.
All inputs are finite; a program needn't handle non-finite values.
Results may differ from a plain program's by a relative error of at most 0.012.
Values may be sent and summed in bfloat16 or wider, within the bound.
A program may use at most 64 MiB of HBM per device.

v0:
```python
import jax
import jax.numpy as jnp
from jax import lax
from jax.sharding import PartitionSpec as P


def on_device(tokens, trainer_panels, panel_home, lengths):
    tp_count = lax.axis_size("tp")
    member_id = lax.axis_index("tp")
    kv_count = (panel_home.shape[0] - tp_count) // 2
    group_size = tp_count // kv_count
    slot_count = trainer_panels.shape[0]
    head_dim = trainer_panels.shape[2]
    needed = jnp.stack(
        [
            member_id,
            tp_count + member_id // group_size,
            tp_count + kv_count + member_id // group_size,
        ]
    )
    wanted = panel_home[needed]
    peer_ids = jnp.arange(tp_count, dtype=jnp.int32)
    reader_need = jnp.stack(
        [peer_ids, tp_count + peer_ids // group_size, tp_count + kv_count + peer_ids // group_size],
        axis=1,
    )
    reader_home = panel_home[reader_need]
    local_slot = reader_home - member_id * slot_count
    owned_here = (local_slot >= 0) & (local_slot < slot_count)
    picked = trainer_panels[jnp.clip(local_slot, 0, slot_count - 1)]
    outbound = jnp.where(owned_here[:, :, None, None], picked, jnp.zeros_like(picked))
    arrived = lax.all_to_all(outbound, "tp", split_axis=0, concat_axis=0, tiled=True)
    source = wanted // slot_count
    selected = jnp.stack([arrived[source[need_pos], need_pos] for need_pos in range(3)], axis=1)
    full_panels = lax.all_gather(selected, "grp", axis=0, tiled=True)
    weights = full_panels.reshape(full_panels.shape[0], 3 * head_dim)
    projected = jnp.dot(tokens, weights, preferred_element_type=jnp.float32).astype(jnp.bfloat16)
    query_rows = projected[:, :head_dim]
    key_rows = projected[:, head_dim : 2 * head_dim]
    value_rows = projected[:, 2 * head_dim :]
    seq_total = query_rows.shape[0]
    position = jnp.arange(seq_total, dtype=jnp.int32)
    bounds = jnp.cumsum(lengths[0])
    segment = jnp.sum((position[:, None] >= bounds[None, :]).astype(jnp.int32), axis=1)
    allowed = (segment[:, None] == segment[None, :]) & (position[None, :] <= position[:, None])
    score_scale = head_dim ** (-0.5)
    scores = (
        lax.dot_general(
            query_rows, key_rows, (((1,), (1,)), ((), ())), preferred_element_type=jnp.float32
        )
        * score_scale
    )
    masked = jnp.where(allowed, scores, -jnp.inf)
    row_peak = jnp.max(masked, axis=1, keepdims=True)
    row_exp = jnp.exp(masked - row_peak)
    attn_probs = (row_exp / jnp.sum(row_exp, axis=1, keepdims=True)).astype(jnp.bfloat16)
    context = jnp.dot(attn_probs, value_rows, preferred_element_type=jnp.float32)
    return lax.all_to_all(context, "tp", split_axis=0, concat_axis=1, tiled=True)


def solution(mesh):
    placed = (P("grp", None), P("tp", "grp", None), P(), P("grp", None))
    return jax.shard_map(
        on_device, mesh=mesh, in_specs=placed, out_specs=P(("grp", "tp"), None), check_vma=False
    )
```

profile of v0, /device:TPU:1, one launch (start us, length us, event | category | flops | bytes accessed | tf_op | source)
XLA Modules:
  0.0 502.3 jit_solution(18027963017694480111)
XLA Ops:
  6.5 0.0 copy-start
  6.5 0.0 copy-start.1
  6.6 0.1 copy.31
  6.7 0.1 reshape.305
  6.8 0.4 copy-done.1
  7.2 1.2 gather_fusion
  8.5 0.1 min.12
  8.6 0.1 copy.32
  8.7 0.1 copy.35
  8.8 0.1 reshape.313
  8.9 0.1 reshape.339
  9.0 0.0 copy-done
  9.0 6.4 %gather_fusion.1 = bf16[96,320,128]{2,1,0:T(8,128)(2,1)} fusion(bf16[2,320,128]{2,1,0:T(8,128)(2,1)S(1)} %copy-done, s32[1024]{0:T(1024)S(1)} %pad_clamp_fusion.1), kind=kCustom, calls=%fused_computation.1 | custom fusion | bytes 15729024 | tf_op jit(solution)/shard_map/gather | solution.py:30
  15.4 6.9 %broadcast_select_fusion = bf16[32,3,320,128]{3,2,1,0:T(8,128)(2,1)} fusion(bf16[32,3,320,128]{3,2,1,0:T(8,128)(2,1)} %bitcast.34, pred[32,3]{1,0:T(8,128)(4,1)S(1)} %reshape.339), kind=kLoop, calls=%fused_computation.3 | loop fusion | flops 3932160 | bytes 15728736 | tf_op jit(solution)/shard_map/jit(_where)/select_n | solution.py:31
  22.3 0.0 copy-start.2
  22.3 17.1 %all-to-all-start = ((bf16[32,3,320,128]{3,2,1,0:T(8,128)(2,1)}), bf16[32,3,320,128]{3,2,1,0:T(8,128)(2,1)}, u32[]{:S(2)}, u32[]{:S(2)}) async-start(bf16[32,3,320,128]{3,2,1,0:T(8,128)(2,1)} %broadcast_select_fusion), calls=%async_computation | async-start | bytes 15728640 | tf_op jit(solution)/shard_map/all_to_all | solution.py:32
  39.5 0.0 all-gather.2.cloned.1.call-start
  39.6 0.1 fusion.8
  39.6 0.6 gather_fusion.2
  40.3 0.7 fusion.9
  46.5 332.2 %all-to-all-done = bf16[32,3,320,128]{3,2,1,0:T(8,128)(2,1)} async-done(((bf16[32,3,320,128]{3,2,1,0:T(8,128)(2,1)}), bf16[32,3,320,128]{3,2,1,0:T(8,128)(2,1)}, u32[]{:S(2)}, u32[]{:S(2)}) %all-to-all-start) | async-done | bytes 7864352 | tf_op jit(solution)/shard_map/all_to_all | solution.py:32
  378.7 1.0 dynamic-slice_bitcast_fusion.2
  379.7 0.7 pad_maximum_fusion
  380.4 0.0 all-gather.2.cloned.1.call-update
  380.4 0.0 copy-done.2
  380.4 0.2 reduce-window.8
  380.6 0.1 convert_reduce_fusion
  380.7 66.1 %all-gather.2.cloned.1.call-done = bf16[5120,3,128]{2,0,1:T(8,128)(2,1)} async-done(((bf16[320,3,128]{2,0,1:T(8,128)(2,1)}), bf16[5120,3,128]{2,0,1:T(8,128)(2,1)}) %all-gather.2.cloned.1.call-update) | async-done | bytes 3932176 | tf_op jit(solution)/shard_map/all_gather | solution.py:35
  446.8 6.3 %copy.36 = bf16[5120,3,128]{0,2,1:T(8,128)(2,1)} copy(bf16[5120,3,128]{2,0,1:T(8,128)(2,1)} %all-gather.2.cloned.1.call-done) | data formatting | bytes 7864320 | tf_op jit(solution)/shard_map/all_gather | solution.py:35
  453.2 5.5 %fusion.1 = bf16[384,384]{0,1:T(8,128)(2,1)S(1)} fusion(bf16[5120,384]{0,1:T(8,128)(2,1)} %bitcast.35, bf16[384,5120]{1,0:T(8,128)(2,1)} %param.4), kind=kOutput, calls=%fused_computation.7 | convolution fusion | flops 1510096896 | bytes 8159232 | tf_op jit(solution)/shard_map/dot_general | solution.py:37
  458.7 0.3 fusion.10
  459.0 0.1 fusion.3
  459.1 0.3 fusion.4
  459.5 35.0 %all_to_all.24 = f32[32,12,128]{2,1,0:T(8,128)S(1)} all-to-all(f32[32,12,128]{2,1,0:T(8,128)S(1)} %all_to_all.18), channel_id=1, replica_groups=mesh['grp'=16,'tp'=32] {'tp'}, dimensions={0} | all-to-all | bytes 393216 | tf_op jit(solution)/shard_map/all_to_all | solution.py:58
  494.5 0.1 copy.37
  494.5 0.9 copy.38
  (12 shorter events, 0.1 us)
Async XLA Ops:
  6.5 2.5 copy-start
  6.5 0.7 copy-start.1
  22.3 358.1 %copy-start.2 = (s32[1,4]{1,0:T(1,128)S(1)}, s32[1,4]{1,0:T(1,128)}, u32[]{:S(2)}) copy-start(s32[1,4]{1,0:T(1,128)} %param.7) | copy-start | bytes 52
  22.3 356.4 %all-to-all-start = ((bf16[32,3,320,128]{3,2,1,0:T(8,128)(2,1)}), bf16[32,3,320,128]{3,2,1,0:T(8,128)(2,1)}, u32[]{:S(2)}, u32[]{:S(2)}) async-start(bf16[32,3,320,128]{3,2,1,0:T(8,128)(2,1)} %broadcast_select_fusion), calls=%async_computation | async-start | bytes 15728640 | tf_op jit(solution)/shard_map/all_to_all | solution.py:32
  39.5 407.3 %all-gather.2.cloned.1.call-start = ((), (), s32[]{:S(2)}) async-start(), calls=%async_computation.2 | async-start | bytes 4177920 | tf_op jit(solution)/shard_map/all_gather | solution.py:35
Sparse Core Ops, SparseCore 0:
  380.5 66.2 all-gather.1
where the time goes:
time: 503 us; the launch traced here: 502 us
  waiting for transfers between devices  398 us (79%)
  blocking collectives  35 us (7%)
  between operations  19.1 us (4%)
  local copies, waits for them, and re-layouts  18.3 us (4%)
  starting transfers between devices  17.2 us (3%)
  other arithmetic  8.16 us (2%)
  matrix products  6.13 us (1%)
    all_to_all x1, waiting for transfers between devices, on_device(): lax.all_to_all(outbound, 'tp', split_axis=0, concat_axis=0, tiled=True)  332 us
    all_gather x1, waiting for transfers between devices, on_device(): full_panels = lax.all_gather(selected, 'grp', axis=0, tiled=True)  66.1 us
    all_to_all x1, blocking collectives, on_device(): lax.all_to_all(context, 'tp', split_axis=0, concat_axis=1, tiled=True)  35 us
    all_to_all x1, starting transfers between devices, on_device(): lax.all_to_all(outbound, 'tp', split_axis=0, concat_axis=0, tiled=True)  17.1 us
  transfers between devices with their start and end apart: 2, of which 2 were waited for; matrix products, arithmetic and copies ran while one was open for 0% of the time, Pallas kernels for 0%

commit v1 on v0

v1 whole, which is shorter than its diff:
```python
import jax
import jax.numpy as jnp
from jax import lax
from jax.sharding import PartitionSpec as P


def on_device(tokens, trainer_panels, panel_home, lengths):
    tp_count = lax.axis_size("tp")
    grp_count = lax.axis_size("grp")
    member_id = lax.axis_index("tp")
    kv_count = (panel_home.shape[0] - tp_count) // 2
    group_size = tp_count // kv_count
    head_dim = trainer_panels.shape[2]
    block_rows = trainer_panels.shape[1]
    half_rows = block_rows // 2
    seq_total = tokens.shape[0]

    all_slots = lax.all_gather(trainer_panels, "tp", axis=0, tiled=True)
    kv_id = member_id // group_size
    quarter = member_id % group_size
    kv_panel = tp_count + kv_id + kv_count * (quarter // 2)
    half = quarter % 2
    q_block = all_slots[panel_home[member_id]]
    kv_block = all_slots[panel_home[kv_panel]]
    kv_half = lax.dynamic_slice_in_dim(kv_block, half * half_rows, half_rows, axis=0)
    piece = jnp.concatenate([q_block, kv_half], axis=0)
    gathered = lax.all_gather(piece, "grp", axis=0, tiled=False)
    q_weights = gathered[:, :block_rows].reshape(grp_count * block_rows, head_dim)
    kv_weights = gathered[:, block_rows:]

    query_rows = jnp.dot(tokens, q_weights, preferred_element_type=jnp.float32).astype(jnp.bfloat16)
    token_halves = tokens.reshape(seq_total, grp_count, 2, half_rows)
    token_half = lax.dynamic_index_in_dim(token_halves, half, axis=2, keepdims=False)
    kv_part = jnp.einsum(
        "sgi,gic->sc", token_half, kv_weights, preferred_element_type=jnp.float32
    )
    pair_perm = [(i, i ^ 1) for i in range(tp_count)]
    kv_full = (kv_part + lax.ppermute(kv_part, "tp", pair_perm)).astype(jnp.bfloat16)
    swap_perm = [(i, i ^ 2) for i in range(tp_count)]
    kv_other = lax.ppermute(kv_full, "tp", swap_perm)
    holds_k = quarter < 2
    key_rows = jnp.where(holds_k, kv_full, kv_other)
    value_rows = jnp.where(holds_k, kv_other, kv_full)

    position = jnp.arange(seq_total, dtype=jnp.int32)
    bounds = jnp.cumsum(lengths[0])
    segment = jnp.sum((position[:, None] >= bounds[None, :]).astype(jnp.int32), axis=1)
    allowed = (segment[:, None] == segment[None, :]) & (position[None, :] <= position[:, None])
    score_scale = head_dim ** (-0.5)
    scores = (
        lax.dot_general(
            query_rows, key_rows, (((1,), (1,)), ((), ())), preferred_element_type=jnp.float32
        )
        * score_scale
    )
    masked = jnp.where(allowed, scores, -jnp.inf)
    row_peak = jnp.max(masked, axis=1, keepdims=True)
    row_exp = jnp.exp(masked - row_peak)
    attn_probs = (row_exp / jnp.sum(row_exp, axis=1, keepdims=True)).astype(jnp.bfloat16)
    context = jnp.dot(attn_probs, value_rows, preferred_element_type=jnp.float32)
    return lax.all_to_all(context, "tp", split_axis=0, concat_axis=1, tiled=True)


def solution(mesh):
    placed = (P("grp", None), P("tp", "grp", None), P(), P("grp", None))
    return jax.shard_map(
        on_device, mesh=mesh, in_specs=placed, out_specs=P(("grp", "tp"), None), check_vma=False
    )
```

time: 503 us -> 210 us (0.42)
  waiting for transfers between devices: 398 us -> 132 us
  starting transfers between devices: 17.2 us -> 6.58 us
  local copies, waits for them, and re-layouts: 18.3 us -> 10.4 us
  other arithmetic: 8.16 us -> 1.07 us
    all_to_all x1 -> x0, waiting for transfers between devices: 332 us -> none  [on_device(): lax.all_to_all(outbound, 'tp', split_axis=0, concat_axis=0, tiled=True)]
    all_gather x1 -> x2, waiting for transfers between devices: 66.1 us -> 128 us  [the longest x1 78.4 us: on_device(): all_slots = lax.all_gather(trainer_panels, 'tp', axis=0, tiled=True)]
    all_to_all x1 -> x0, starting transfers between devices: 17.1 us -> none  [on_device(): lax.all_to_all(outbound, 'tp', split_axis=0, concat_axis=0, tiled=True)]
    gather x3 -> x0, local copies, waits for them, and re-layouts: 8.28 us -> none  [the longest x1 6.41 us: on_device(): picked = trainer_panels[jnp.clip(local_slot, 0, slot_count - 1)]]
    select_n x5 -> x0, other arithmetic: 6.99 us -> none  [the longest x1 6.89 us: on_device(): jnp.where(owned_here[:, :, None, None], picked, jnp.zeros_like(picked))]
    ppermute x0 -> x2, starting transfers between devices: none -> 6.54 us  [the longest x1 3.36 us: on_device(): lax.ppermute(kv_part, 'tp', pair_perm)]
    all_gather x1 -> x0, local copies, waits for them, and re-layouts: 6.33 us -> none  [on_device(): full_panels = lax.all_gather(selected, 'grp', axis=0, tiled=True)]
    unnamed x8 -> x7, local copies, waits for them, and re-layouts: 1.33 us -> 7.16 us
  transfers between devices with their start and end apart: 2 -> 4, of which waited for: 2 -> 4; matrix products, arithmetic and copies ran while one was open for 0% -> 4% of each run, Pallas kernels for 0% -> 0%
where the time goes in v1:
time: 210 us; the launch traced here: 209 us
  waiting for transfers between devices  132 us (63%)
  blocking collectives  35.3 us (17%)
  between operations  17.4 us (8%)
  local copies, waits for them, and re-layouts  10.4 us (5%)
  starting transfers between devices  6.58 us (3%)
  matrix products  6.57 us (3%)
    all_gather x1, waiting for transfers between devices, on_device(): all_slots = lax.all_gather(trainer_panels, 'tp', axis=0, tiled=True)  78.4 us
    all_gather x1, waiting for transfers between devices, on_device(): gathered = lax.all_gather(piece, 'grp', axis=0, tiled=False)  49.6 us
    all_to_all x1, blocking collectives, on_device(): lax.all_to_all(context, 'tp', split_axis=0, concat_axis=1, tiled=True)  35.3 us
    unnamed x7, local copies, waits for them, and re-layouts  7.16 us
  transfers between devices with their start and end apart: 4, of which 4 were waited for; matrix products, arithmetic and copies ran while one was open for 4% of the time, Pallas kernels for 0%

profile of v1, /device:TPU:1, one launch (start us, length us, event | category | flops | bytes accessed | tf_op | source)
XLA Modules:
  0.0 209.4 jit_solution(2811401276876923710)
XLA Ops:
  6.5 0.0 all-gather.4.cloned.1.call-start
  6.5 0.7 all-gather.4.cloned.1.call-update
  7.3 0.0 all-gather.6.cloned.1.call-start
  7.4 1.4 fusion.16
  12.6 78.4 %all-gather.4.cloned.1.call-done = bf16[64,320,128]{2,1,0:T(8,128)(2,1)} async-done(((bf16[2,320,128]{2,1,0:T(8,128)(2,1)}), bf16[64,320,128]{2,1,0:T(8,128)(2,1)}) %all-gather.4.cloned.1.call-update) | async-done | bytes 5242896 | tf_op jit(solution)/shard_map/all_gather | solution.py:18
  91.0 0.9 dynamic-slice_bitcast_fusion
  91.9 0.8 dynamic-slice_bitcast_fusion.1
  92.7 0.7 pad_maximum_fusion
  93.3 0.0 all-gather.6.cloned.1.call-update
  93.4 0.0 copy-start.1
  93.4 6.3 %copy.12 = bf16[384,5120]{0,1:T(8,128)(2,1)} copy(bf16[384,5120]{1,0:T(8,128)(2,1)} %param.4) | data formatting | bytes 7864320 | tf_op args[0]
  99.6 49.6 %all-gather.6.cloned.1.call-done = bf16[7680,128]{1,0:T(8,128)(2,1)} async-done(((bf16[480,128]{1,0:T(8,128)(2,1)}), bf16[7680,128]{1,0:T(8,128)(2,1)}) %all-gather.6.cloned.1.call-update) | async-done | bytes 1966096 | tf_op jit(solution)/shard_map/all_gather | solution.py:27
  149.2 0.0 copy-start
  149.2 2.5 %fusion.4 = f32[384,128]{1,0:T(8,128)S(1)} fusion(bf16[384,16,2,160]{0,3,2,1:T(8,128)(2,1)} %bitcast.25, s32[]{:T(128)S(6)} %select_n.69, bf16[16,480,128]{2,1,0:T(8,128)(2,1)} %bitcast.28), kind=kOutput, calls=%fused_computation.5 | convolution fusion | flops 251658240 | bytes 2818052 | tf_op jit(solution)/shard_map/sgi,gic->sc/dot_general | solution.py:34
  151.8 3.4 %collective-permute-start = (f32[384,128]{1,0:T(8,128)S(1)}, f32[384,128]{1,0:T(8,128)S(1)}, u32[]{:S(2)}, u32[]{:S(2)}) collective-permute-start(f32[384,128]{1,0:T(8,128)S(1)} %fusion.4), channel_id=1, source_target_pairs={{0,1},{1,0},{2,3},{3,2},{4,5},{5,4},{6,7},{7,6},{8,9},{9,8},{10,11... | collective-permute-start | bytes 589832 | tf_op jit(solution)/shard_map/ppermute | solution.py:38
  155.1 0.0 copy-done.1
  155.2 0.2 reduce-window.8
  155.3 0.9 collective-permute-done
  156.2 3.2 %collective-permute-start.1 = (bf16[384,128]{1,0:T(8,128)(2,1)S(1)}, bf16[384,128]{1,0:T(8,128)(2,1)S(1)}, u32[]{:S(2)}, u32[]{:S(2)}) collective-permute-start(bf16[384,128]{1,0:T(8,128)(2,1)S(1)} %add_convert_fusion), channel_id=1, source_target_pairs={{0,2},{1,3},{2,0},{3,1},{4,6},{5,7},{6,4},{7,5},{8,10},{9,11},{10,... | collective-permute-start | bytes 294920 | tf_op jit(solution)/shard_map/ppermute | solution.py:40
  159.4 0.1 convert_reduce_fusion
  159.5 0.0 copy-done
  159.5 0.1 slice.9
  159.6 2.5 %collective-permute-done.1 = bf16[384,128]{1,0:T(8,128)(2,1)S(1)} collective-permute-done((bf16[384,128]{1,0:T(8,128)(2,1)S(1)}, bf16[384,128]{1,0:T(8,128)(2,1)S(1)}, u32[]{:S(2)}, u32[]{:S(2)}) %collective-permute-start.1) | collective-permute-done | bytes 98336 | tf_op jit(solution)/shard_map/ppermute | solution.py:40
  162.1 3.7 %fusion.17 = (f32[384]{0:T(512)S(1)}, f32[384,384]{0,1:T(8,128)S(1)}) fusion(bf16[5120,128]{1,0:T(8,128)(2,1)S(1)} %bitcast.24, bf16[384,5120]{1,0:T(8,128)(2,1)} %param.4, bf16[384,128]{1,0:T(8,128)(2,1)S(1)} %add_convert_fusion, bf16[384,128]{1,0:T(8,128)(2,1)S(1)} %collective-permute-done.1, pred[]{:T(512)S(6)} %lt.39, s32[384]{0:T(512)S(1)} %convert_reduce_fusion), kind=kOutput, calls=%fused_computation.26 | convolution fusion | flops 542047872 | bytes 6032385 | tf_op jit(solution)/shard_map/dot_general | solution.py:51
  165.9 0.1 fusion.9
  166.0 0.3 fusion.10
  166.3 35.3 %all_to_all.19 = f32[32,12,128]{2,1,0:T(8,128)S(1)} all-to-all(f32[32,12,128]{2,1,0:T(8,128)S(1)} %all_to_all.14), channel_id=1, replica_groups=mesh['grp'=16,'tp'=32] {'tp'}, dimensions={0} | all-to-all | bytes 393216 | tf_op jit(solution)/shard_map/all_to_all | solution.py:61
  201.7 0.1 copy.13
  201.8 0.9 copy.14
  (3 shorter events, 0.1 us)
Async XLA Ops:
  6.5 84.4 %all-gather.4.cloned.1.call-start = ((), (), s32[]{:S(2)}) async-start(), calls=%async_computation.1 | async-start | bytes 5406720 | tf_op jit(solution)/shard_map/all_gather | solution.py:18
  7.3 142.0 %all-gather.6.cloned.1.call-start = ((), (), s32[]{:S(2)}) async-start(), calls=%async_computation.2 | async-start | bytes 2088960 | tf_op jit(solution)/shard_map/all_gather | solution.py:27
  93.4 61.8 %copy-start.1 = (s32[1,4]{1,0:T(1,128)S(1)}, s32[1,4]{1,0:T(1,128)}, u32[]{:S(2)}) copy-start(s32[1,4]{1,0:T(1,128)} %param.7) | copy-start | bytes 52
  149.2 10.3 %copy-start = (bf16[7680,128]{1,0:T(8,128)(2,1)S(1)}, bf16[7680,128]{1,0:T(8,128)(2,1)}, u32[]{:S(2)}) copy-start(bf16[7680,128]{1,0:T(8,128)(2,1)} %all-gather.6.cloned.1.call-done) | copy-start | bytes 5898244
  151.8 4.4 %collective-permute-start = (f32[384,128]{1,0:T(8,128)S(1)}, f32[384,128]{1,0:T(8,128)S(1)}, u32[]{:S(2)}, u32[]{:S(2)}) collective-permute-start(f32[384,128]{1,0:T(8,128)S(1)} %fusion.4), channel_id=1, source_target_pairs={{0,1},{1,0},{2,3},{3,2},{4,5},{5,4},{6,7},{7,6},{8,9},{9,8},{10,11... | collective-permute-start | bytes 589832 | tf_op jit(solution)/shard_map/ppermute | solution.py:38
  156.2 5.9 %collective-permute-start.1 = (bf16[384,128]{1,0:T(8,128)(2,1)S(1)}, bf16[384,128]{1,0:T(8,128)(2,1)S(1)}, u32[]{:S(2)}, u32[]{:S(2)}) collective-permute-start(bf16[384,128]{1,0:T(8,128)(2,1)S(1)} %add_convert_fusion), channel_id=1, source_target_pairs={{0,2},{1,3},{2,0},{3,1},{4,6},{5,7},{6,4},{7,5},{8,10},{9,11},{10,... | collective-permute-start | bytes 294920 | tf_op jit(solution)/shard_map/ppermute | solution.py:40
Sparse Core Ops, SparseCore 0:
  9.5 81.4 all-gather.3
  94.0 55.1 all-gather.5

commit v2 on v1

--- a/solution.py
+++ b/solution.py
@@ -15,14 +15,25 @@
     half_rows = block_rows // 2
     seq_total = tokens.shape[0]
 
-    all_slots = lax.all_gather(trainer_panels, "tp", axis=0, tiled=True)
+    core = member_id % 2
+    partner_perm = [(i, i ^ 1) for i in range(tp_count)]
+    mine = lax.dynamic_slice_in_dim(trainer_panels, core * half_rows, half_rows, axis=1)
+    other = lax.dynamic_slice_in_dim(trainer_panels, (1 - core) * half_rows, half_rows, axis=1)
+    from_partner = lax.ppermute(other, "tp", partner_perm)
+    chip_slots = jnp.where(core == 0, jnp.concatenate([mine, from_partner], axis=0),
+                           jnp.concatenate([from_partner, mine], axis=0))
+    same_core = [list(range(c, tp_count, 2)) for c in range(2)]
+    all_halves = lax.all_gather(chip_slots, "tp", axis=0, tiled=True, axis_index_groups=same_core)
     kv_id = member_id // group_size
     quarter = member_id % group_size
     kv_panel = tp_count + kv_id + kv_count * (quarter // 2)
-    half = quarter % 2
-    q_block = all_slots[panel_home[member_id]]
-    kv_block = all_slots[panel_home[kv_panel]]
-    kv_half = lax.dynamic_slice_in_dim(kv_block, half * half_rows, half_rows, axis=0)
+    half = core
+    partner_id = member_id ^ 1
+    q_mine = all_halves[panel_home[member_id]]
+    q_theirs = lax.ppermute(all_halves[panel_home[partner_id]], "tp", partner_perm)
+    q_block = jnp.where(core == 0, jnp.concatenate([q_mine, q_theirs], axis=0),
+                        jnp.concatenate([q_theirs, q_mine], axis=0))
+    kv_half = all_halves[panel_home[kv_panel]]
     piece = jnp.concatenate([q_block, kv_half], axis=0)
     gathered = lax.all_gather(piece, "grp", axis=0, tiled=False)
     q_weights = gathered[:, :block_rows].reshape(grp_count * block_rows, head_dim)
@@ -58,7 +69,8 @@
     row_exp = jnp.exp(masked - row_peak)
     attn_probs = (row_exp / jnp.sum(row_exp, axis=1, keepdims=True)).astype(jnp.bfloat16)
     context = jnp.dot(attn_probs, value_rows, preferred_element_type=jnp.float32)
-    return lax.all_to_all(context, "tp", split_axis=0, concat_axis=1, tiled=True)
+    sent = lax.all_to_all(context.astype(jnp.bfloat16), "tp", split_axis=0, concat_axis=1, tiled=True)
+    return sent.astype(jnp.float32)
 
 
 def solution(mesh):

time: 210 us -> 207 us (0.986)
  starting transfers between devices: 6.58 us -> 26.9 us
  waiting for transfers between devices: 132 us -> 112 us
  blocking collectives: 35.3 us -> 29.2 us
  between operations: 17.4 us -> 19.6 us
    all_gather x1, waiting for transfers between devices: 78.4 us -> 57.4 us  [on_device(): lax.all_gather(chip_slots, 'tp', axis=0, tiled=True, axis_index_groups=sa...]
    ppermute x0 -> x2, starting transfers between devices: none -> 20.3 us  [the longest x1 11.5 us: on_device(): lax.ppermute(all_halves[panel_home[partner_id]], 'tp', partner_perm)]
    all_to_all x1, blocking collectives: 35.3 us -> 29.2 us  [on_device(): lax.all_to_all(context.astype(jnp.bfloat16), 'tp', split_axis=0, concat_a...]
  transfers between devices with their start and end apart: 4 -> 6, of which waited for: 4 -> 6; matrix products, arithmetic and copies ran while one was open for 4% -> 4% of each run, Pallas kernels for 0% -> 0%
where the time goes in v2:
time: 207 us; the launch traced here: 206 us
  waiting for transfers between devices  112 us (54%)
  blocking collectives  29.2 us (14%)
  starting transfers between devices  26.9 us (13%)
  between operations  19.6 us (9%)
  local copies, waits for them, and re-layouts  10.6 us (5%)
  matrix products  6.57 us (3%)
    all_gather x1, waiting for transfers between devices, on_device(): lax.all_gather(chip_slots, 'tp', axis=0, tiled=True, axis_index_groups=sa...  57.4 us
    all_gather x1, waiting for transfers between devices, on_device(): gathered = lax.all_gather(piece, 'grp', axis=0, tiled=False)  49.2 us
    all_to_all x1, blocking collectives, on_device(): lax.all_to_all(context.astype(jnp.bfloat16), 'tp', split_axis=0, concat_a...  29.2 us
    ppermute x1, starting transfers between devices, on_device(): lax.ppermute(all_halves[panel_home[partner_id]], 'tp', partner_perm)  11.5 us
    ppermute x1, starting transfers between devices, on_device(): from_partner = lax.ppermute(other, 'tp', partner_perm)  8.79 us
    unnamed x7, local copies, waits for them, and re-layouts  7.15 us
  transfers between devices with their start and end apart: 6, of which 6 were waited for; matrix products, arithmetic and copies ran while one was open for 4% of the time, Pallas kernels for 0%

profile of v2, /device:TPU:1, one launch (start us, length us, event | category | flops | bytes accessed | tf_op | source)
XLA Modules:
  0.0 206.3 jit_solution(11476017731040818014)
XLA Ops:
  6.5 0.0 all-gather.4.cloned.1.call-start
  6.5 0.9 constant_dynamic-slice_fusion.1
  7.5 8.8 %collective-permute-start = (bf16[2,160,128]{2,1,0:T(8,128)(2,1)S(1)}, bf16[2,160,128]{2,1,0:T(8,128)(2,1)S(1)}, u32[]{:S(2)}, u32[]{:S(2)}) collective-permute-start(bf16[2,160,128]{2,1,0:T(8,128)(2,1)S(1)} %get-tuple-element.9), channel_id=1, source_target_pairs={{0,1},{1,0},{2,3},{3,2},{4,5},{5,4},{6,7},{7,6},{8,9},{9,8},{10,11... | collective-permute-start | bytes 245768 | tf_op jit(solution)/shard_map/ppermute | solution.py:22
  16.3 0.9 collective-permute-done
  17.2 0.7 maximum_select_fusion
  17.9 0.0 all-gather.4.cloned.1.call-update
  17.9 0.0 all-gather.6.cloned.1.call-start
  18.0 1.4 fusion.15
  25.5 57.4 %all-gather.4.cloned.1.call-done = bf16[64,160,128]{2,1,0:T(8,128)(2,1)} async-done(((bf16[4,160,128]{2,1,0:T(8,128)(2,1)}), bf16[64,160,128]{2,1,0:T(8,128)(2,1)}) %all-gather.4.cloned.1.call-update) | async-done | bytes 2621456 | tf_op jit(solution)/shard_map/all_gather | solution.py:26
  82.8 0.8 dynamic-slice_bitcast_fusion.2
  83.7 11.5 %collective-permute-start.1 = (bf16[160,128]{1,0:T(8,128)(2,1)S(1)}, bf16[160,128]{1,0:T(8,128)(2,1)S(1)}, u32[]{:S(2)}, u32[]{:S(2)}) collective-permute-start(bf16[160,128]{1,0:T(8,128)(2,1)S(1)} %get-tuple-element.7), channel_id=1, source_target_pairs={{0,1},{1,0},{2,3},{3,2},{4,5},{5,4},{6,7},{7,6},{8,9},{9,8},{10,11... | collective-permute-start | bytes 122888 | tf_op jit(solution)/shard_map/ppermute | solution.py:33
  95.2 0.8 collective-permute-done.1
  96.1 0.7 pad_maximum_fusion
  96.7 0.0 all-gather.6.cloned.1.call-update
  96.8 6.3 %copy.12 = bf16[384,5120]{0,1:T(8,128)(2,1)} copy(bf16[384,5120]{1,0:T(8,128)(2,1)} %param.4) | data formatting | bytes 7864320 | tf_op args[0]
  103.0 0.0 copy-start.1
  103.0 49.2 %all-gather.6.cloned.1.call-done = bf16[7680,128]{1,0:T(8,128)(2,1)} async-done(((bf16[480,128]{1,0:T(8,128)(2,1)}), bf16[7680,128]{1,0:T(8,128)(2,1)}) %all-gather.6.cloned.1.call-update) | async-done | bytes 1966096 | tf_op jit(solution)/shard_map/all_gather | solution.py:38
  152.2 0.0 copy-start
  152.2 2.5 %fusion.4 = f32[384,128]{1,0:T(8,128)S(1)} fusion(bf16[384,16,2,160]{0,3,2,1:T(8,128)(2,1)} %bitcast.29, s32[]{:T(128)S(6)} %select_n.95, bf16[16,480,128]{2,1,0:T(8,128)(2,1)} %bitcast.31), kind=kOutput, calls=%fused_computation.5 | convolution fusion | flops 251658240 | bytes 2818052 | tf_op jit(solution)/shard_map/sgi,gic->sc/dot_general | solution.py:45
  154.7 3.4 %collective-permute-start.2 = (f32[384,128]{1,0:T(8,128)S(1)}, f32[384,128]{1,0:T(8,128)S(1)}, u32[]{:S(2)}, u32[]{:S(2)}) collective-permute-start(f32[384,128]{1,0:T(8,128)S(1)} %fusion.4), channel_id=1, source_target_pairs={{0,1},{1,0},{2,3},{3,2},{4,5},{5,4},{6,7},{7,6},{8,9},{9,8},{10,11... | collective-permute-start | bytes 589832 | tf_op jit(solution)/shard_map/ppermute | solution.py:49
  158.1 0.0 copy-done.1
  158.1 0.2 reduce-window.8
  158.3 0.9 collective-permute-done.2
  159.2 3.2 %collective-permute-start.3 = (bf16[384,128]{1,0:T(8,128)(2,1)S(1)}, bf16[384,128]{1,0:T(8,128)(2,1)S(1)}, u32[]{:S(2)}, u32[]{:S(2)}) collective-permute-start(bf16[384,128]{1,0:T(8,128)(2,1)S(1)} %add_convert_fusion), channel_id=1, source_target_pairs={{0,2},{1,3},{2,0},{3,1},{4,6},{5,7},{6,4},{7,5},{8,10},{9,11},{10,... | collective-permute-start | bytes 294920 | tf_op jit(solution)/shard_map/ppermute | solution.py:51
  162.4 0.1 convert_reduce_fusion
  162.5 0.0 copy-done
  162.5 0.1 slice.9
  162.6 2.5 %collective-permute-done.3 = bf16[384,128]{1,0:T(8,128)(2,1)S(1)} collective-permute-done((bf16[384,128]{1,0:T(8,128)(2,1)S(1)}, bf16[384,128]{1,0:T(8,128)(2,1)S(1)}, u32[]{:S(2)}, u32[]{:S(2)}) %collective-permute-start.3) | collective-permute-done | bytes 98336 | tf_op jit(solution)/shard_map/ppermute | solution.py:51
  165.1 3.7 %fusion.16 = (f32[384]{0:T(512)S(1)}, f32[384,384]{0,1:T(8,128)S(1)}) fusion(bf16[5120,128]{1,0:T(8,128)(2,1)S(1)} %bitcast.28, bf16[384,5120]{1,0:T(8,128)(2,1)} %param.4, bf16[384,128]{1,0:T(8,128)(2,1)S(1)} %add_convert_fusion, bf16[384,128]{1,0:T(8,128)(2,1)S(1)} %collective-permute-done.3, pred[]{:T(512)S(6)} %lt.48, s32[384]{0:T(512)S(1)} %convert_reduce_fusion), kind=kOutput, calls=%fused_computation.32 | convolution fusion | flops 542047872 | bytes 6032385 | tf_op jit(solution)/shard_map/dot_general | solution.py:62
  168.8 0.1 fusion.9
  169.0 0.3 convolution_convert_fusion
  169.3 29.2 %all_to_all.13 = bf16[32,12,128]{2,1,0:T(8,128)(2,1)S(1)} all-to-all(bf16[32,12,128]{2,1,0:T(8,128)(2,1)S(1)} %all_to_all.10), channel_id=1, replica_groups=mesh['grp'=16,'tp'=32] {'tp'}, dimensions={0} | all-to-all | bytes 196608 | tf_op jit(solution)/shard_map/all_to_all | solution.py:72
  198.5 0.1 copy.13
  198.6 0.9 copy.14
  (5 shorter events, 0.1 us)
Async XLA Ops:
  6.5 76.3 %all-gather.4.cloned.1.call-start = ((), (), s32[]{:S(2)}) async-start(), calls=%async_computation.1 | async-start | bytes 2785280 | tf_op jit(solution)/shard_map/all_gather | solution.py:26
  7.5 9.7 %collective-permute-start = (bf16[2,160,128]{2,1,0:T(8,128)(2,1)S(1)}, bf16[2,160,128]{2,1,0:T(8,128)(2,1)S(1)}, u32[]{:S(2)}, u32[]{:S(2)}) collective-permute-start(bf16[2,160,128]{2,1,0:T(8,128)(2,1)S(1)} %get-tuple-element.9), channel_id=1, source_target_pairs={{0,1},{1,0},{2,3},{3,2},{4,5},{5,4},{6,7},{7,6},{8,9},{9,8},{10,11... | collective-permute-start | bytes 245768 | tf_op jit(solution)/shard_map/ppermute | solution.py:22
  17.9 134.3 %all-gather.6.cloned.1.call-start = ((), (), s32[]{:S(2)}) async-start(), calls=%async_computation.2 | async-start | bytes 2088960 | tf_op jit(solution)/shard_map/all_gather | solution.py:38
  83.7 12.4 %collective-permute-start.1 = (bf16[160,128]{1,0:T(8,128)(2,1)S(1)}, bf16[160,128]{1,0:T(8,128)(2,1)S(1)}, u32[]{:S(2)}, u32[]{:S(2)}) collective-permute-start(bf16[160,128]{1,0:T(8,128)(2,1)S(1)} %get-tuple-element.7), channel_id=1, source_target_pairs={{0,1},{1,0},{2,3},{3,2},{4,5},{5,4},{6,7},{7,6},{8,9},{9,8},{10,11... | collective-permute-start | bytes 122888 | tf_op jit(solution)/shard_map/ppermute | solution.py:33
  103.0 55.1 %copy-start.1 = (s32[1,4]{1,0:T(1,128)S(1)}, s32[1,4]{1,0:T(1,128)}, u32[]{:S(2)}) copy-start(s32[1,4]{1,0:T(1,128)} %param.7) | copy-start | bytes 52
  152.2 10.3 %copy-start = (bf16[7680,128]{1,0:T(8,128)(2,1)S(1)}, bf16[7680,128]{1,0:T(8,128)(2,1)}, u32[]{:S(2)}) copy-start(bf16[7680,128]{1,0:T(8,128)(2,1)} %all-gather.6.cloned.1.call-done) | copy-start | bytes 5898244
  154.7 4.4 %collective-permute-start.2 = (f32[384,128]{1,0:T(8,128)S(1)}, f32[384,128]{1,0:T(8,128)S(1)}, u32[]{:S(2)}, u32[]{:S(2)}) collective-permute-start(f32[384,128]{1,0:T(8,128)S(1)} %fusion.4), channel_id=1, source_target_pairs={{0,1},{1,0},{2,3},{3,2},{4,5},{5,4},{6,7},{7,6},{8,9},{9,8},{10,11... | collective-permute-start | bytes 589832 | tf_op jit(solution)/shard_map/ppermute | solution.py:49
  159.2 5.9 %collective-permute-start.3 = (bf16[384,128]{1,0:T(8,128)(2,1)S(1)}, bf16[384,128]{1,0:T(8,128)(2,1)S(1)}, u32[]{:S(2)}, u32[]{:S(2)}) collective-permute-start(bf16[384,128]{1,0:T(8,128)(2,1)S(1)} %add_convert_fusion), channel_id=1, source_target_pairs={{0,2},{1,3},{2,0},{3,1},{4,6},{5,7},{6,4},{7,5},{8,10},{9,11},{10,... | collective-permute-start | bytes 294920 | tf_op jit(solution)/shard_map/ppermute | solution.py:51
Sparse Core Ops, SparseCore 0:
  18.0 64.7 all-gather.3
  96.9 55.2 all-gather.5

commit v3 on v2

--- a/solution.py
+++ b/solution.py
@@ -1,7 +1,56 @@
+import functools
+
 import jax
 import jax.numpy as jnp
 from jax import lax
+from jax.experimental import pallas as pl
+from jax.experimental.pallas import tpu as pltpu
 from jax.sharding import PartitionSpec as P
+
+MESH = pl.DeviceIdType.MESH
+
+
+def exchange_kernel(axis, count, scatter, send_ref, out_ref, landed, send_sems, recv_sems):
+    me = lax.axis_index(axis)
+    barrier = pltpu.get_barrier_semaphore()
+    for step in range(1, count):
+        peer = lax.rem(me + step, count)
+        pl.semaphore_signal(barrier, inc=1, device_id={axis: peer}, device_id_type=MESH)
+    pl.semaphore_wait(barrier, count - 1)
+    copies = []
+    for step in range(1, count):
+        peer = lax.rem(me + step, count)
+        source = send_ref.at[peer] if scatter else send_ref
+        copy = pltpu.make_async_remote_copy(
+            src_ref=source,
+            dst_ref=landed.at[me],
+            send_sem=send_sems.at[step],
+            recv_sem=recv_sems.at[step],
+            device_id={axis: peer},
+            device_id_type=MESH,
+        )
+        copy.start()
+        copies.append(copy)
+    landed[me] = send_ref[me] if scatter else send_ref[...]
+    for copy in copies:
+        copy.wait()
+    out_ref[...] = landed[...]
+
+
+def exchange(x, axis, count, scatter, collective_id):
+    piece = x.shape[1:] if scatter else x.shape
+    return pl.pallas_call(
+        functools.partial(exchange_kernel, axis, count, scatter),
+        out_shape=jax.ShapeDtypeStruct((count,) + piece, x.dtype),
+        in_specs=[pl.BlockSpec(memory_space=pltpu.VMEM)],
+        out_specs=pl.BlockSpec(memory_space=pltpu.VMEM),
+        scratch_shapes=[
+            pltpu.VMEM((count,) + piece, x.dtype),
+            pltpu.SemaphoreType.DMA((count,)),
+            pltpu.SemaphoreType.DMA((count,)),
+        ],
+        compiler_params=pltpu.CompilerParams(collective_id=collective_id, has_side_effects=True),
+    )(x)
 
 
 def on_device(tokens, trainer_panels, panel_home, lengths):
@@ -35,7 +84,7 @@
                         jnp.concatenate([q_theirs, q_mine], axis=0))
     kv_half = all_halves[panel_home[kv_panel]]
     piece = jnp.concatenate([q_block, kv_half], axis=0)
-    gathered = lax.all_gather(piece, "grp", axis=0, tiled=False)
+    gathered = exchange(piece, "grp", grp_count, False, 0)
     q_weights = gathered[:, :block_rows].reshape(grp_count * block_rows, head_dim)
     kv_weights = gathered[:, block_rows:]
 
@@ -69,8 +118,9 @@
     row_exp = jnp.exp(masked - row_peak)
     attn_probs = (row_exp / jnp.sum(row_exp, axis=1, keepdims=True)).astype(jnp.bfloat16)
     context = jnp.dot(attn_probs, value_rows, preferred_element_type=jnp.float32)
-    sent = lax.all_to_all(context.astype(jnp.bfloat16), "tp", split_axis=0, concat_axis=1, tiled=True)
-    return sent.astype(jnp.float32)
+    outgoing = context.reshape(tp_count, seq_total // tp_count, head_dim)
+    arrived = exchange(outgoing, "tp", tp_count, True, 1)
+    return jnp.transpose(arrived, (1, 0, 2)).reshape(seq_total // tp_count, tp_count * head_dim)
 
 
 def solution(mesh):

time: 207 us -> 188 us (0.908)
  Pallas kernels: 0 us -> 59.1 us
  waiting for transfers between devices: 112 us -> 61.8 us
  blocking collectives: 29.2 us -> 0 us
    pallas_call x0 -> x2, Pallas kernels: none -> 59.1 us  [exchange(): pl.pallas_call(functools.partial(exchange_kernel, axis, count, scatter),...]
    all_gather x1 -> x0, waiting for transfers between devices: 49.2 us -> none  [on_device(): gathered = lax.all_gather(piece, 'grp', axis=0, tiled=False)]
    all_to_all x1 -> x0, blocking collectives: 29.2 us -> none  [on_device(): lax.all_to_all(context.astype(jnp.bfloat16), 'tp', split_axis=0, concat_a...]
    unnamed x7 -> x5, local copies, waits for them, and re-layouts: 7.15 us -> 7.15 us
  transfers between devices with their start and end apart: 6 -> 5, of which waited for: 6 -> 4; matrix products, arithmetic and copies ran while one was open for 4% -> 4% of each run, Pallas kernels for 0% -> 0%
where the time goes in v3:
time: 188 us; the launch traced here: 187 us
  waiting for transfers between devices  61.8 us (33%)
  Pallas kernels  59.1 us (31%)
  starting transfers between devices  26.1 us (14%)
  between operations  19.7 us (10%)
  local copies, waits for them, and re-layouts  12.1 us (6%)
  matrix products  6.49 us (3%)
    pallas_call x2, Pallas kernels, exchange(): pl.pallas_call(functools.partial(exchange_kernel, axis, count, scatter),...  59.1 us
    all_gather x1, waiting for transfers between devices, on_device(): lax.all_gather(chip_slots, 'tp', axis=0, tiled=True, axis_index_groups=sa...  57.4 us
    ppermute x1, starting transfers between devices, on_device(): lax.ppermute(all_halves[panel_home[partner_id]], 'tp', partner_perm)  11.5 us
    ppermute x1, starting transfers between devices, on_device(): from_partner = lax.ppermute(other, 'tp', partner_perm)  8.79 us
    unnamed x5, local copies, waits for them, and re-layouts  7.15 us
  transfers between devices with their start and end apart: 5, of which 4 were waited for; matrix products, arithmetic and copies ran while one was open for 4% of the time, Pallas kernels for 0%

profile of v3, /device:TPU:1, one launch (start us, length us, event | category | flops | bytes accessed | tf_op | source)
XLA Modules:
  0.0 187.1 jit_solution(7408313987676583104)
XLA Ops:
  6.5 0.0 all-gather.2.cloned.1.call-start
  6.5 0.9 constant_dynamic-slice_fusion.1
  7.5 8.8 %collective-permute-start = (bf16[2,160,128]{2,1,0:T(8,128)(2,1)S(1)}, bf16[2,160,128]{2,1,0:T(8,128)(2,1)S(1)}, u32[]{:S(2)}, u32[]{:S(2)}) collective-permute-start(bf16[2,160,128]{2,1,0:T(8,128)(2,1)S(1)} %get-tuple-element.9), channel_id=1, source_target_pairs={{0,1},{1,0},{2,3},{3,2},{4,5},{5,4},{6,7},{7,6},{8,9},{9,8},{10,11... | collective-permute-start | bytes 245768 | tf_op jit(solution)/shard_map/ppermute | solution.py:71
  16.3 0.9 collective-permute-done
  17.2 0.7 maximum_select_fusion
  17.9 0.0 all-gather.2.cloned.1.call-update
  17.9 1.4 fusion.16
  25.5 57.4 %all-gather.2.cloned.1.call-done = bf16[64,160,128]{2,1,0:T(8,128)(2,1)} async-done(((bf16[4,160,128]{2,1,0:T(8,128)(2,1)}), bf16[64,160,128]{2,1,0:T(8,128)(2,1)}) %all-gather.2.cloned.1.call-update) | async-done | bytes 2621456 | tf_op jit(solution)/shard_map/all_gather | solution.py:75
  82.9 0.8 dynamic-slice_bitcast_fusion.2
  83.7 11.5 %collective-permute-start.1 = (bf16[160,128]{1,0:T(8,128)(2,1)S(1)}, bf16[160,128]{1,0:T(8,128)(2,1)S(1)}, u32[]{:S(2)}, u32[]{:S(2)}) collective-permute-start(bf16[160,128]{1,0:T(8,128)(2,1)S(1)} %get-tuple-element.7), channel_id=1, source_target_pairs={{0,1},{1,0},{2,3},{3,2},{4,5},{5,4},{6,7},{7,6},{8,9},{9,8},{10,11... | collective-permute-start | bytes 122888 | tf_op jit(solution)/shard_map/ppermute | solution.py:82
  95.3 6.3 %copy.10 = bf16[384,5120]{0,1:T(8,128)(2,1)} copy(bf16[384,5120]{1,0:T(8,128)(2,1)} %param.4) | data formatting | bytes 7864320 | tf_op args[0]
  101.5 0.0 collective-permute-done.1
  101.6 0.7 pad_maximum_fusion.send_ref
  102.2 0.0 copy-start
  102.2 38.5 %shard_map.46 = bf16[16,480,128]{2,1,0:T(8,128)(2,1)} custom-call(bf16[480,128]{1,0:T(8,128)(2,1)} %pad_maximum_fusion.send_ref), custom_call_target="tpu_custom_call" | custom-call | tf_op jit(solution)/shard_map/pallas_call | solution.py:42
  140.7 0.0 slice-start
  140.8 2.5 %fusion.4 = f32[384,128]{1,0:T(8,128)S(1)} fusion(bf16[384,16,2,160]{0,3,2,1:T(8,128)(2,1)} %bitcast.27, s32[]{:T(128)S(6)} %select_n.95, bf16[16,480,128]{2,1,0:T(8,128)(2,1)} %shard_map.46), kind=kOutput, calls=%fused_computation.5 | convolution fusion | flops 251658240 | bytes 2818052 | tf_op jit(solution)/shard_map/sgi,gic->sc/dot_general | solution.py:94
  143.3 2.7 %collective-permute-start.2 = (f32[384,128]{1,0:T(8,128)S(1)}, f32[384,128]{1,0:T(8,128)S(1)}, u32[]{:S(2)}, u32[]{:S(2)}) collective-permute-start(f32[384,128]{1,0:T(8,128)S(1)} %fusion.4), channel_id=1, source_target_pairs={{0,1},{1,0},{2,3},{3,2},{4,5},{5,4},{6,7},{7,6},{8,9},{9,8},{10,11... | collective-permute-start | bytes 589832 | tf_op jit(solution)/shard_map/ppermute | solution.py:98
  146.0 0.0 copy-done
  146.0 0.2 reduce-window.8
  146.2 0.9 collective-permute-done.2
  147.0 3.1 %collective-permute-start.3 = (bf16[384,128]{1,0:T(8,128)(2,1)S(1)}, bf16[384,128]{1,0:T(8,128)(2,1)S(1)}, u32[]{:S(2)}, u32[]{:S(2)}) collective-permute-start(bf16[384,128]{1,0:T(8,128)(2,1)S(1)} %add_convert_fusion), channel_id=1, source_target_pairs={{0,2},{1,3},{2,0},{3,1},{4,6},{5,7},{6,4},{7,5},{8,10},{9,11},{10,... | collective-permute-start | bytes 294920 | tf_op jit(solution)/shard_map/ppermute | solution.py:100
  150.2 0.1 convert_reduce_fusion
  150.3 2.7 %collective-permute-done.3 = bf16[384,128]{1,0:T(8,128)(2,1)S(1)} collective-permute-done((bf16[384,128]{1,0:T(8,128)(2,1)S(1)}, bf16[384,128]{1,0:T(8,128)(2,1)S(1)}, u32[]{:S(2)}, u32[]{:S(2)}) %collective-permute-start.3) | collective-permute-done | bytes 98336 | tf_op jit(solution)/shard_map/ppermute | solution.py:100
  152.9 0.0 slice-done
  152.9 3.7 %fusion.17 = (f32[384]{0:T(512)S(1)}, f32[384,384]{0,1:T(8,128)S(1)}) fusion(bf16[5120,128]{1,0:T(8,128)(2,1)S(1)} %bitcast.26, bf16[384,5120]{1,0:T(8,128)(2,1)} %param.4, bf16[384,128]{1,0:T(8,128)(2,1)S(1)} %add_convert_fusion, bf16[384,128]{1,0:T(8,128)(2,1)S(1)} %collective-permute-done.3, pred[]{:T(512)S(6)} %lt.48, s32[384]{0:T(512)S(1)} %convert_reduce_fusion), kind=kOutput, calls=%fused_computation.31 | convolution fusion | flops 542047872 | bytes 6032385 | tf_op jit(solution)/shard_map/dot_general | solution.py:111
  156.7 0.1 fusion.9
  156.8 0.3 fusion.10
  157.1 0.7 reshape.44.send_ref
  157.8 20.6 %shard_map.47 = f32[32,12,128]{2,1,0:T(8,128)} custom-call(f32[32,12,128]{2,1,0:T(8,128)} %reshape.44.send_ref), custom_call_target="tpu_custom_call" | custom-call | tf_op jit(solution)/shard_map/pallas_call | solution.py:42
  178.4 1.0 copy.11
  179.4 0.9 copy.12
  (3 shorter events, 0.1 us)
Async XLA Ops:
  6.5 76.4 %all-gather.2.cloned.1.call-start = ((), (), s32[]{:S(2)}) async-start(), calls=%async_computation | async-start | bytes 2785280 | tf_op jit(solution)/shard_map/all_gather | solution.py:75
  7.5 9.7 %collective-permute-start = (bf16[2,160,128]{2,1,0:T(8,128)(2,1)S(1)}, bf16[2,160,128]{2,1,0:T(8,128)(2,1)S(1)}, u32[]{:S(2)}, u32[]{:S(2)}) collective-permute-start(bf16[2,160,128]{2,1,0:T(8,128)(2,1)S(1)} %get-tuple-element.9), channel_id=1, source_target_pairs={{0,1},{1,0},{2,3},{3,2},{4,5},{5,4},{6,7},{7,6},{8,9},{9,8},{10,11... | collective-permute-start | bytes 245768 | tf_op jit(solution)/shard_map/ppermute | solution.py:71
  83.7 17.8 %collective-permute-start.1 = (bf16[160,128]{1,0:T(8,128)(2,1)S(1)}, bf16[160,128]{1,0:T(8,128)(2,1)S(1)}, u32[]{:S(2)}, u32[]{:S(2)}) collective-permute-start(bf16[160,128]{1,0:T(8,128)(2,1)S(1)} %get-tuple-element.7), channel_id=1, source_target_pairs={{0,1},{1,0},{2,3},{3,2},{4,5},{5,4},{6,7},{7,6},{8,9},{9,8},{10,11... | collective-permute-start | bytes 122888 | tf_op jit(solution)/shard_map/ppermute | solution.py:82
  102.2 43.8 %copy-start = (s32[1,4]{1,0:T(1,128)S(1)}, s32[1,4]{1,0:T(1,128)}, u32[]{:S(2)}) copy-start(s32[1,4]{1,0:T(1,128)} %param.7) | copy-start | bytes 52
  140.7 12.2 %slice-start = ((bf16[16,480,128]{2,1,0:T(8,128)(2,1)}), bf16[16,320,128]{2,1,0:T(8,128)(2,1)S(1)}, s32[]{:S(2)}) async-start(bf16[16,480,128]{2,1,0:T(8,128)(2,1)} %shard_map.46), calls=%async_computation.1 | async-start | bytes 2621440 | tf_op jit(solution)/shard_map/slice | solution.py:88
  143.3 3.8 %collective-permute-start.2 = (f32[384,128]{1,0:T(8,128)S(1)}, f32[384,128]{1,0:T(8,128)S(1)}, u32[]{:S(2)}, u32[]{:S(2)}) collective-permute-start(f32[384,128]{1,0:T(8,128)S(1)} %fusion.4), channel_id=1, source_target_pairs={{0,1},{1,0},{2,3},{3,2},{4,5},{5,4},{6,7},{7,6},{8,9},{9,8},{10,11... | collective-permute-start | bytes 589832 | tf_op jit(solution)/shard_map/ppermute | solution.py:98
  147.0 5.9 %collective-permute-start.3 = (bf16[384,128]{1,0:T(8,128)(2,1)S(1)}, bf16[384,128]{1,0:T(8,128)(2,1)S(1)}, u32[]{:S(2)}, u32[]{:S(2)}) collective-permute-start(bf16[384,128]{1,0:T(8,128)(2,1)S(1)} %add_convert_fusion), channel_id=1, source_target_pairs={{0,2},{1,3},{2,0},{3,1},{4,6},{5,7},{6,4},{7,5},{8,10},{9,11},{10,... | collective-permute-start | bytes 294920 | tf_op jit(solution)/shard_map/ppermute | solution.py:100
Sparse Core Ops, SparseCore 0:
  18.0 64.8 all-gather.1

commit v4 on v3

--- a/solution.py
+++ b/solution.py
@@ -37,6 +37,69 @@
     out_ref[...] = landed[...]
 
 
+def ring_kernel(count, stride, send_ref, out_ref, landed, send_sems, recv_sems):
+    me = lax.axis_index("tp")
+    total = count * stride
+    right, left = lax.rem(me + stride, total), lax.rem(me + total - stride, total)
+    spot = me // stride
+    barrier = pltpu.get_barrier_semaphore()
+    for neighbour in (left, right):
+        pl.semaphore_signal(barrier, inc=1, device_id={"tp": neighbour}, device_id_type=MESH)
+    pl.semaphore_wait(barrier, 2)
+
+    def incoming(origin):
+        return pltpu.make_async_remote_copy(
+            src_ref=send_ref,
+            dst_ref=landed.at[origin],
+            send_sem=send_sems.at[0, 0],
+            recv_sem=recv_sems.at[origin],
+            device_id={"tp": right},
+            device_id_type=MESH,
+        )
+
+    landed[spot] = send_ref[...]
+    sends = []
+    far_right, far_left = count // 2, (count - 1) // 2
+    for step in range(1, far_right + 1):
+        streams = [(0, right, lax.rem(spot + count - (step - 1), count))]
+        if step <= far_left:
+            streams.append((1, left, lax.rem(spot + step - 1, count)))
+        for way, target, origin in streams:
+            if step > 1:
+                incoming(origin).wait_recv()
+            source = send_ref if step == 1 else landed.at[origin]
+            copy = pltpu.make_async_remote_copy(
+                src_ref=source,
+                dst_ref=landed.at[origin],
+                send_sem=send_sems.at[way, step],
+                recv_sem=recv_sems.at[origin],
+                device_id={"tp": target},
+                device_id_type=MESH,
+            )
+            copy.start()
+            sends.append(copy)
+    incoming(lax.rem(spot + count - far_right, count)).wait_recv()
+    incoming(lax.rem(spot + far_left, count)).wait_recv()
+    for copy in sends:
+        copy.wait_send()
+    out_ref[...] = landed[...]
+
+
+def ring_gather(x, count, stride, collective_id):
+    return pl.pallas_call(
+        functools.partial(ring_kernel, count, stride),
+        out_shape=jax.ShapeDtypeStruct((count,) + x.shape, x.dtype),
+        in_specs=[pl.BlockSpec(memory_space=pltpu.VMEM)],
+        out_specs=pl.BlockSpec(memory_space=pltpu.VMEM),
+        scratch_shapes=[
+            pltpu.VMEM((count,) + x.shape, x.dtype),
+            pltpu.SemaphoreType.DMA((2, count // 2 + 1)),
+            pltpu.SemaphoreType.DMA((count,)),
+        ],
+        compiler_params=pltpu.CompilerParams(collective_id=collective_id, has_side_effects=True),
+    )(x)
+
+
 def exchange(x, axis, count, scatter, collective_id):
     piece = x.shape[1:] if scatter else x.shape
     return pl.pallas_call(
@@ -71,8 +134,8 @@
     from_partner = lax.ppermute(other, "tp", partner_perm)
     chip_slots = jnp.where(core == 0, jnp.concatenate([mine, from_partner], axis=0),
                            jnp.concatenate([from_partner, mine], axis=0))
-    same_core = [list(range(c, tp_count, 2)) for c in range(2)]
-    all_halves = lax.all_gather(chip_slots, "tp", axis=0, tiled=True, axis_index_groups=same_core)
+    ring_slots = ring_gather(chip_slots, tp_count // 2, 2, 2)
+    all_halves = ring_slots.reshape((-1,) + chip_slots.shape[1:])
     kv_id = member_id // group_size
     quarter = member_id % group_size
     kv_panel = tp_count + kv_id + kv_count * (quarter // 2)

time: 188 us -> 156 us (0.83)
  waiting for transfers between devices: 61.8 us -> 4.28 us
  Pallas kernels: 59.1 us -> 103 us
  between operations: 19.7 us -> 5.88 us
  starting transfers between devices: 26.1 us -> 21.8 us
    all_gather x1 -> x0, waiting for transfers between devices: 57.4 us -> none  [on_device(): lax.all_gather(chip_slots, 'tp', axis=0, tiled=True, axis_index_groups=sa...]
    pallas_call x0 -> x1, Pallas kernels: none -> 43.7 us  [ring_gather(): pl.pallas_call(functools.partial(ring_kernel, count, stride), out_shape=j...]
    ppermute x1, starting transfers between devices: 11.5 us -> 7.93 us  [on_device(): lax.ppermute(all_halves[panel_home[partner_id]], 'tp', partner_perm)]
  transfers between devices with their start and end apart: 5 -> 4, of which waited for: 4 -> 2; matrix products, arithmetic and copies ran while one was open for 4% -> 5% of each run, Pallas kernels for 0% -> 0%
where the time goes in v4:
time: 156 us; the launch traced here: 155 us
  Pallas kernels  103 us (66%)
  starting transfers between devices  21.8 us (14%)
  local copies, waits for them, and re-layouts  12.1 us (8%)
  matrix products  6.49 us (4%)
  between operations  5.88 us (4%)
  waiting for transfers between devices  4.28 us (3%)
  other arithmetic  1.78 us (1%)
    pallas_call x2, Pallas kernels, exchange(): pl.pallas_call(functools.partial(exchange_kernel, axis, count, scatter),...  59.3 us
    pallas_call x1, Pallas kernels, ring_gather(): pl.pallas_call(functools.partial(ring_kernel, count, stride), out_shape=j...  43.7 us
    ppermute x1, starting transfers between devices, on_device(): from_partner = lax.ppermute(other, 'tp', partner_perm)  8.79 us
    ppermute x1, starting transfers between devices, on_device(): lax.ppermute(all_halves[panel_home[partner_id]], 'tp', partner_perm)  7.93 us
    unnamed x5, local copies, waits for them, and re-layouts  7.15 us
    dot_general x1, matrix products, on_device(): lax.dot_general(query_rows, key_rows, (((1,), (1,)), ((), ())), preferred...  3.7 us
    ppermute x1, waiting for transfers between devices, on_device(): kv_other = lax.ppermute(kv_full, 'tp', swap_perm)  3.42 us
  transfers between devices with their start and end apart: 4, of which 2 were waited for; matrix products, arithmetic and copies ran while one was open for 5% of the time, Pallas kernels for 0%

profile of v4, /device:TPU:1, one launch (start us, length us, event | category | flops | bytes accessed | tf_op | source)
XLA Modules:
  0.0 155.4 jit_solution(16788391834598188098)
XLA Ops:
  0.0 0.9 constant_dynamic-slice_fusion.1
  0.9 8.8 %collective-permute-start = (bf16[2,160,128]{2,1,0:T(8,128)(2,1)S(1)}, bf16[2,160,128]{2,1,0:T(8,128)(2,1)S(1)}, u32[]{:S(2)}, u32[]{:S(2)}) collective-permute-start(bf16[2,160,128]{2,1,0:T(8,128)(2,1)S(1)} %get-tuple-element.9), channel_id=1, source_target_pairs={{0,1},{1,0},{2,3},{3,2},{4,5},{5,4},{6,7},{7,6},{8,9},{9,8},{10,11... | collective-permute-start | bytes 245768 | tf_op jit(solution)/shard_map/ppermute | solution.py:134
  9.8 1.4 fusion.16
  16.9 0.0 collective-permute-done
  16.9 0.7 maximum_select_fusion.send_ref
  17.6 43.7 %shard_map.46 = bf16[16,4,160,128]{3,2,1,0:T(8,128)(2,1)} custom-call(bf16[4,160,128]{2,1,0:T(8,128)(2,1)} %maximum_select_fusion.send_ref), custom_call_target="tpu_custom_call" | custom-call | tf_op jit(solution)/shard_map/pallas_call | solution.py:89
  61.3 0.8 dynamic-slice_bitcast_fusion.2
  62.2 7.9 %collective-permute-start.1 = (bf16[160,128]{1,0:T(8,128)(2,1)S(1)}, bf16[160,128]{1,0:T(8,128)(2,1)S(1)}, u32[]{:S(2)}, u32[]{:S(2)}) collective-permute-start(bf16[160,128]{1,0:T(8,128)(2,1)S(1)} %get-tuple-element.7), channel_id=1, source_target_pairs={{0,1},{1,0},{2,3},{3,2},{4,5},{5,4},{6,7},{7,6},{8,9},{9,8},{10,11... | collective-permute-start | bytes 122888 | tf_op jit(solution)/shard_map/ppermute | solution.py:145
  70.1 6.3 %copy.8 = bf16[384,5120]{0,1:T(8,128)(2,1)} copy(bf16[384,5120]{1,0:T(8,128)(2,1)} %param.4) | data formatting | bytes 7864320 | tf_op args[0]
  76.4 0.0 collective-permute-done.1
  76.4 0.7 pad_maximum_fusion.send_ref
  77.1 0.0 copy-start
  77.1 38.7 %shard_map.47 = bf16[16,480,128]{2,1,0:T(8,128)(2,1)} custom-call(bf16[480,128]{1,0:T(8,128)(2,1)} %pad_maximum_fusion.send_ref), custom_call_target="tpu_custom_call" | custom-call | tf_op jit(solution)/shard_map/pallas_call | solution.py:105
  115.8 0.0 slice-start
  115.8 2.5 %fusion.4 = f32[384,128]{1,0:T(8,128)S(1)} fusion(bf16[384,16,2,160]{0,3,2,1:T(8,128)(2,1)} %bitcast.28, s32[]{:T(128)S(6)} %select_n.95, bf16[16,480,128]{2,1,0:T(8,128)(2,1)} %shard_map.47), kind=kOutput, calls=%fused_computation.5 | convolution fusion | flops 251658240 | bytes 2818052 | tf_op jit(solution)/shard_map/sgi,gic->sc/dot_general | solution.py:157
  118.3 2.7 %collective-permute-start.2 = (f32[384,128]{1,0:T(8,128)S(1)}, f32[384,128]{1,0:T(8,128)S(1)}, u32[]{:S(2)}, u32[]{:S(2)}) collective-permute-start(f32[384,128]{1,0:T(8,128)S(1)} %fusion.4), channel_id=1, source_target_pairs={{0,1},{1,0},{2,3},{3,2},{4,5},{5,4},{6,7},{7,6},{8,9},{9,8},{10,11... | collective-permute-start | bytes 589832 | tf_op jit(solution)/shard_map/ppermute | solution.py:161
  121.0 0.0 copy-done
  121.1 0.2 reduce-window.8
  121.2 0.9 collective-permute-done.2
  122.1 2.4 %collective-permute-start.3 = (bf16[384,128]{1,0:T(8,128)(2,1)S(1)}, bf16[384,128]{1,0:T(8,128)(2,1)S(1)}, u32[]{:S(2)}, u32[]{:S(2)}) collective-permute-start(bf16[384,128]{1,0:T(8,128)(2,1)S(1)} %add_convert_fusion), channel_id=1, source_target_pairs={{0,2},{1,3},{2,0},{3,1},{4,6},{5,7},{6,4},{7,5},{8,10},{9,11},{10,... | collective-permute-start | bytes 294920 | tf_op jit(solution)/shard_map/ppermute | solution.py:163
  124.5 0.1 convert_reduce_fusion
  124.6 3.4 %collective-permute-done.3 = bf16[384,128]{1,0:T(8,128)(2,1)S(1)} collective-permute-done((bf16[384,128]{1,0:T(8,128)(2,1)S(1)}, bf16[384,128]{1,0:T(8,128)(2,1)S(1)}, u32[]{:S(2)}, u32[]{:S(2)}) %collective-permute-start.3) | collective-permute-done | bytes 98336 | tf_op jit(solution)/shard_map/ppermute | solution.py:163
  128.0 0.0 slice-done
  128.0 3.7 %fusion.17 = (f32[384]{0:T(512)S(1)}, f32[384,384]{0,1:T(8,128)S(1)}) fusion(bf16[5120,128]{1,0:T(8,128)(2,1)S(1)} %bitcast.27, bf16[384,5120]{1,0:T(8,128)(2,1)} %param.4, bf16[384,128]{1,0:T(8,128)(2,1)S(1)} %add_convert_fusion, bf16[384,128]{1,0:T(8,128)(2,1)S(1)} %collective-permute-done.3, pred[]{:T(512)S(6)} %lt.48, s32[384]{0:T(512)S(1)} %convert_reduce_fusion), kind=kOutput, calls=%fused_computation.31 | convolution fusion | flops 542047872 | bytes 6032385 | tf_op jit(solution)/shard_map/dot_general | solution.py:174
  131.7 0.1 fusion.9
  131.8 0.3 fusion.10
  132.1 0.7 reshape.48.send_ref
  132.9 20.6 %shard_map.48 = f32[32,12,128]{2,1,0:T(8,128)} custom-call(f32[32,12,128]{2,1,0:T(8,128)} %reshape.48.send_ref), custom_call_target="tpu_custom_call" | custom-call | tf_op jit(solution)/shard_map/pallas_call | solution.py:105
  153.4 1.0 copy.9
  154.5 0.9 copy.10
  (3 shorter events, 0.1 us)
Async XLA Ops:
  0.9 16.0 %collective-permute-start = (bf16[2,160,128]{2,1,0:T(8,128)(2,1)S(1)}, bf16[2,160,128]{2,1,0:T(8,128)(2,1)S(1)}, u32[]{:S(2)}, u32[]{:S(2)}) collective-permute-start(bf16[2,160,128]{2,1,0:T(8,128)(2,1)S(1)} %get-tuple-element.9), channel_id=1, source_target_pairs={{0,1},{1,0},{2,3},{3,2},{4,5},{5,4},{6,7},{7,6},{8,9},{9,8},{10,11... | collective-permute-start | bytes 245768 | tf_op jit(solution)/shard_map/ppermute | solution.py:134
  62.2 14.2 %collective-permute-start.1 = (bf16[160,128]{1,0:T(8,128)(2,1)S(1)}, bf16[160,128]{1,0:T(8,128)(2,1)S(1)}, u32[]{:S(2)}, u32[]{:S(2)}) collective-permute-start(bf16[160,128]{1,0:T(8,128)(2,1)S(1)} %get-tuple-element.7), channel_id=1, source_target_pairs={{0,1},{1,0},{2,3},{3,2},{4,5},{5,4},{6,7},{7,6},{8,9},{9,8},{10,11... | collective-permute-start | bytes 122888 | tf_op jit(solution)/shard_map/ppermute | solution.py:145
  77.1 44.0 %copy-start = (s32[1,4]{1,0:T(1,128)S(1)}, s32[1,4]{1,0:T(1,128)}, u32[]{:S(2)}) copy-start(s32[1,4]{1,0:T(1,128)} %param.7) | copy-start | bytes 52
  115.8 12.2 %slice-start = ((bf16[16,480,128]{2,1,0:T(8,128)(2,1)}), bf16[16,320,128]{2,1,0:T(8,128)(2,1)S(1)}, s32[]{:S(2)}) async-start(bf16[16,480,128]{2,1,0:T(8,128)(2,1)} %shard_map.47), calls=%async_computation | async-start | bytes 2621440 | tf_op jit(solution)/shard_map/slice | solution.py:151
  118.3 3.8 %collective-permute-start.2 = (f32[384,128]{1,0:T(8,128)S(1)}, f32[384,128]{1,0:T(8,128)S(1)}, u32[]{:S(2)}, u32[]{:S(2)}) collective-permute-start(f32[384,128]{1,0:T(8,128)S(1)} %fusion.4), channel_id=1, source_target_pairs={{0,1},{1,0},{2,3},{3,2},{4,5},{5,4},{6,7},{7,6},{8,9},{9,8},{10,11... | collective-permute-start | bytes 589832 | tf_op jit(solution)/shard_map/ppermute | solution.py:161
  122.1 5.9 %collective-permute-start.3 = (bf16[384,128]{1,0:T(8,128)(2,1)S(1)}, bf16[384,128]{1,0:T(8,128)(2,1)S(1)}, u32[]{:S(2)}, u32[]{:S(2)}) collective-permute-start(bf16[384,128]{1,0:T(8,128)(2,1)S(1)} %add_convert_fusion), channel_id=1, source_target_pairs={{0,2},{1,3},{2,0},{3,1},{4,6},{5,7},{6,4},{7,5},{8,10},{9,11},{10,... | collective-permute-start | bytes 294920 | tf_op jit(solution)/shard_map/ppermute | solution.py:163

commit v5 on v3

--- a/solution.py
+++ b/solution.py
@@ -8,6 +8,73 @@
 from jax.sharding import PartitionSpec as P
 
 MESH = pl.DeviceIdType.MESH
+
+
+def ring_kernel(count, stride, chunks, send_ref, out_ref, landed, send_sems, recv_sems):
+    me = lax.axis_index("tp")
+    total = count * stride
+    right, left = lax.rem(me + stride, total), lax.rem(me + total - stride, total)
+    spot = me // stride
+    barrier = pltpu.get_barrier_semaphore()
+    for neighbour in (left, right):
+        pl.semaphore_signal(barrier, inc=1, device_id={"tp": neighbour}, device_id_type=MESH)
+    pl.semaphore_wait(barrier, 2)
+
+    def incoming(origin, chunk):
+        return pltpu.make_async_remote_copy(
+            src_ref=send_ref.at[chunk],
+            dst_ref=landed.at[origin, chunk],
+            send_sem=send_sems.at[0, 0, 0],
+            recv_sem=recv_sems.at[origin, chunk],
+            device_id={"tp": right},
+            device_id_type=MESH,
+        )
+
+    landed[spot] = send_ref[...]
+    sends = []
+    far_right, far_left = count // 2, (count - 1) // 2
+    for step in range(1, far_right + 1):
+        for chunk in range(chunks):
+            streams = [(0, right, lax.rem(spot + count - (step - 1), count))]
+            if step <= far_left:
+                streams.append((1, left, lax.rem(spot + step - 1, count)))
+            for way, target, origin in streams:
+                if step > 1:
+                    incoming(origin, chunk).wait_recv()
+                source = send_ref.at[chunk] if step == 1 else landed.at[origin, chunk]
+                copy = pltpu.make_async_remote_copy(
+                    src_ref=source,
+                    dst_ref=landed.at[origin, chunk],
+                    send_sem=send_sems.at[way, step, chunk],
+                    recv_sem=recv_sems.at[origin, chunk],
+                    device_id={"tp": target},
+                    device_id_type=MESH,
+                )
+                copy.start()
+                sends.append(copy)
+    for chunk in range(chunks):
+        incoming(lax.rem(spot + count - far_right, count), chunk).wait_recv()
+        incoming(lax.rem(spot + far_left, count), chunk).wait_recv()
+    for copy in sends:
+        copy.wait_send()
+    out_ref[...] = landed[...]
+
+
+def ring_gather(x, count, stride, chunks, collective_id):
+    x = x.reshape((chunks, x.shape[0] // chunks) + x.shape[1:])
+    gathered = pl.pallas_call(
+        functools.partial(ring_kernel, count, stride, chunks),
+        out_shape=jax.ShapeDtypeStruct((count,) + x.shape, x.dtype),
+        in_specs=[pl.BlockSpec(memory_space=pltpu.VMEM)],
+        out_specs=pl.BlockSpec(memory_space=pltpu.VMEM),
+        scratch_shapes=[
+            pltpu.VMEM((count,) + x.shape, x.dtype),
+            pltpu.SemaphoreType.DMA((2, count // 2 + 1, chunks)),
+            pltpu.SemaphoreType.DMA((count, chunks)),
+        ],
+        compiler_params=pltpu.CompilerParams(collective_id=collective_id, has_side_effects=True),
+    )(x)
+    return gathered.reshape((count * x.shape[0] * x.shape[1],) + x.shape[2:])
 
 
 def exchange_kernel(axis, count, scatter, send_ref, out_ref, landed, send_sems, recv_sems):
@@ -34,14 +101,20 @@
     landed[me] = send_ref[me] if scatter else send_ref[...]
     for copy in copies:
         copy.wait()
-    out_ref[...] = landed[...]
+    if scatter:
+        width = landed.shape[-1]
+        for source in range(count):
+            out_ref[:, source * width:(source + 1) * width] = landed[source]
+    else:
+        out_ref[...] = landed[...]
 
 
 def exchange(x, axis, count, scatter, collective_id):
     piece = x.shape[1:] if scatter else x.shape
+    result = (piece[0], count * piece[1]) if scatter else (count,) + piece
     return pl.pallas_call(
         functools.partial(exchange_kernel, axis, count, scatter),
-        out_shape=jax.ShapeDtypeStruct((count,) + piece, x.dtype),
+        out_shape=jax.ShapeDtypeStruct(result, x.dtype),
         in_specs=[pl.BlockSpec(memory_space=pltpu.VMEM)],
         out_specs=pl.BlockSpec(memory_space=pltpu.VMEM),
         scratch_shapes=[
@@ -71,8 +144,7 @@
     from_partner = lax.ppermute(other, "tp", partner_perm)
     chip_slots = jnp.where(core == 0, jnp.concatenate([mine, from_partner], axis=0),
                            jnp.concatenate([from_partner, mine], axis=0))
-    same_core = [list(range(c, tp_count, 2)) for c in range(2)]
-    all_halves = lax.all_gather(chip_slots, "tp", axis=0, tiled=True, axis_index_groups=same_core)
+    all_halves = ring_gather(chip_slots, tp_count // 2, 2, 2, 2)
     kv_id = member_id // group_size
     quarter = member_id % group_size
     kv_panel = tp_count + kv_id + kv_count * (quarter // 2)
@@ -88,12 +160,14 @@
     q_weights = gathered[:, :block_rows].reshape(grp_count * block_rows, head_dim)
     kv_weights = gathered[:, block_rows:]
 
-    query_rows = jnp.dot(tokens, q_weights, preferred_element_type=jnp.float32).astype(jnp.bfloat16)
-    token_halves = tokens.reshape(seq_total, grp_count, 2, half_rows)
-    token_half = lax.dynamic_index_in_dim(token_halves, half, axis=2, keepdims=False)
-    kv_part = jnp.einsum(
-        "sgi,gic->sc", token_half, kv_weights, preferred_element_type=jnp.float32
+    use_half = lax.broadcasted_iota(jnp.int32, (1, 2, 1, 1), 1) == half
+    kv_rows = jnp.where(use_half, kv_weights[:, None], jnp.zeros_like(kv_weights[:, None]))
+    both_weights = jnp.concatenate(
+        [q_weights, kv_rows.reshape(grp_count * block_rows, head_dim)], axis=1
     )
+    projected = jnp.dot(tokens, both_weights, preferred_element_type=jnp.float32)
+    query_rows = projected[:, :head_dim].astype(jnp.bfloat16)
+    kv_part = projected[:, head_dim:]
     pair_perm = [(i, i ^ 1) for i in range(tp_count)]
     kv_full = (kv_part + lax.ppermute(kv_part, "tp", pair_perm)).astype(jnp.bfloat16)
     swap_perm = [(i, i ^ 2) for i in range(tp_count)]
@@ -119,8 +193,7 @@
     attn_probs = (row_exp / jnp.sum(row_exp, axis=1, keepdims=True)).astype(jnp.bfloat16)
     context = jnp.dot(attn_probs, value_rows, preferred_element_type=jnp.float32)
     outgoing = context.reshape(tp_count, seq_total // tp_count, head_dim)
-    arrived = exchange(outgoing, "tp", tp_count, True, 1)
-    return jnp.transpose(arrived, (1, 0, 2)).reshape(seq_total // tp_count, tp_count * head_dim)
+    return exchange(outgoing, "tp", tp_count, True, 1)
 
 
 def solution(mesh):

time: 188 us -> 140 us (0.74)
  waiting for transfers between devices: 61.8 us -> 4.67 us
  Pallas kernels: 59.1 us -> 95.7 us
  between operations: 19.7 us -> 5.89 us
  starting transfers between devices: 26.1 us -> 21 us
  local copies, waits for them, and re-layouts: 12.1 us -> 7.73 us
  matrix products: 6.49 us -> 2.16 us
    all_gather x1 -> x0, waiting for transfers between devices: 57.4 us -> none  [on_device(): lax.all_gather(chip_slots, 'tp', axis=0, tiled=True, axis_index_groups=sa...]
    pallas_call x0 -> x1, Pallas kernels: none -> 37.8 us  [ring_gather(): pl.pallas_call(functools.partial(ring_kernel, count, stride, chunks), out...]
    ppermute x1, starting transfers between devices: 11.5 us -> 6.49 us  [on_device(): lax.ppermute(all_halves[panel_home[partner_id]], 'tp', partner_perm)]
    unnamed x5, local copies, waits for them, and re-layouts: 7.15 us -> 2.17 us
    dot_general x1, matrix products: 3.7 us -> 0.31 us  [on_device(): lax.dot_general(query_rows, key_rows, (((1,), (1,)), ((), ())), preferred...]
  transfers between devices with their start and end apart: 5 -> 4, of which waited for: 4 -> 3; matrix products, arithmetic and copies ran while one was open for 4% -> 1% of each run, Pallas kernels for 0% -> 0%
where the time goes in v5:
time: 140 us
  Pallas kernels  95.7 us (68%)
  starting transfers between devices  21 us (15%)
  local copies, waits for them, and re-layouts  7.73 us (6%)
  between operations  5.89 us (4%)
  waiting for transfers between devices  4.67 us (3%)
  other arithmetic  2.52 us (2%)
  matrix products  2.16 us (2%)
    pallas_call x2, Pallas kernels, exchange(): pl.pallas_call(functools.partial(exchange_kernel, axis, count, scatter),...  58 us
    pallas_call x1, Pallas kernels, ring_gather(): pl.pallas_call(functools.partial(ring_kernel, count, stride, chunks), out...  37.8 us
    ppermute x1, starting transfers between devices, on_device(): from_partner = lax.ppermute(other, 'tp', partner_perm)  8.79 us
    ppermute x1, starting transfers between devices, on_device(): lax.ppermute(all_halves[panel_home[partner_id]], 'tp', partner_perm)  6.49 us
    ppermute x1, waiting for transfers between devices, on_device(): kv_other = lax.ppermute(kv_full, 'tp', swap_perm)  3.17 us
    ppermute x1, starting transfers between devices, on_device(): lax.ppermute(kv_part, 'tp', pair_perm)  3.09 us
  transfers between devices with their start and end apart: 4, of which 3 were waited for; matrix products, arithmetic and copies ran while one was open for 1% of the time, Pallas kernels for 0%

profile of v5, /device:TPU:1, one launch (start us, length us, event | category | flops | bytes accessed | tf_op | source)
XLA Modules:
  0.0 139.7 jit_solution(7020168539856850670)
XLA Ops:
  0.0 0.9 constant_dynamic-slice_fusion.1
  0.9 8.8 %collective-permute-start = (bf16[2,160,128]{2,1,0:T(8,128)(2,1)S(1)}, bf16[2,160,128]{2,1,0:T(8,128)(2,1)S(1)}, u32[]{:S(2)}, u32[]{:S(2)}) collective-permute-start(bf16[2,160,128]{2,1,0:T(8,128)(2,1)S(1)} %get-tuple-element.9), channel_id=1, source_target_pairs={{0,1},{1,0},{2,3},{3,2},{4,5},{5,4},{6,7},{7,6},{8,9},{9,8},{10,11... | collective-permute-start | bytes 245768 | tf_op jit(solution)/shard_map/ppermute | solution.py:144
  9.8 1.4 %fusion.16 = (s32[1]{0:T(128)}, s32[1]{0:T(128)}, s32[1]{0:T(128)}) fusion(s32[48]{0:T(128)} %param.6, s32[]{:T(128)S(6)} %select_n.90, s32[]{:T(128)S(6)} %select_n.98, s32[]{:T(128)S(6)} %select_n.92), kind=kLoop, calls=%fused_computation.32 | loop fusion | bytes 36 | tf_op jit(solution)/shard_map/dynamic_slice | solution.py:153
  16.9 0.0 collective-permute-done
  16.9 0.7 maximum_select_fusion
  17.6 37.8 %shard_map.46 = bf16[16,2,2,160,128]{4,3,2,1,0:T(8,128)(2,1)} custom-call(bf16[2,2,160,128]{3,2,1,0:T(8,128)(2,1)} %bitcast.21), custom_call_target="tpu_custom_call" | custom-call | tf_op jit(solution)/shard_map/pallas_call | solution.py:65
  55.3 0.8 dynamic-slice_bitcast_fusion.2
  56.2 6.5 %collective-permute-start.1 = (bf16[160,128]{1,0:T(8,128)(2,1)S(1)}, bf16[160,128]{1,0:T(8,128)(2,1)S(1)}, u32[]{:S(2)}, u32[]{:S(2)}) collective-permute-start(bf16[160,128]{1,0:T(8,128)(2,1)S(1)} %get-tuple-element.7), channel_id=1, source_target_pairs={{0,1},{1,0},{2,3},{3,2},{4,5},{5,4},{6,7},{7,6},{8,9},{9,8},{10,11... | collective-permute-start | bytes 122888 | tf_op jit(solution)/shard_map/ppermute | solution.py:154
  62.7 0.1 broadcast_in_dim.44
  62.8 0.1 broadcast_in_dim.45
  62.9 0.7 collective-permute-done.1
  63.6 0.7 pad_maximum_fusion.send_ref
  64.2 36.9 %shard_map.47 = bf16[16,480,128]{2,1,0:T(8,128)(2,1)} custom-call(bf16[480,128]{1,0:T(8,128)(2,1)} %pad_maximum_fusion.send_ref), custom_call_target="tpu_custom_call" | custom-call | tf_op jit(solution)/shard_map/pallas_call | solution.py:115
  101.1 0.0 slice-start
  101.1 0.0 copy-start
  101.1 0.0 slice-start.1
  101.1 1.1 slice-done
  102.2 0.7 bitcast_select_fusion
  102.9 0.5 copy-done
  103.4 0.4 slice-done.1
  103.8 0.0 copy-start.1
  103.8 1.6 %fusion.5 = f32[384,256]{0,1:T(8,128)S(1)} fusion(bf16[384,5120]{1,0:T(8,128)(2,1)S(1)} %copy-done, bf16[5120,128]{1,0:T(8,128)(2,1)S(1)} %bitcast_select_fusion, bf16[5120,128]{1,0:T(8,128)(2,1)S(1)} %bitcast.19), kind=kOutput, calls=%fused_computation.7 | convolution fusion | flops 1011875840 | bytes 6946816 | tf_op jit(solution)/shard_map/dot_general | solution.py:168
  105.4 3.1 %collective-permute-start.2 = (f32[384,128]{0,1:T(8,128)S(1)}, f32[384,128]{0,1:T(8,128)S(1)}, u32[]{:S(2)}, u32[]{:S(2)}) collective-permute-start(f32[384,128]{0,1:T(8,128)S(1)} %slice.18), channel_id=1, source_target_pairs={{0,1},{1,0},{2,3},{3,2},{4,5},{5,4},{6,7},{7,6},{8,9},{9,8},{10,11... | collective-permute-start | bytes 589832 | tf_op jit(solution)/shard_map/ppermute | solution.py:172
  108.5 0.0 copy-done.1
  108.5 0.2 reduce-window.8
  108.7 0.9 collective-permute-done.2
  109.5 2.6 %collective-permute-start.3 = (bf16[384,128]{0,1:T(8,128)(2,1)S(1)}, bf16[384,128]{0,1:T(8,128)(2,1)S(1)}, u32[]{:S(2)}, u32[]{:S(2)}) collective-permute-start(bf16[384,128]{0,1:T(8,128)(2,1)S(1)} %add_convert_fusion), channel_id=1, source_target_pairs={{0,2},{1,3},{2,0},{3,1},{4,6},{5,7},{6,4},{7,5},{8,10},{9,11},{10,... | collective-permute-start | bytes 294920 | tf_op jit(solution)/shard_map/ppermute | solution.py:174
  112.2 0.1 convert_reduce_fusion
  112.3 3.2 %collective-permute-done.3 = bf16[384,128]{0,1:T(8,128)(2,1)S(1)} collective-permute-done((bf16[384,128]{0,1:T(8,128)(2,1)S(1)}, bf16[384,128]{0,1:T(8,128)(2,1)S(1)}, u32[]{:S(2)}, u32[]{:S(2)}) %collective-permute-start.3) | collective-permute-done | bytes 98336 | tf_op jit(solution)/shard_map/ppermute | solution.py:174
  115.5 0.3 fusion.17
  115.8 0.1 fusion.9
  115.9 0.3 fusion.10
  116.2 0.7 reshape.56.send_ref
  116.9 21.1 %shard_map.48 = f32[12,4096]{1,0:T(8,128)} custom-call(f32[32,12,128]{2,1,0:T(8,128)} %reshape.56.send_ref), custom_call_target="tpu_custom_call" | custom-call | tf_op jit(solution)/shard_map/pallas_call | solution.py:115
  138.0 1.7 %copy.6 = f32[12,4096]{1,0:T(8,128)} copy(f32[12,4096]{1,0:T(8,128)} %shard_map.48) | data formatting | bytes 393216
  (4 shorter events, 0.1 us)
Async XLA Ops:
  0.9 15.9 %collective-permute-start = (bf16[2,160,128]{2,1,0:T(8,128)(2,1)S(1)}, bf16[2,160,128]{2,1,0:T(8,128)(2,1)S(1)}, u32[]{:S(2)}, u32[]{:S(2)}) collective-permute-start(bf16[2,160,128]{2,1,0:T(8,128)(2,1)S(1)} %get-tuple-element.9), channel_id=1, source_target_pairs={{0,1},{1,0},{2,3},{3,2},{4,5},{5,4},{6,7},{7,6},{8,9},{9,8},{10,11... | collective-permute-start | bytes 245768 | tf_op jit(solution)/shard_map/ppermute | solution.py:144
  56.2 7.3 %collective-permute-start.1 = (bf16[160,128]{1,0:T(8,128)(2,1)S(1)}, bf16[160,128]{1,0:T(8,128)(2,1)S(1)}, u32[]{:S(2)}, u32[]{:S(2)}) collective-permute-start(bf16[160,128]{1,0:T(8,128)(2,1)S(1)} %get-tuple-element.7), channel_id=1, source_target_pairs={{0,1},{1,0},{2,3},{3,2},{4,5},{5,4},{6,7},{7,6},{8,9},{9,8},{10,11... | collective-permute-start | bytes 122888 | tf_op jit(solution)/shard_map/ppermute | solution.py:154
  101.1 1.1 slice-start
  101.1 2.3 %copy-start = (bf16[384,5120]{1,0:T(8,128)(2,1)S(1)}, bf16[384,5120]{1,0:T(8,128)(2,1)}, u32[]{:S(2)}) copy-start(bf16[384,5120]{1,0:T(8,128)(2,1)} %param.4) | copy-start | bytes 11796484
  101.1 2.7 %slice-start.1 = ((bf16[16,480,128]{2,1,0:T(8,128)(2,1)}), bf16[16,320,128]{2,1,0:T(8,128)(2,1)S(1)}, s32[]{:S(2)}) async-start(bf16[16,480,128]{2,1,0:T(8,128)(2,1)} %shard_map.47), calls=%async_computation.1 | async-start | bytes 2621440 | tf_op jit(solution)/shard_map/slice | solution.py:160
  103.8 4.7 %copy-start.1 = (s32[1,4]{1,0:T(1,128)S(1)}, s32[1,4]{1,0:T(1,128)}, u32[]{:S(2)}) copy-start(s32[1,4]{1,0:T(1,128)} %param.7) | copy-start | bytes 52
  105.4 4.1 %collective-permute-start.2 = (f32[384,128]{0,1:T(8,128)S(1)}, f32[384,128]{0,1:T(8,128)S(1)}, u32[]{:S(2)}, u32[]{:S(2)}) collective-permute-start(f32[384,128]{0,1:T(8,128)S(1)} %slice.18), channel_id=1, source_target_pairs={{0,1},{1,0},{2,3},{3,2},{4,5},{5,4},{6,7},{7,6},{8,9},{9,8},{10,11... | collective-permute-start | bytes 589832 | tf_op jit(solution)/shard_map/ppermute | solution.py:172
  109.5 5.9 %collective-permute-start.3 = (bf16[384,128]{0,1:T(8,128)(2,1)S(1)}, bf16[384,128]{0,1:T(8,128)(2,1)S(1)}, u32[]{:S(2)}, u32[]{:S(2)}) collective-permute-start(bf16[384,128]{0,1:T(8,128)(2,1)S(1)} %add_convert_fusion), channel_id=1, source_target_pairs={{0,2},{1,3},{2,0},{3,1},{4,6},{5,7},{6,4},{7,5},{8,10},{9,11},{10,... | collective-permute-start | bytes 294920 | tf_op jit(solution)/shard_map/ppermute | solution.py:174

commit v6 on v5

--- a/solution.py
+++ b/solution.py
@@ -77,6 +77,95 @@
     return gathered.reshape((count * x.shape[0] * x.shape[1],) + x.shape[2:])
 
 
+def grid_kernel(width, send_ref, out_ref, landed, send_sems, recv_sems):
+    me = lax.axis_index("grp")
+    core = lax.axis_index("tp") % 2
+    col, row = me % width, me // width
+
+    def node(c, r):
+        return lax.rem(r + width, width) * width + lax.rem(c + width, width)
+
+    def along(dim, c, r, k):
+        return node(c + k, r) if dim == 0 else node(c, r + k)
+
+    barrier = pltpu.get_barrier_semaphore()
+    neighbours = [node(col + 1, row), node(col - 1, row), node(col, row + 1), node(col, row - 1)]
+    for neighbour in neighbours:
+        pl.semaphore_signal(barrier, inc=1, device_id={"grp": neighbour}, device_id_type=MESH)
+    pl.semaphore_wait(barrier, 4)
+
+    landed[me] = send_ref[...]
+    sends = []
+
+    def send(source, origin, half, target):
+        copy = pltpu.make_async_remote_copy(
+            src_ref=source,
+            dst_ref=landed.at[origin, half],
+            send_sem=send_sems.at[len(sends)],
+            recv_sem=recv_sems.at[origin, half],
+            device_id={"grp": target},
+            device_id_type=MESH,
+        )
+        copy.start()
+        sends.append(copy)
+
+    def arrive(origin, half):
+        pltpu.make_async_remote_copy(
+            src_ref=send_ref.at[half],
+            dst_ref=landed.at[origin, half],
+            send_sem=send_sems.at[0],
+            recv_sem=recv_sems.at[origin, half],
+            device_id={"grp": neighbours[0]},
+            device_id_type=MESH,
+        ).wait_recv()
+
+    ahead = 1 - 2 * core
+
+    def phase(lines, half, dim):
+        for k in (1, -1):
+            for line in lines:
+                origin = along(1 - dim, col, row, line)
+                source = send_ref.at[half] if line == 0 else landed.at[origin, half]
+                send(source, origin, half, along(dim, col, row, k))
+        for line in lines:
+            for k in (1, -1):
+                arrive(along(dim, along(1 - dim, col, row, line) % width, along(1 - dim, col, row, line) // width, k), half)
+        for line in lines:
+            base = along(1 - dim, col, row, line)
+            bc, br = base % width, base // width
+            send(landed.at[along(dim, bc, br, -ahead), half], along(dim, bc, br, -ahead), half,
+                 along(dim, col, row, ahead))
+        for line in lines:
+            base = along(1 - dim, col, row, line)
+            arrive(along(dim, base % width, base // width, 2), half)
+
+    phase([0], 0, 0)
+    phase([0], 1, 1)
+    phase([0, 1, -1, 2], 0, 1)
+    phase([0, 1, -1, 2], 1, 0)
+    for copy in sends:
+        copy.wait_send()
+    out_ref[...] = landed[...]
+
+
+def grid_gather(x, width, collective_id):
+    count = width * width
+    x = x.reshape((2, x.shape[0] // 2) + x.shape[1:])
+    gathered = pl.pallas_call(
+        functools.partial(grid_kernel, width),
+        out_shape=jax.ShapeDtypeStruct((count,) + x.shape, x.dtype),
+        in_specs=[pl.BlockSpec(memory_space=pltpu.VMEM)],
+        out_specs=pl.BlockSpec(memory_space=pltpu.VMEM),
+        scratch_shapes=[
+            pltpu.VMEM((count,) + x.shape, x.dtype),
+            pltpu.SemaphoreType.DMA((2 * (count - 1),)),
+            pltpu.SemaphoreType.DMA((count, 2)),
+        ],
+        compiler_params=pltpu.CompilerParams(collective_id=collective_id, has_side_effects=True),
+    )(x)
+    return gathered.reshape((count, x.shape[0] * x.shape[1]) + x.shape[2:])
+
+
 def exchange_kernel(axis, count, scatter, send_ref, out_ref, landed, send_sems, recv_sems):
     me = lax.axis_index(axis)
     barrier = pltpu.get_barrier_semaphore()
@@ -144,7 +233,7 @@
     from_partner = lax.ppermute(other, "tp", partner_perm)
     chip_slots = jnp.where(core == 0, jnp.concatenate([mine, from_partner], axis=0),
                            jnp.concatenate([from_partner, mine], axis=0))
-    all_halves = ring_gather(chip_slots, tp_count // 2, 2, 2, 2)
+    all_halves = ring_gather(chip_slots, tp_count // 2, 2, 4, 2)
     kv_id = member_id // group_size
     quarter = member_id % group_size
     kv_panel = tp_count + kv_id + kv_count * (quarter // 2)
@@ -156,7 +245,7 @@
                         jnp.concatenate([q_theirs, q_mine], axis=0))
     kv_half = all_halves[panel_home[kv_panel]]
     piece = jnp.concatenate([q_block, kv_half], axis=0)
-    gathered = exchange(piece, "grp", grp_count, False, 0)
+    gathered = grid_gather(piece, 4, 0)
     q_weights = gathered[:, :block_rows].reshape(grp_count * block_rows, head_dim)
     kv_weights = gathered[:, block_rows:]
 

time: 140 us -> 150 us (1.071)
  starting transfers between devices: 21 us -> 28.1 us
    pallas_call x0 -> x1, Pallas kernels: none -> 38.8 us  [grid_gather(): pl.pallas_call(functools.partial(grid_kernel, width), out_shape=jax.Shape...]
    pallas_call x2 -> x1, Pallas kernels: 58 us -> 21.2 us  [exchange(): pl.pallas_call(functools.partial(exchange_kernel, axis, count, scatter),...]
    ppermute x1, starting transfers between devices: 3.09 us -> 11.9 us  [on_device(): lax.ppermute(kv_part, 'tp', pair_perm)]
where the time goes in v6:
time: 150 us; the launch traced here: 149 us
  Pallas kernels  97 us (65%)
  starting transfers between devices  28.1 us (19%)
  local copies, waits for them, and re-layouts  8.68 us (6%)
  between operations  5.91 us (4%)
  waiting for transfers between devices  4.99 us (3%)
  other arithmetic  2.52 us (2%)
  matrix products  2.17 us (1%)
    pallas_call x1, Pallas kernels, grid_gather(): pl.pallas_call(functools.partial(grid_kernel, width), out_shape=jax.Shape...  38.8 us
    pallas_call x1, Pallas kernels, ring_gather(): pl.pallas_call(functools.partial(ring_kernel, count, stride, chunks), out...  37 us
    pallas_call x1, Pallas kernels, exchange(): pl.pallas_call(functools.partial(exchange_kernel, axis, count, scatter),...  21.2 us
    ppermute x1, starting transfers between devices, on_device(): lax.ppermute(kv_part, 'tp', pair_perm)  11.9 us
    ppermute x1, starting transfers between devices, on_device(): from_partner = lax.ppermute(other, 'tp', partner_perm)  8.79 us
    ppermute x1, starting transfers between devices, on_device(): lax.ppermute(all_halves[panel_home[partner_id]], 'tp', partner_perm)  5.06 us
    ppermute x1, waiting for transfers between devices, on_device(): kv_other = lax.ppermute(kv_full, 'tp', swap_perm)  3.48 us
  transfers between devices with their start and end apart: 4, of which 3 were waited for; matrix products, arithmetic and copies ran while one was open for 1% of the time, Pallas kernels for 0%

profile of v6, /device:TPU:1, one launch (start us, length us, event | category | flops | bytes accessed | tf_op | source)
XLA Modules:
  0.0 149.3 jit_solution(12646824827402421664)
XLA Ops:
  0.0 0.9 dynamic-slice_bitcast_fusion
  0.9 8.8 %collective-permute-start = (bf16[2,160,128]{2,1,0:T(8,128)(2,1)S(1)}, bf16[2,160,128]{2,1,0:T(8,128)(2,1)S(1)}, u32[]{:S(2)}, u32[]{:S(2)}) collective-permute-start(bf16[2,160,128]{2,1,0:T(8,128)(2,1)S(1)} %get-tuple-element.9), channel_id=1, source_target_pairs={{0,1},{1,0},{2,3},{3,2},{4,5},{5,4},{6,7},{7,6},{8,9},{9,8},{10,11... | collective-permute-start | bytes 245768 | tf_op jit(solution)/shard_map/ppermute | solution.py:233
  9.8 1.4 fusion.16
  16.9 0.0 collective-permute-done
  16.9 0.7 maximum_select_fusion.send_ref
  17.6 37.0 %shard_map.46 = bf16[16,4,1,160,128]{4,3,2,1,0:T(8,128)(2,1)} custom-call(bf16[4,1,160,128]{3,2,1,0:T(8,128)(2,1)} %maximum_select_fusion.send_ref), custom_call_target="tpu_custom_call" | custom-call | tf_op jit(solution)/shard_map/pallas_call | solution.py:65
  54.6 0.8 dynamic-slice_bitcast_fusion.3
  55.5 5.1 %collective-permute-start.1 = (bf16[160,128]{1,0:T(8,128)(2,1)S(1)}, bf16[160,128]{1,0:T(8,128)(2,1)S(1)}, u32[]{:S(2)}, u32[]{:S(2)}) collective-permute-start(bf16[160,128]{1,0:T(8,128)(2,1)S(1)} %get-tuple-element.7), channel_id=1, source_target_pairs={{0,1},{1,0},{2,3},{3,2},{4,5},{5,4},{6,7},{7,6},{8,9},{9,8},{10,11... | collective-permute-start | bytes 122888 | tf_op jit(solution)/shard_map/ppermute | solution.py:243
  60.6 0.1 broadcast_in_dim.44
  60.6 0.1 broadcast_in_dim.45
  60.7 0.7 collective-permute-done.1
  61.4 0.7 pad_maximum_fusion
  62.1 38.8 %shard_map.47 = bf16[16,2,240,128]{3,2,1,0:T(8,128)(2,1)} custom-call(bf16[2,240,128]{2,1,0:T(8,128)(2,1)} %bitcast.27), custom_call_target="tpu_custom_call" | custom-call | tf_op jit(solution)/shard_map/pallas_call | solution.py:154
  100.9 1.1 slice.18
  102.0 0.0 copy-start
  102.0 1.6 %slice.17 = bf16[16,320,128]{2,1,0:T(8,128)(2,1)S(1)} slice(bf16[16,480,128]{2,1,0:T(8,128)(2,1)} %bitcast.24), slice={[0:16], [0:320], [0:128]} | slice | bytes 2621440 | tf_op jit(solution)/shard_map/slice | solution.py:249
  103.6 0.7 bitcast_select_fusion
  104.4 0.2 copy-done
  104.5 0.0 copy-start.1
  104.5 1.6 %fusion.5 = f32[384,256]{0,1:T(8,128)S(1)} fusion(bf16[384,5120]{1,0:T(8,128)(2,1)S(1)} %copy-done, bf16[5120,128]{1,0:T(8,128)(2,1)S(1)} %bitcast_select_fusion, bf16[5120,128]{1,0:T(8,128)(2,1)S(1)} %bitcast.26), kind=kOutput, calls=%fused_computation.7 | convolution fusion | flops 1011875840 | bytes 6946816 | tf_op jit(solution)/shard_map/dot_general | solution.py:257
  106.1 11.9 %collective-permute-start.2 = (f32[384,128]{0,1:T(8,128)S(1)}, f32[384,128]{0,1:T(8,128)S(1)}, u32[]{:S(2)}, u32[]{:S(2)}) collective-permute-start(f32[384,128]{0,1:T(8,128)S(1)} %slice.20), channel_id=1, source_target_pairs={{0,1},{1,0},{2,3},{3,2},{4,5},{5,4},{6,7},{7,6},{8,9},{9,8},{10,11... | collective-permute-start | bytes 589832 | tf_op jit(solution)/shard_map/ppermute | solution.py:261
  118.1 0.0 copy-done.1
  118.1 0.2 reduce-window.8
  118.3 0.9 collective-permute-done.2
  119.1 2.3 %collective-permute-start.3 = (bf16[384,128]{0,1:T(8,128)(2,1)S(1)}, bf16[384,128]{0,1:T(8,128)(2,1)S(1)}, u32[]{:S(2)}, u32[]{:S(2)}) collective-permute-start(bf16[384,128]{0,1:T(8,128)(2,1)S(1)} %add_convert_fusion), channel_id=1, source_target_pairs={{0,2},{1,3},{2,0},{3,1},{4,6},{5,7},{6,4},{7,5},{8,10},{9,11},{10,... | collective-permute-start | bytes 294920 | tf_op jit(solution)/shard_map/ppermute | solution.py:263
  121.5 0.1 convert_reduce_fusion
  121.6 3.5 %collective-permute-done.3 = bf16[384,128]{0,1:T(8,128)(2,1)S(1)} collective-permute-done((bf16[384,128]{0,1:T(8,128)(2,1)S(1)}, bf16[384,128]{0,1:T(8,128)(2,1)S(1)}, u32[]{:S(2)}, u32[]{:S(2)}) %collective-permute-start.3) | collective-permute-done | bytes 98336 | tf_op jit(solution)/shard_map/ppermute | solution.py:263
  125.0 0.3 fusion.17
  125.4 0.1 fusion.9
  125.5 0.3 fusion.10
  125.8 0.7 reshape.115.send_ref
  126.5 21.2 %shard_map.48 = f32[12,4096]{1,0:T(8,128)} custom-call(f32[32,12,128]{2,1,0:T(8,128)} %reshape.115.send_ref), custom_call_target="tpu_custom_call" | custom-call | tf_op jit(solution)/shard_map/pallas_call | solution.py:204
  147.7 1.7 %copy.6 = f32[12,4096]{1,0:T(8,128)} copy(f32[12,4096]{1,0:T(8,128)} %shard_map.48) | data formatting | bytes 393216
  (4 shorter events, 0.1 us)
Async XLA Ops:
  0.9 16.0 %collective-permute-start = (bf16[2,160,128]{2,1,0:T(8,128)(2,1)S(1)}, bf16[2,160,128]{2,1,0:T(8,128)(2,1)S(1)}, u32[]{:S(2)}, u32[]{:S(2)}) collective-permute-start(bf16[2,160,128]{2,1,0:T(8,128)(2,1)S(1)} %get-tuple-element.9), channel_id=1, source_target_pairs={{0,1},{1,0},{2,3},{3,2},{4,5},{5,4},{6,7},{7,6},{8,9},{9,8},{10,11... | collective-permute-start | bytes 245768 | tf_op jit(solution)/shard_map/ppermute | solution.py:233
  55.5 5.9 %collective-permute-start.1 = (bf16[160,128]{1,0:T(8,128)(2,1)S(1)}, bf16[160,128]{1,0:T(8,128)(2,1)S(1)}, u32[]{:S(2)}, u32[]{:S(2)}) collective-permute-start(bf16[160,128]{1,0:T(8,128)(2,1)S(1)} %get-tuple-element.7), channel_id=1, source_target_pairs={{0,1},{1,0},{2,3},{3,2},{4,5},{5,4},{6,7},{7,6},{8,9},{9,8},{10,11... | collective-permute-start | bytes 122888 | tf_op jit(solution)/shard_map/ppermute | solution.py:243
  102.0 2.5 %copy-start = (bf16[384,5120]{1,0:T(8,128)(2,1)S(1)}, bf16[384,5120]{1,0:T(8,128)(2,1)}, u32[]{:S(2)}) copy-start(bf16[384,5120]{1,0:T(8,128)(2,1)} %param.4) | copy-start | bytes 11796484
  104.5 13.5 %copy-start.1 = (s32[1,4]{1,0:T(1,128)S(1)}, s32[1,4]{1,0:T(1,128)}, u32[]{:S(2)}) copy-start(s32[1,4]{1,0:T(1,128)} %param.7) | copy-start | bytes 52
  106.1 13.0 %collective-permute-start.2 = (f32[384,128]{0,1:T(8,128)S(1)}, f32[384,128]{0,1:T(8,128)S(1)}, u32[]{:S(2)}, u32[]{:S(2)}) collective-permute-start(f32[384,128]{0,1:T(8,128)S(1)} %slice.20), channel_id=1, source_target_pairs={{0,1},{1,0},{2,3},{3,2},{4,5},{5,4},{6,7},{7,6},{8,9},{9,8},{10,11... | collective-permute-start | bytes 589832 | tf_op jit(solution)/shard_map/ppermute | solution.py:261
  119.1 5.9 %collective-permute-start.3 = (bf16[384,128]{0,1:T(8,128)(2,1)S(1)}, bf16[384,128]{0,1:T(8,128)(2,1)S(1)}, u32[]{:S(2)}, u32[]{:S(2)}) collective-permute-start(bf16[384,128]{0,1:T(8,128)(2,1)S(1)} %add_convert_fusion), channel_id=1, source_target_pairs={{0,2},{1,3},{2,0},{3,1},{4,6},{5,7},{6,4},{7,5},{8,10},{9,11},{10,... | collective-permute-start | bytes 294920 | tf_op jit(solution)/shard_map/ppermute | solution.py:263

commit v7 on v6

--- a/solution.py
+++ b/solution.py
@@ -77,6 +77,92 @@
     return gathered.reshape((count * x.shape[0] * x.shape[1],) + x.shape[2:])
 
 
+def chip_ring_kernel(count, panels_ref, out_ref, landed, send_sems, recv_sems):
+    me = lax.axis_index("tp")
+    total = 2 * count
+    core = me % 2
+    partner = me + 1 - 2 * core
+    right, left = lax.rem(me + 2, total), lax.rem(me + total - 2, total)
+    spot = me // 2
+    half = panels_ref.shape[1] // 2
+    barrier = pltpu.get_barrier_semaphore()
+    for neighbour in (left, right, partner):
+        pl.semaphore_signal(barrier, inc=1, device_id={"tp": neighbour}, device_id_type=MESH)
+    pl.semaphore_wait(barrier, 3)
+
+    def rows_of(slot, which):
+        return panels_ref.at[slot, pl.ds(pl.multiple_of(which * half, 16), half)]
+
+    def incoming(origin, chunk):
+        return pltpu.make_async_remote_copy(
+            src_ref=rows_of(0, 0),
+            dst_ref=landed.at[origin, chunk],
+            send_sem=send_sems.at[0, 0, 0],
+            recv_sem=recv_sems.at[origin, chunk],
+            device_id={"tp": right},
+            device_id_type=MESH,
+        )
+
+    sends = []
+
+    def send(source, origin, chunk, sem, target):
+        copy = pltpu.make_async_remote_copy(
+            src_ref=source,
+            dst_ref=landed.at[origin, chunk],
+            send_sem=sem,
+            recv_sem=recv_sems.at[origin, chunk],
+            device_id={"tp": target},
+            device_id_type=MESH,
+        )
+        copy.start()
+        sends.append(copy)
+
+    own = [2 * core + j for j in range(2)]
+    theirs = [2 * (1 - core) + j for j in range(2)]
+    for j in range(2):
+        send(rows_of(j, 1 - core), spot, own[j], send_sems.at[0, 0, 1 + j], partner)
+        landed[spot, own[j]] = rows_of(j, core)[...]
+    far_right, far_left = count // 2, (count - 1) // 2
+    first = [(rows_of(j, core), own[j]) for j in range(2)] + [(None, theirs[j]) for j in range(2)]
+    for position, (source, chunk) in enumerate(first):
+        if source is None:
+            incoming(spot, chunk).wait_recv()
+            source = landed.at[spot, chunk]
+        send(source, spot, chunk, send_sems.at[0, 1, position], right)
+        if far_left >= 1:
+            send(source, spot, chunk, send_sems.at[1, 1, position], left)
+    for step in range(2, far_right + 1):
+        for chunk in range(4):
+            streams = [(0, right, lax.rem(spot + count - (step - 1), count))]
+            if step <= far_left:
+                streams.append((1, left, lax.rem(spot + step - 1, count)))
+            for way, target, origin in streams:
+                incoming(origin, chunk).wait_recv()
+                send(landed.at[origin, chunk], origin, chunk, send_sems.at[way, step, chunk], target)
+    for chunk in range(4):
+        incoming(lax.rem(spot + count - far_right, count), chunk).wait_recv()
+        incoming(lax.rem(spot + far_left, count), chunk).wait_recv()
+    for copy in sends:
+        copy.wait_send()
+    out_ref[...] = landed[...]
+
+
+def chip_ring_gather(panels, count, collective_id):
+    slots, rows, width = panels.shape
+    return pl.pallas_call(
+        functools.partial(chip_ring_kernel, count),
+        out_shape=jax.ShapeDtypeStruct((count, 2 * slots, rows // 2, width), panels.dtype),
+        in_specs=[pl.BlockSpec(memory_space=pltpu.VMEM)],
+        out_specs=pl.BlockSpec(memory_space=pltpu.VMEM),
+        scratch_shapes=[
+            pltpu.VMEM((count, 2 * slots, rows // 2, width), panels.dtype),
+            pltpu.SemaphoreType.DMA((2, count // 2 + 1, 2 * slots)),
+            pltpu.SemaphoreType.DMA((count, 2 * slots)),
+        ],
+        compiler_params=pltpu.CompilerParams(collective_id=collective_id, has_side_effects=True),
+    )(panels)
+
+
 def grid_kernel(width, send_ref, out_ref, landed, send_sems, recv_sems):
     me = lax.axis_index("grp")
     core = lax.axis_index("tp") % 2
@@ -228,12 +314,8 @@
 
     core = member_id % 2
     partner_perm = [(i, i ^ 1) for i in range(tp_count)]
-    mine = lax.dynamic_slice_in_dim(trainer_panels, core * half_rows, half_rows, axis=1)
-    other = lax.dynamic_slice_in_dim(trainer_panels, (1 - core) * half_rows, half_rows, axis=1)
-    from_partner = lax.ppermute(other, "tp", partner_perm)
-    chip_slots = jnp.where(core == 0, jnp.concatenate([mine, from_partner], axis=0),
-                           jnp.concatenate([from_partner, mine], axis=0))
-    all_halves = ring_gather(chip_slots, tp_count // 2, 2, 4, 2)
+    all_halves = chip_ring_gather(trainer_panels, tp_count // 2, 2)
+    all_halves = all_halves.reshape((-1,) + all_halves.shape[2:])
     kv_id = member_id // group_size
     quarter = member_id % group_size
     kv_panel = tp_count + kv_id + kv_count * (quarter // 2)
@@ -245,7 +327,7 @@
                         jnp.concatenate([q_theirs, q_mine], axis=0))
     kv_half = all_halves[panel_home[kv_panel]]
     piece = jnp.concatenate([q_block, kv_half], axis=0)
-    gathered = grid_gather(piece, 4, 0)
+    gathered = exchange(piece, "grp", grp_count, False, 0)
     q_weights = gathered[:, :block_rows].reshape(grp_count * block_rows, head_dim)
     kv_weights = gathered[:, block_rows:]
 

time: 150 us -> 133 us (0.89)
  starting transfers between devices: 28.1 us -> 9.24 us
  Pallas kernels: 97 us -> 102 us
  local copies, waits for them, and re-layouts: 8.68 us -> 6.78 us
    pallas_call x1 -> x2, Pallas kernels: 21.2 us -> 57.4 us  [exchange(): pl.pallas_call(functools.partial(exchange_kernel, axis, count, scatter),...]
    pallas_call x2 -> x1, Pallas kernels: 75.8 us -> 44.8 us  [chip_ring_gather(): pl.pallas_call(functools.partial(chip_ring_kernel, count), out_shape=jax....]
    ppermute x1, starting transfers between devices: 11.9 us -> 3.09 us  [on_device(): lax.ppermute(kv_part, 'tp', pair_perm)]
    ppermute x1 -> x0, starting transfers between devices: 8.79 us -> none  [on_device(): from_partner = lax.ppermute(other, 'tp', partner_perm)]
  transfers between devices with their start and end apart: 4 -> 3, of which waited for: 3 -> 3; matrix products, arithmetic and copies ran while one was open for 1% -> 0% of each run, Pallas kernels for 0% -> 0%
where the time goes in v7:
time: 133 us
  Pallas kernels  102 us (77%)
  starting transfers between devices  9.24 us (7%)
  local copies, waits for them, and re-layouts  6.78 us (5%)
  between operations  5.69 us (4%)
  waiting for transfers between devices  4.89 us (4%)
  matrix products  2.16 us (2%)
  other arithmetic  1.84 us (1%)
    pallas_call x2, Pallas kernels, exchange(): pl.pallas_call(functools.partial(exchange_kernel, axis, count, scatter),...  57.4 us
    pallas_call x1, Pallas kernels, chip_ring_gather(): pl.pallas_call(functools.partial(chip_ring_kernel, count), out_shape=jax....  44.8 us
    ppermute x1, starting transfers between devices, on_device(): lax.ppermute(all_halves[panel_home[partner_id]], 'tp', partner_perm)  3.74 us
    ppermute x1, waiting for transfers between devices, on_device(): kv_other = lax.ppermute(kv_full, 'tp', swap_perm)  3.4 us
    ppermute x1, starting transfers between devices, on_device(): lax.ppermute(kv_part, 'tp', pair_perm)  3.09 us
  transfers between devices with their start and end apart: 3, of which 3 were waited for; matrix products, arithmetic and copies ran while one was open for 0% of the time, Pallas kernels for 0%

profile of v7, /device:TPU:1, one launch (start us, length us, event | category | flops | bytes accessed | tf_op | source)
XLA Modules:
  0.0 132.7 jit_solution(3363407218345342182)
XLA Ops:
  0.0 1.4 %fusion.16 = (s32[1]{0:T(128)}, s32[1]{0:T(128)}, s32[1]{0:T(128)}) fusion(s32[48]{0:T(128)} %param.6, s32[]{:T(128)S(6)} %select_n.67, s32[]{:T(128)S(6)} %select_n.75, s32[]{:T(128)S(6)} %select_n.69), kind=kLoop, calls=%fused_computation.29 | loop fusion | bytes 36 | tf_op jit(solution)/shard_map/dynamic_slice | solution.py:324
  5.1 44.8 %shard_map.46 = bf16[16,4,160,128]{3,2,1,0:T(8,128)(2,1)} custom-call(bf16[2,320,128]{2,1,0:T(8,128)(2,1)} %panels_ref.1), custom_call_target="tpu_custom_call" | custom-call | tf_op jit(solution)/shard_map/pallas_call | solution.py:152
  51.7 0.8 dynamic-slice_bitcast_fusion.2
  52.6 3.7 %collective-permute-start = (bf16[160,128]{1,0:T(8,128)(2,1)S(1)}, bf16[160,128]{1,0:T(8,128)(2,1)S(1)}, u32[]{:S(2)}, u32[]{:S(2)}) collective-permute-start(bf16[160,128]{1,0:T(8,128)(2,1)S(1)} %get-tuple-element.7), channel_id=1, source_target_pairs={{0,1},{1,0},{2,3},{3,2},{4,5},{5,4},{6,7},{7,6},{8,9},{9,8},{10,11... | collective-permute-start | bytes 122888 | tf_op jit(solution)/shard_map/ppermute | solution.py:325
  56.3 0.1 broadcast_in_dim.44
  56.4 0.1 broadcast_in_dim.45
  56.5 0.6 collective-permute-done
  57.2 0.7 pad_maximum_fusion.send_ref
  57.8 36.8 %shard_map.47 = bf16[16,480,128]{2,1,0:T(8,128)(2,1)} custom-call(bf16[480,128]{1,0:T(8,128)(2,1)} %pad_maximum_fusion.send_ref), custom_call_target="tpu_custom_call" | custom-call | tf_op jit(solution)/shard_map/pallas_call | solution.py:290
  94.7 0.0 slice-start
  94.7 0.0 copy-start
  94.7 0.0 slice-start.1
  94.7 1.1 slice-done
  95.8 0.7 bitcast_select_fusion
  96.5 0.5 copy-done
  97.0 0.4 slice-done.1
  97.4 0.0 copy-start.1
  97.4 1.6 %fusion.5 = f32[384,256]{0,1:T(8,128)S(1)} fusion(bf16[384,5120]{1,0:T(8,128)(2,1)S(1)} %copy-done, bf16[5120,128]{1,0:T(8,128)(2,1)S(1)} %bitcast_select_fusion, bf16[5120,128]{1,0:T(8,128)(2,1)S(1)} %bitcast.18), kind=kOutput, calls=%fused_computation.7 | convolution fusion | flops 1011875840 | bytes 6946816 | tf_op jit(solution)/shard_map/dot_general | solution.py:339
  99.0 3.1 %collective-permute-start.1 = (f32[384,128]{0,1:T(8,128)S(1)}, f32[384,128]{0,1:T(8,128)S(1)}, u32[]{:S(2)}, u32[]{:S(2)}) collective-permute-start(f32[384,128]{0,1:T(8,128)S(1)} %slice.18), channel_id=1, source_target_pairs={{0,1},{1,0},{2,3},{3,2},{4,5},{5,4},{6,7},{7,6},{8,9},{9,8},{10,11... | collective-permute-start | bytes 589832 | tf_op jit(solution)/shard_map/ppermute | solution.py:343
  102.1 0.0 copy-done.1
  102.1 0.2 reduce-window.8
  102.3 0.9 collective-permute-done.1
  103.2 2.4 %collective-permute-start.2 = (bf16[384,128]{0,1:T(8,128)(2,1)S(1)}, bf16[384,128]{0,1:T(8,128)(2,1)S(1)}, u32[]{:S(2)}, u32[]{:S(2)}) collective-permute-start(bf16[384,128]{0,1:T(8,128)(2,1)S(1)} %add_convert_fusion), channel_id=1, source_target_pairs={{0,2},{1,3},{2,0},{3,1},{4,6},{5,7},{6,4},{7,5},{8,10},{9,11},{10,... | collective-permute-start | bytes 294920 | tf_op jit(solution)/shard_map/ppermute | solution.py:345
  105.6 0.1 convert_reduce_fusion
  105.7 3.4 %collective-permute-done.2 = bf16[384,128]{0,1:T(8,128)(2,1)S(1)} collective-permute-done((bf16[384,128]{0,1:T(8,128)(2,1)S(1)}, bf16[384,128]{0,1:T(8,128)(2,1)S(1)}, u32[]{:S(2)}, u32[]{:S(2)}) %collective-permute-start.2) | collective-permute-done | bytes 98336 | tf_op jit(solution)/shard_map/ppermute | solution.py:345
  109.1 0.3 fusion.17
  109.4 0.1 fusion.9
  109.5 0.3 fusion.10
  109.8 0.7 reshape.51.send_ref
  110.5 20.5 %shard_map.48 = f32[12,4096]{1,0:T(8,128)} custom-call(f32[32,12,128]{2,1,0:T(8,128)} %reshape.51.send_ref), custom_call_target="tpu_custom_call" | custom-call | tf_op jit(solution)/shard_map/pallas_call | solution.py:290
  131.1 1.7 %copy.6 = f32[12,4096]{1,0:T(8,128)} copy(f32[12,4096]{1,0:T(8,128)} %shard_map.48) | data formatting | bytes 393216
  (4 shorter events, 0.1 us)
Async XLA Ops:
  52.6 4.6 %collective-permute-start = (bf16[160,128]{1,0:T(8,128)(2,1)S(1)}, bf16[160,128]{1,0:T(8,128)(2,1)S(1)}, u32[]{:S(2)}, u32[]{:S(2)}) collective-permute-start(bf16[160,128]{1,0:T(8,128)(2,1)S(1)} %get-tuple-element.7), channel_id=1, source_target_pairs={{0,1},{1,0},{2,3},{3,2},{4,5},{5,4},{6,7},{7,6},{8,9},{9,8},{10,11... | collective-permute-start | bytes 122888 | tf_op jit(solution)/shard_map/ppermute | solution.py:325
  94.7 1.1 slice-start
  94.7 2.3 %copy-start = (bf16[384,5120]{1,0:T(8,128)(2,1)S(1)}, bf16[384,5120]{1,0:T(8,128)(2,1)}, u32[]{:S(2)}) copy-start(bf16[384,5120]{1,0:T(8,128)(2,1)} %param.4) | copy-start | bytes 11796484
  94.7 2.7 %slice-start.1 = ((bf16[16,480,128]{2,1,0:T(8,128)(2,1)}), bf16[16,320,128]{2,1,0:T(8,128)(2,1)S(1)}, s32[]{:S(2)}) async-start(bf16[16,480,128]{2,1,0:T(8,128)(2,1)} %shard_map.47), calls=%async_computation.1 | async-start | bytes 2621440 | tf_op jit(solution)/shard_map/slice | solution.py:331
  97.4 4.7 %copy-start.1 = (s32[1,4]{1,0:T(1,128)S(1)}, s32[1,4]{1,0:T(1,128)}, u32[]{:S(2)}) copy-start(s32[1,4]{1,0:T(1,128)} %param.7) | copy-start | bytes 52
  99.0 4.1 %collective-permute-start.1 = (f32[384,128]{0,1:T(8,128)S(1)}, f32[384,128]{0,1:T(8,128)S(1)}, u32[]{:S(2)}, u32[]{:S(2)}) collective-permute-start(f32[384,128]{0,1:T(8,128)S(1)} %slice.18), channel_id=1, source_target_pairs={{0,1},{1,0},{2,3},{3,2},{4,5},{5,4},{6,7},{7,6},{8,9},{9,8},{10,11... | collective-permute-start | bytes 589832 | tf_op jit(solution)/shard_map/ppermute | solution.py:343
  103.2 5.9 %collective-permute-start.2 = (bf16[384,128]{0,1:T(8,128)(2,1)S(1)}, bf16[384,128]{0,1:T(8,128)(2,1)S(1)}, u32[]{:S(2)}, u32[]{:S(2)}) collective-permute-start(bf16[384,128]{0,1:T(8,128)(2,1)S(1)} %add_convert_fusion), channel_id=1, source_target_pairs={{0,2},{1,3},{2,0},{3,1},{4,6},{5,7},{6,4},{7,5},{8,10},{9,11},{10,... | collective-permute-start | bytes 294920 | tf_op jit(solution)/shard_map/ppermute | solution.py:345

commit v8 on v7

--- a/solution.py
+++ b/solution.py
@@ -252,13 +252,14 @@
     return gathered.reshape((count, x.shape[0] * x.shape[1]) + x.shape[2:])
 
 
-def exchange_kernel(axis, count, scatter, send_ref, out_ref, landed, send_sems, recv_sems):
+def exchange_kernel(axis, count, scatter, own_barrier, send_ref, out_ref, landed, send_sems, recv_sems):
     me = lax.axis_index(axis)
-    barrier = pltpu.get_barrier_semaphore()
-    for step in range(1, count):
-        peer = lax.rem(me + step, count)
-        pl.semaphore_signal(barrier, inc=1, device_id={axis: peer}, device_id_type=MESH)
-    pl.semaphore_wait(barrier, count - 1)
+    if own_barrier:
+        barrier = pltpu.get_barrier_semaphore()
+        for step in range(1, count):
+            peer = lax.rem(me + step, count)
+            pl.semaphore_signal(barrier, inc=1, device_id={axis: peer}, device_id_type=MESH)
+        pl.semaphore_wait(barrier, count - 1)
     copies = []
     for step in range(1, count):
         peer = lax.rem(me + step, count)
@@ -287,8 +288,10 @@
 def exchange(x, axis, count, scatter, collective_id):
     piece = x.shape[1:] if scatter else x.shape
     result = (piece[0], count * piece[1]) if scatter else (count,) + piece
+    own_barrier = collective_id is not None
+    params = dict(collective_id=collective_id) if own_barrier else {}
     return pl.pallas_call(
-        functools.partial(exchange_kernel, axis, count, scatter),
+        functools.partial(exchange_kernel, axis, count, scatter, own_barrier),
         out_shape=jax.ShapeDtypeStruct(result, x.dtype),
         in_specs=[pl.BlockSpec(memory_space=pltpu.VMEM)],
         out_specs=pl.BlockSpec(memory_space=pltpu.VMEM),
@@ -297,7 +300,7 @@
             pltpu.SemaphoreType.DMA((count,)),
             pltpu.SemaphoreType.DMA((count,)),
         ],
-        compiler_params=pltpu.CompilerParams(collective_id=collective_id, has_side_effects=True),
+        compiler_params=pltpu.CompilerParams(has_side_effects=True, **params),
     )(x)
 
 
@@ -364,7 +367,7 @@
     attn_probs = (row_exp / jnp.sum(row_exp, axis=1, keepdims=True)).astype(jnp.bfloat16)
     context = jnp.dot(attn_probs, value_rows, preferred_element_type=jnp.float32)
     outgoing = context.reshape(tp_count, seq_total // tp_count, head_dim)
-    return exchange(outgoing, "tp", tp_count, True, 1)
+    return exchange(outgoing, "tp", tp_count, True, None)
 
 
 def solution(mesh):

time: 133 us -> 147 us (1.11)
  Pallas kernels: 102 us -> 116 us
    pallas_call x2, Pallas kernels: 57.4 us -> 71.2 us  [exchange(): pl.pallas_call(functools.partial(exchange_kernel, axis, count, scatter, o...]
where the time goes in v8:
time: 147 us
  Pallas kernels  116 us (79%)
  starting transfers between devices  9.24 us (6%)
  local copies, waits for them, and re-layouts  6.78 us (5%)
  between operations  5.69 us (4%)
  waiting for transfers between devices  4.89 us (3%)
  matrix products  2.16 us (1%)
  other arithmetic  1.84 us (1%)
    pallas_call x2, Pallas kernels, exchange(): pl.pallas_call(functools.partial(exchange_kernel, axis, count, scatter, o...  71.2 us
    pallas_call x1, Pallas kernels, chip_ring_gather(): pl.pallas_call(functools.partial(chip_ring_kernel, count), out_shape=jax....  44.8 us
    ppermute x1, starting transfers between devices, on_device(): lax.ppermute(all_halves[panel_home[partner_id]], 'tp', partner_perm)  3.74 us
    ppermute x1, waiting for transfers between devices, on_device(): kv_other = lax.ppermute(kv_full, 'tp', swap_perm)  3.4 us
    ppermute x1, starting transfers between devices, on_device(): lax.ppermute(kv_part, 'tp', pair_perm)  3.09 us
  transfers between devices with their start and end apart: 3, of which 3 were waited for; matrix products, arithmetic and copies ran while one was open for 0% of the time, Pallas kernels for 0%

profile of v8, /device:TPU:1, one launch (start us, length us, event | category | flops | bytes accessed | tf_op | source)
XLA Modules:
  0.0 146.6 jit_solution(8301808493483794768)
XLA Ops:
  0.0 1.4 fusion.16
  5.1 44.8 %shard_map.46 = bf16[16,4,160,128]{3,2,1,0:T(8,128)(2,1)} custom-call(bf16[2,320,128]{2,1,0:T(8,128)(2,1)} %panels_ref.1), custom_call_target="tpu_custom_call" | custom-call | tf_op jit(solution)/shard_map/pallas_call | solution.py:152
  51.7 0.8 dynamic-slice_bitcast_fusion.2
  52.6 3.7 %collective-permute-start = (bf16[160,128]{1,0:T(8,128)(2,1)S(1)}, bf16[160,128]{1,0:T(8,128)(2,1)S(1)}, u32[]{:S(2)}, u32[]{:S(2)}) collective-permute-start(bf16[160,128]{1,0:T(8,128)(2,1)S(1)} %get-tuple-element.7), channel_id=1, source_target_pairs={{0,1},{1,0},{2,3},{3,2},{4,5},{5,4},{6,7},{7,6},{8,9},{9,8},{10,11... | collective-permute-start | bytes 122888 | tf_op jit(solution)/shard_map/ppermute | solution.py:328
  56.3 0.1 broadcast_in_dim.44
  56.4 0.1 broadcast_in_dim.45
  56.5 0.6 collective-permute-done
  57.2 0.7 pad_maximum_fusion.send_ref
  57.8 36.8 %shard_map.47 = bf16[16,480,128]{2,1,0:T(8,128)(2,1)} custom-call(bf16[480,128]{1,0:T(8,128)(2,1)} %pad_maximum_fusion.send_ref), custom_call_target="tpu_custom_call" | custom-call | tf_op jit(solution)/shard_map/pallas_call | solution.py:293
  94.7 0.0 slice-start
  94.7 0.0 copy-start
  94.7 0.0 slice-start.1
  94.7 1.1 slice-done
  95.8 0.7 bitcast_select_fusion
  96.5 0.5 copy-done
  97.0 0.4 slice-done.1
  97.4 0.0 copy-start.1
  97.4 1.6 %fusion.5 = f32[384,256]{0,1:T(8,128)S(1)} fusion(bf16[384,5120]{1,0:T(8,128)(2,1)S(1)} %copy-done, bf16[5120,128]{1,0:T(8,128)(2,1)S(1)} %bitcast_select_fusion, bf16[5120,128]{1,0:T(8,128)(2,1)S(1)} %bitcast.18), kind=kOutput, calls=%fused_computation.7 | convolution fusion | flops 1011875840 | bytes 6946816 | tf_op jit(solution)/shard_map/dot_general | solution.py:342
  99.0 3.1 %collective-permute-start.1 = (f32[384,128]{0,1:T(8,128)S(1)}, f32[384,128]{0,1:T(8,128)S(1)}, u32[]{:S(2)}, u32[]{:S(2)}) collective-permute-start(f32[384,128]{0,1:T(8,128)S(1)} %slice.18), channel_id=1, source_target_pairs={{0,1},{1,0},{2,3},{3,2},{4,5},{5,4},{6,7},{7,6},{8,9},{9,8},{10,11... | collective-permute-start | bytes 589832 | tf_op jit(solution)/shard_map/ppermute | solution.py:346
  102.1 0.0 copy-done.1
  102.1 0.2 reduce-window.8
  102.3 0.9 collective-permute-done.1
  103.2 2.4 %collective-permute-start.2 = (bf16[384,128]{0,1:T(8,128)(2,1)S(1)}, bf16[384,128]{0,1:T(8,128)(2,1)S(1)}, u32[]{:S(2)}, u32[]{:S(2)}) collective-permute-start(bf16[384,128]{0,1:T(8,128)(2,1)S(1)} %add_convert_fusion), channel_id=1, source_target_pairs={{0,2},{1,3},{2,0},{3,1},{4,6},{5,7},{6,4},{7,5},{8,10},{9,11},{10,... | collective-permute-start | bytes 294920 | tf_op jit(solution)/shard_map/ppermute | solution.py:348
  105.6 0.1 convert_reduce_fusion
  105.7 3.4 %collective-permute-done.2 = bf16[384,128]{0,1:T(8,128)(2,1)S(1)} collective-permute-done((bf16[384,128]{0,1:T(8,128)(2,1)S(1)}, bf16[384,128]{0,1:T(8,128)(2,1)S(1)}, u32[]{:S(2)}, u32[]{:S(2)}) %collective-permute-start.2) | collective-permute-done | bytes 98336 | tf_op jit(solution)/shard_map/ppermute | solution.py:348
  109.1 0.3 fusion.17
  109.4 0.1 fusion.9
  109.5 0.3 fusion.10
  109.8 0.7 reshape.51.send_ref
  110.5 34.3 %shard_map.48 = f32[12,4096]{1,0:T(8,128)} custom-call(f32[32,12,128]{2,1,0:T(8,128)} %reshape.51.send_ref), custom_call_target="tpu_custom_call" | custom-call | tf_op jit(solution)/shard_map/pallas_call | solution.py:293
  144.9 1.7 %copy.6 = f32[12,4096]{1,0:T(8,128)} copy(f32[12,4096]{1,0:T(8,128)} %shard_map.48) | data formatting | bytes 393216
  (4 shorter events, 0.1 us)
Async XLA Ops:
  52.6 4.6 %collective-permute-start = (bf16[160,128]{1,0:T(8,128)(2,1)S(1)}, bf16[160,128]{1,0:T(8,128)(2,1)S(1)}, u32[]{:S(2)}, u32[]{:S(2)}) collective-permute-start(bf16[160,128]{1,0:T(8,128)(2,1)S(1)} %get-tuple-element.7), channel_id=1, source_target_pairs={{0,1},{1,0},{2,3},{3,2},{4,5},{5,4},{6,7},{7,6},{8,9},{9,8},{10,11... | collective-permute-start | bytes 122888 | tf_op jit(solution)/shard_map/ppermute | solution.py:328
  94.7 1.1 slice-start
  94.7 2.3 %copy-start = (bf16[384,5120]{1,0:T(8,128)(2,1)S(1)}, bf16[384,5120]{1,0:T(8,128)(2,1)}, u32[]{:S(2)}) copy-start(bf16[384,5120]{1,0:T(8,128)(2,1)} %param.4) | copy-start | bytes 11796484
  94.7 2.7 %slice-start.1 = ((bf16[16,480,128]{2,1,0:T(8,128)(2,1)}), bf16[16,320,128]{2,1,0:T(8,128)(2,1)S(1)}, s32[]{:S(2)}) async-start(bf16[16,480,128]{2,1,0:T(8,128)(2,1)} %shard_map.47), calls=%async_computation.1 | async-start | bytes 2621440 | tf_op jit(solution)/shard_map/slice | solution.py:334
  97.4 4.7 %copy-start.1 = (s32[1,4]{1,0:T(1,128)S(1)}, s32[1,4]{1,0:T(1,128)}, u32[]{:S(2)}) copy-start(s32[1,4]{1,0:T(1,128)} %param.7) | copy-start | bytes 52
  99.0 4.1 %collective-permute-start.1 = (f32[384,128]{0,1:T(8,128)S(1)}, f32[384,128]{0,1:T(8,128)S(1)}, u32[]{:S(2)}, u32[]{:S(2)}) collective-permute-start(f32[384,128]{0,1:T(8,128)S(1)} %slice.18), channel_id=1, source_target_pairs={{0,1},{1,0},{2,3},{3,2},{4,5},{5,4},{6,7},{7,6},{8,9},{9,8},{10,11... | collective-permute-start | bytes 589832 | tf_op jit(solution)/shard_map/ppermute | solution.py:346
  103.2 5.9 %collective-permute-start.2 = (bf16[384,128]{0,1:T(8,128)(2,1)S(1)}, bf16[384,128]{0,1:T(8,128)(2,1)S(1)}, u32[]{:S(2)}, u32[]{:S(2)}) collective-permute-start(bf16[384,128]{0,1:T(8,128)(2,1)S(1)} %add_convert_fusion), channel_id=1, source_target_pairs={{0,2},{1,3},{2,0},{3,1},{4,6},{5,7},{6,4},{7,5},{8,10},{9,11},{10,... | collective-permute-start | bytes 294920 | tf_op jit(solution)/shard_map/ppermute | solution.py:348

commit v9 on v7

--- a/solution.py
+++ b/solution.py
@@ -163,6 +163,49 @@
     )(panels)
 
 
+def kv_share_kernel(part_ref, out_ref, partner_part, mine, theirs, send_sems, recv_sems):
+    me = lax.axis_index("tp")
+    partner = me + 1 - 2 * (me % 2)
+    across = me + 2 - 4 * ((me // 2) % 2)
+    barrier = pltpu.get_barrier_semaphore()
+    for neighbour in (partner, across):
+        pl.semaphore_signal(barrier, inc=1, device_id={"tp": neighbour}, device_id_type=MESH)
+    pl.semaphore_wait(barrier, 2)
+    first = pltpu.make_async_remote_copy(
+        src_ref=part_ref, dst_ref=partner_part, send_sem=send_sems.at[0], recv_sem=recv_sems.at[0],
+        device_id={"tp": partner}, device_id_type=MESH,
+    )
+    first.start()
+    first.wait()
+    mine[...] = (part_ref[...] + partner_part[...]).astype(mine.dtype)
+    second = pltpu.make_async_remote_copy(
+        src_ref=mine, dst_ref=theirs, send_sem=send_sems.at[1], recv_sem=recv_sems.at[1],
+        device_id={"tp": across}, device_id_type=MESH,
+    )
+    second.start()
+    second.wait()
+    holds_k = (me % 4) < 2
+    out_ref[0] = jnp.where(holds_k, mine[...], theirs[...])
+    out_ref[1] = jnp.where(holds_k, theirs[...], mine[...])
+
+
+def kv_share(part, collective_id):
+    return pl.pallas_call(
+        kv_share_kernel,
+        out_shape=jax.ShapeDtypeStruct((2,) + part.shape, jnp.bfloat16),
+        in_specs=[pl.BlockSpec(memory_space=pltpu.VMEM)],
+        out_specs=pl.BlockSpec(memory_space=pltpu.VMEM),
+        scratch_shapes=[
+            pltpu.VMEM(part.shape, part.dtype),
+            pltpu.VMEM(part.shape, jnp.bfloat16),
+            pltpu.VMEM(part.shape, jnp.bfloat16),
+            pltpu.SemaphoreType.DMA((2,)),
+            pltpu.SemaphoreType.DMA((2,)),
+        ],
+        compiler_params=pltpu.CompilerParams(collective_id=collective_id, has_side_effects=True),
+    )(part)
+
+
 def grid_kernel(width, send_ref, out_ref, landed, send_sems, recv_sems):
     me = lax.axis_index("grp")
     core = lax.axis_index("tp") % 2
@@ -339,13 +382,7 @@
     projected = jnp.dot(tokens, both_weights, preferred_element_type=jnp.float32)
     query_rows = projected[:, :head_dim].astype(jnp.bfloat16)
     kv_part = projected[:, head_dim:]
-    pair_perm = [(i, i ^ 1) for i in range(tp_count)]
-    kv_full = (kv_part + lax.ppermute(kv_part, "tp", pair_perm)).astype(jnp.bfloat16)
-    swap_perm = [(i, i ^ 2) for i in range(tp_count)]
-    kv_other = lax.ppermute(kv_full, "tp", swap_perm)
-    holds_k = quarter < 2
-    key_rows = jnp.where(holds_k, kv_full, kv_other)
-    value_rows = jnp.where(holds_k, kv_other, kv_full)
+    key_rows, value_rows = kv_share(kv_part, 3)
 
     position = jnp.arange(seq_total, dtype=jnp.int32)
     bounds = jnp.cumsum(lengths[0])

time: 133 us -> 134 us (level)
  Pallas kernels: 102 us -> 111 us
  starting transfers between devices: 9.24 us -> 3.74 us
  waiting for transfers between devices: 4.89 us -> 0.37 us
    pallas_call x0 -> x1, Pallas kernels: none -> 9.25 us  [kv_share(): pl.pallas_call(kv_share_kernel, out_shape=jax.ShapeDtypeStruct((2,) + par...]
    ppermute x2 -> x0, starting transfers between devices: 5.49 us -> none  [the longest x1 3.09 us: on_device(): lax.ppermute(kv_part, 'tp', pair_perm)]
    ppermute x2 -> x0, waiting for transfers between devices: 4.26 us -> none  [the longest x1 3.4 us: on_device(): kv_other = lax.ppermute(kv_full, 'tp', swap_perm)]
  transfers between devices with their start and end apart: 3 -> 1, of which waited for: 3 -> 1; matrix products, arithmetic and copies ran while one was open for 0% -> 0% of each run, Pallas kernels for 0% -> 0%
where the time goes in v9:
time: 134 us; the launch traced here: 133 us
  Pallas kernels  111 us (83%)
  local copies, waits for them, and re-layouts  7.63 us (6%)
  between operations  5.85 us (4%)
  starting transfers between devices  3.74 us (3%)
  matrix products  2.73 us (2%)
  other arithmetic  2.15 us (2%)
    pallas_call x2, Pallas kernels, exchange(): pl.pallas_call(functools.partial(exchange_kernel, axis, count, scatter),...  56.9 us
    pallas_call x1, Pallas kernels, chip_ring_gather(): pl.pallas_call(functools.partial(chip_ring_kernel, count), out_shape=jax....  44.8 us
    pallas_call x1, Pallas kernels, kv_share(): pl.pallas_call(kv_share_kernel, out_shape=jax.ShapeDtypeStruct((2,) + par...  9.25 us
    ppermute x1, starting transfers between devices, on_device(): lax.ppermute(all_halves[panel_home[partner_id]], 'tp', partner_perm)  3.74 us
  transfers between devices with their start and end apart: 1, of which 1 were waited for; matrix products, arithmetic and copies ran while one was open for 0% of the time, Pallas kernels for 0%

profile of v9, /device:TPU:1, one launch (start us, length us, event | category | flops | bytes accessed | tf_op | source)
XLA Modules:
  0.0 133.4 jit_solution(18366666039585361177)
XLA Ops:
  0.0 0.0 copy-start.2
  0.0 1.4 %fusion.17 = (s32[1]{0:T(128)}, s32[1]{0:T(128)}, s32[1]{0:T(128)}) fusion(s32[48]{0:T(128)} %param.6, s32[]{:T(128)S(6)} %select_n.55, s32[]{:T(128)S(6)} %select_n.63, s32[]{:T(128)S(6)} %select_n.57), kind=kLoop, calls=%fused_computation.29 | loop fusion | bytes 36 | tf_op jit(solution)/shard_map/dynamic_slice | solution.py:367
  5.2 44.8 %shard_map.46 = bf16[16,4,160,128]{3,2,1,0:T(8,128)(2,1)} custom-call(bf16[2,320,128]{2,1,0:T(8,128)(2,1)} %panels_ref.1), custom_call_target="tpu_custom_call" | custom-call | tf_op jit(solution)/shard_map/pallas_call | solution.py:152
  51.9 0.8 dynamic-slice_bitcast_fusion.2
  52.7 3.7 %collective-permute-start = (bf16[160,128]{1,0:T(8,128)(2,1)S(1)}, bf16[160,128]{1,0:T(8,128)(2,1)S(1)}, u32[]{:S(2)}, u32[]{:S(2)}) collective-permute-start(bf16[160,128]{1,0:T(8,128)(2,1)S(1)} %get-tuple-element.7), channel_id=1, source_target_pairs={{0,1},{1,0},{2,3},{3,2},{4,5},{5,4},{6,7},{7,6},{8,9},{9,8},{10,11... | collective-permute-start | bytes 122888 | tf_op jit(solution)/shard_map/ppermute | solution.py:368
  56.5 0.0 copy-done.2
  56.5 0.2 reduce-window.8
  56.7 0.1 convert_reduce_fusion
  56.8 0.1 broadcast_in_dim.44
  56.9 0.1 broadcast_in_dim.45
  57.0 0.4 collective-permute-done
  57.4 0.7 pad_maximum_fusion.send_ref
  58.0 36.8 %shard_map.47 = bf16[16,480,128]{2,1,0:T(8,128)(2,1)} custom-call(bf16[480,128]{1,0:T(8,128)(2,1)} %pad_maximum_fusion.send_ref), custom_call_target="tpu_custom_call" | custom-call | tf_op jit(solution)/shard_map/pallas_call | solution.py:333
  94.9 0.0 slice-start
  94.9 0.0 copy-start.1
  94.9 0.0 slice-start.1
  94.9 1.1 slice-done
  95.9 0.7 bitcast_select_fusion
  96.7 0.5 copy-done.1
  97.2 0.4 slice-done.1
  97.6 1.2 fusion.5
  98.8 0.7 slice.18.part_ref
  99.4 9.3 %shard_map.48 = bf16[2,384,128]{2,1,0:T(8,128)(2,1)} custom-call(f32[384,128]{1,0:T(8,128)} %slice.18.part_ref), custom_call_target="tpu_custom_call" | custom-call | tf_op jit(solution)/shard_map/pallas_call | solution.py:193
  108.7 0.0 copy-start
  108.7 1.3 fusion.18
  110.0 0.3 fusion.9
  110.3 0.2 divide_convert_fusion
  110.5 0.1 dot_general.16
  110.6 0.0 copy-done
  110.6 0.2 fusion.10
  110.8 0.8 copy.13.send_ref
  111.6 20.0 %shard_map.49 = f32[12,4096]{1,0:T(8,128)} custom-call(f32[32,12,128]{2,1,0:T(8,128)} %copy.13.send_ref), custom_call_target="tpu_custom_call" | custom-call | tf_op jit(solution)/shard_map/pallas_call | solution.py:333
  131.7 1.7 %copy.18 = f32[12,4096]{1,0:T(8,128)} copy(f32[12,4096]{1,0:T(8,128)} %shard_map.49) | data formatting | bytes 393216
  (2 shorter events, 0.0 us)
Async XLA Ops:
  0.0 56.5 %copy-start.2 = (s32[1,4]{1,0:T(1,128)S(1)}, s32[1,4]{1,0:T(1,128)}, u32[]{:S(2)}) copy-start(s32[1,4]{1,0:T(1,128)} %param.7) | copy-start | bytes 52
  52.7 4.6 %collective-permute-start = (bf16[160,128]{1,0:T(8,128)(2,1)S(1)}, bf16[160,128]{1,0:T(8,128)(2,1)S(1)}, u32[]{:S(2)}, u32[]{:S(2)}) collective-permute-start(bf16[160,128]{1,0:T(8,128)(2,1)S(1)} %get-tuple-element.7), channel_id=1, source_target_pairs={{0,1},{1,0},{2,3},{3,2},{4,5},{5,4},{6,7},{7,6},{8,9},{9,8},{10,11... | collective-permute-start | bytes 122888 | tf_op jit(solution)/shard_map/ppermute | solution.py:368
  94.9 1.1 slice-start
  94.9 2.3 %copy-start.1 = (bf16[384,5120]{1,0:T(8,128)(2,1)S(1)}, bf16[384,5120]{1,0:T(8,128)(2,1)}, u32[]{:S(2)}) copy-start(bf16[384,5120]{1,0:T(8,128)(2,1)} %param.4) | copy-start | bytes 11796484
  94.9 2.7 %slice-start.1 = ((bf16[16,480,128]{2,1,0:T(8,128)(2,1)}), bf16[16,320,128]{2,1,0:T(8,128)(2,1)S(1)}, s32[]{:S(2)}) async-start(bf16[16,480,128]{2,1,0:T(8,128)(2,1)} %shard_map.47), calls=%async_computation.1 | async-start | bytes 2621440 | tf_op jit(solution)/shard_map/slice | solution.py:374
  108.7 1.9 %copy-start = (bf16[2,384,128]{2,1,0:T(8,128)(2,1)S(1)}, bf16[2,384,128]{2,1,0:T(8,128)(2,1)}, u32[]{:S(2)}) copy-start(bf16[2,384,128]{2,1,0:T(8,128)(2,1)} %shard_map.48) | copy-start | bytes 589828

commit v10 on v9

--- a/solution.py
+++ b/solution.py
@@ -295,6 +295,48 @@
     return gathered.reshape((count, x.shape[0] * x.shape[1]) + x.shape[2:])
 
 
+def gather_hbm_kernel(axis, count, send_ref, out_ref, send_sems, recv_sems, local_sem):
+    me = lax.axis_index(axis)
+    barrier = pltpu.get_barrier_semaphore()
+    for step in range(1, count):
+        peer = lax.rem(me + step, count)
+        pl.semaphore_signal(barrier, inc=1, device_id={axis: peer}, device_id_type=MESH)
+    pl.semaphore_wait(barrier, count - 1)
+    copies = []
+    for step in range(1, count):
+        peer = lax.rem(me + step, count)
+        copy = pltpu.make_async_remote_copy(
+            src_ref=send_ref,
+            dst_ref=out_ref.at[me],
+            send_sem=send_sems.at[step],
+            recv_sem=recv_sems.at[step],
+            device_id={axis: peer},
+            device_id_type=MESH,
+        )
+        copy.start()
+        copies.append(copy)
+    local = pltpu.make_async_copy(send_ref, out_ref.at[me], local_sem)
+    local.start()
+    for copy in copies:
+        copy.wait()
+    local.wait()
+
+
+def gather_hbm(x, axis, count, collective_id):
+    return pl.pallas_call(
+        functools.partial(gather_hbm_kernel, axis, count),
+        out_shape=jax.ShapeDtypeStruct((count,) + x.shape, x.dtype),
+        in_specs=[pl.BlockSpec(memory_space=pltpu.VMEM)],
+        out_specs=pl.BlockSpec(memory_space=pl.ANY),
+        scratch_shapes=[
+            pltpu.SemaphoreType.DMA((count,)),
+            pltpu.SemaphoreType.DMA((count,)),
+            pltpu.SemaphoreType.DMA(()),
+        ],
+        compiler_params=pltpu.CompilerParams(collective_id=collective_id, has_side_effects=True),
+    )(x)
+
+
 def exchange_kernel(axis, count, scatter, send_ref, out_ref, landed, send_sems, recv_sems):
     me = lax.axis_index(axis)
     barrier = pltpu.get_barrier_semaphore()
@@ -370,7 +412,7 @@
                         jnp.concatenate([q_theirs, q_mine], axis=0))
     kv_half = all_halves[panel_home[kv_panel]]
     piece = jnp.concatenate([q_block, kv_half], axis=0)
-    gathered = exchange(piece, "grp", grp_count, False, 0)
+    gathered = gather_hbm(piece, "grp", grp_count, 0)
     q_weights = gathered[:, :block_rows].reshape(grp_count * block_rows, head_dim)
     kv_weights = gathered[:, block_rows:]
 

time: 134 us -> 133 us (level)
    pallas_call x2 -> x1, Pallas kernels: 56.9 us -> 20 us  [exchange(): pl.pallas_call(functools.partial(exchange_kernel, axis, count, scatter),...]
    pallas_call x0 -> x1, Pallas kernels: none -> 35.5 us  [gather_hbm(): pl.pallas_call(functools.partial(gather_hbm_kernel, axis, count), out_sha...]
where the time goes in v10:
time: 133 us; the launch traced here: 132 us
  Pallas kernels  110 us (83%)
  local copies, waits for them, and re-layouts  7.63 us (6%)
  between operations  5.85 us (4%)
  starting transfers between devices  3.74 us (3%)
  matrix products  2.73 us (2%)
  other arithmetic  2.15 us (2%)
    pallas_call x1, Pallas kernels, chip_ring_gather(): pl.pallas_call(functools.partial(chip_ring_kernel, count), out_shape=jax....  44.8 us
    pallas_call x1, Pallas kernels, gather_hbm(): pl.pallas_call(functools.partial(gather_hbm_kernel, axis, count), out_sha...  35.5 us
    pallas_call x1, Pallas kernels, exchange(): pl.pallas_call(functools.partial(exchange_kernel, axis, count, scatter),...  20 us
    pallas_call x1, Pallas kernels, kv_share(): pl.pallas_call(kv_share_kernel, out_shape=jax.ShapeDtypeStruct((2,) + par...  9.25 us
    ppermute x1, starting transfers between devices, on_device(): lax.ppermute(all_halves[panel_home[partner_id]], 'tp', partner_perm)  3.74 us
  transfers between devices with their start and end apart: 1, of which 1 were waited for; matrix products, arithmetic and copies ran while one was open for 0% of the time, Pallas kernels for 0%

profile of v10, /device:TPU:1, one launch (start us, length us, event | category | flops | bytes accessed | tf_op | source)
XLA Modules:
  0.0 132.1 jit_solution(5499933120919989584)
XLA Ops:
  0.0 0.0 copy-start.2
  0.0 1.4 %fusion.17 = (s32[1]{0:T(128)}, s32[1]{0:T(128)}, s32[1]{0:T(128)}) fusion(s32[48]{0:T(128)} %param.6, s32[]{:T(128)S(6)} %select_n.55, s32[]{:T(128)S(6)} %select_n.63, s32[]{:T(128)S(6)} %select_n.57), kind=kLoop, calls=%fused_computation.29 | loop fusion | bytes 36 | tf_op jit(solution)/shard_map/dynamic_slice | solution.py:409
  5.2 44.8 %shard_map.46 = bf16[16,4,160,128]{3,2,1,0:T(8,128)(2,1)} custom-call(bf16[2,320,128]{2,1,0:T(8,128)(2,1)} %panels_ref.1), custom_call_target="tpu_custom_call" | custom-call | tf_op jit(solution)/shard_map/pallas_call | solution.py:152
  51.9 0.8 dynamic-slice_bitcast_fusion.2
  52.7 3.7 %collective-permute-start = (bf16[160,128]{1,0:T(8,128)(2,1)S(1)}, bf16[160,128]{1,0:T(8,128)(2,1)S(1)}, u32[]{:S(2)}, u32[]{:S(2)}) collective-permute-start(bf16[160,128]{1,0:T(8,128)(2,1)S(1)} %get-tuple-element.7), channel_id=1, source_target_pairs={{0,1},{1,0},{2,3},{3,2},{4,5},{5,4},{6,7},{7,6},{8,9},{9,8},{10,11... | collective-permute-start | bytes 122888 | tf_op jit(solution)/shard_map/ppermute | solution.py:410
  56.5 0.0 copy-done.2
  56.5 0.2 reduce-window.8
  56.7 0.1 convert_reduce_fusion
  56.8 0.1 broadcast_in_dim.44
  56.9 0.1 broadcast_in_dim.45
  57.0 0.4 collective-permute-done
  57.4 0.7 pad_maximum_fusion.send_ref
  58.0 35.5 %shard_map.47 = bf16[16,480,128]{2,1,0:T(8,128)(2,1)} custom-call(bf16[480,128]{1,0:T(8,128)(2,1)} %pad_maximum_fusion.send_ref), custom_call_target="tpu_custom_call" | custom-call | tf_op jit(solution)/shard_map/pallas_call | solution.py:326
  93.6 0.0 slice-start
  93.6 0.0 copy-start.1
  93.6 0.0 slice-start.1
  93.6 1.1 slice-done
  94.7 0.7 bitcast_select_fusion
  95.4 0.5 copy-done.1
  95.9 0.4 slice-done.1
  96.3 1.2 fusion.5
  97.5 0.7 slice.18.part_ref
  98.2 9.3 %shard_map.48 = bf16[2,384,128]{2,1,0:T(8,128)(2,1)} custom-call(f32[384,128]{1,0:T(8,128)} %slice.18.part_ref), custom_call_target="tpu_custom_call" | custom-call | tf_op jit(solution)/shard_map/pallas_call | solution.py:193
  107.4 0.0 copy-start
  107.4 1.3 fusion.18
  108.7 0.3 fusion.9
  109.0 0.2 divide_convert_fusion
  109.2 0.1 dot_general.16
  109.3 0.0 copy-done
  109.3 0.2 fusion.10
  109.5 0.8 copy.13.send_ref
  110.4 20.0 %shard_map.49 = f32[12,4096]{1,0:T(8,128)} custom-call(f32[32,12,128]{2,1,0:T(8,128)} %copy.13.send_ref), custom_call_target="tpu_custom_call" | custom-call | tf_op jit(solution)/shard_map/pallas_call | solution.py:375
  130.4 1.7 %copy.18 = f32[12,4096]{1,0:T(8,128)} copy(f32[12,4096]{1,0:T(8,128)} %shard_map.49) | data formatting | bytes 393216
  (2 shorter events, 0.0 us)
Async XLA Ops:
  0.0 56.5 %copy-start.2 = (s32[1,4]{1,0:T(1,128)S(1)}, s32[1,4]{1,0:T(1,128)}, u32[]{:S(2)}) copy-start(s32[1,4]{1,0:T(1,128)} %param.7) | copy-start | bytes 52
  52.7 4.6 %collective-permute-start = (bf16[160,128]{1,0:T(8,128)(2,1)S(1)}, bf16[160,128]{1,0:T(8,128)(2,1)S(1)}, u32[]{:S(2)}, u32[]{:S(2)}) collective-permute-start(bf16[160,128]{1,0:T(8,128)(2,1)S(1)} %get-tuple-element.7), channel_id=1, source_target_pairs={{0,1},{1,0},{2,3},{3,2},{4,5},{5,4},{6,7},{7,6},{8,9},{9,8},{10,11... | collective-permute-start | bytes 122888 | tf_op jit(solution)/shard_map/ppermute | solution.py:410
  93.6 1.1 slice-start
  93.6 2.3 %copy-start.1 = (bf16[384,5120]{1,0:T(8,128)(2,1)S(1)}, bf16[384,5120]{1,0:T(8,128)(2,1)}, u32[]{:S(2)}) copy-start(bf16[384,5120]{1,0:T(8,128)(2,1)} %param.4) | copy-start | bytes 11796484
  93.6 2.7 %slice-start.1 = ((bf16[16,480,128]{2,1,0:T(8,128)(2,1)}), bf16[16,320,128]{2,1,0:T(8,128)(2,1)S(1)}, s32[]{:S(2)}) async-start(bf16[16,480,128]{2,1,0:T(8,128)(2,1)} %shard_map.47), calls=%async_computation.1 | async-start | bytes 2621440 | tf_op jit(solution)/shard_map/slice | solution.py:416
  107.4 1.9 %copy-start = (bf16[2,384,128]{2,1,0:T(8,128)(2,1)S(1)}, bf16[2,384,128]{2,1,0:T(8,128)(2,1)}, u32[]{:S(2)}) copy-start(bf16[2,384,128]{2,1,0:T(8,128)(2,1)} %shard_map.48) | copy-start | bytes 589828

commit v11 on v10

--- a/solution.py
+++ b/solution.py
@@ -206,6 +206,92 @@
     )(part)
 
 
+def tail_kernel(count, scale, part_ref, q_ref, segq_ref, segk_ref, out_ref,
+                partner_part, mine, theirs, staged, landed, send_sems, recv_sems):
+    me = lax.axis_index("tp")
+    partner = me + 1 - 2 * (me % 2)
+    across = me + 2 - 4 * ((me // 2) % 2)
+    barrier = pltpu.get_barrier_semaphore()
+    for step in range(1, count):
+        peer = lax.rem(me + step, count)
+        pl.semaphore_signal(barrier, inc=1, device_id={"tp": peer}, device_id_type=MESH)
+    pl.semaphore_wait(barrier, count - 1)
+    first = pltpu.make_async_remote_copy(
+        src_ref=part_ref, dst_ref=partner_part, send_sem=send_sems.at[0], recv_sem=recv_sems.at[0],
+        device_id={"tp": partner}, device_id_type=MESH,
+    )
+    first.start()
+    first.wait()
+    mine[...] = (part_ref[...] + partner_part[...]).astype(mine.dtype)
+    second = pltpu.make_async_remote_copy(
+        src_ref=mine, dst_ref=theirs, send_sem=send_sems.at[1], recv_sem=recv_sems.at[1],
+        device_id={"tp": across}, device_id_type=MESH,
+    )
+    second.start()
+    second.wait()
+    holds_k = (me % 4) < 2
+    keys = jnp.where(holds_k, mine[...], theirs[...])
+    values = jnp.where(holds_k, theirs[...], mine[...])
+
+    scores = lax.dot_general(
+        q_ref[...], keys, (((1,), (1,)), ((), ())), preferred_element_type=jnp.float32
+    ) * scale
+    seq = scores.shape[0]
+    row = lax.broadcasted_iota(jnp.int32, (seq, seq), 0)
+    col = lax.broadcasted_iota(jnp.int32, (seq, seq), 1)
+    allowed = (segq_ref[...] == segk_ref[...]) & (col <= row)
+    masked = jnp.where(allowed, scores, -jnp.inf)
+    peak = jnp.max(masked, axis=1, keepdims=True)
+    weights = jnp.exp(masked - peak)
+    probs = (weights / jnp.sum(weights, axis=1, keepdims=True)).astype(jnp.bfloat16)
+    context = jnp.dot(probs, values, preferred_element_type=jnp.float32)
+    rows = seq // count
+    for target in range(count):
+        staged[target] = context[target * rows:(target + 1) * rows]
+
+    copies = []
+    for step in range(1, count):
+        peer = lax.rem(me + step, count)
+        copy = pltpu.make_async_remote_copy(
+            src_ref=staged.at[peer],
+            dst_ref=landed.at[me],
+            send_sem=send_sems.at[1 + step],
+            recv_sem=recv_sems.at[1 + step],
+            device_id={"tp": peer},
+            device_id_type=MESH,
+        )
+        copy.start()
+        copies.append(copy)
+    landed[me] = staged[me]
+    for copy in copies:
+        copy.wait()
+    width = landed.shape[-1]
+    for source in range(count):
+        out_ref[:, source * width:(source + 1) * width] = landed[source]
+
+
+def tail(part, query, segment, count, collective_id):
+    seq, width = query.shape
+    rows = seq // count
+    vmem = pl.BlockSpec(memory_space=pltpu.VMEM)
+    return pl.pallas_call(
+        functools.partial(tail_kernel, count, width ** (-0.5)),
+        out_shape=jax.ShapeDtypeStruct((rows, count * width), jnp.float32),
+        in_specs=[vmem] * 4,
+        out_specs=vmem,
+        scratch_shapes=[
+            pltpu.VMEM(part.shape, part.dtype),
+            pltpu.VMEM(part.shape, jnp.bfloat16),
+            pltpu.VMEM(part.shape, jnp.bfloat16),
+            pltpu.VMEM((count, rows, width), jnp.float32),
+            pltpu.VMEM((count, rows, width), jnp.float32),
+            pltpu.SemaphoreType.DMA((count + 1,)),
+            pltpu.SemaphoreType.DMA((count + 1,)),
+        ],
+        compiler_params=pltpu.CompilerParams(collective_id=collective_id, has_side_effects=True),
+    )(part, query, segment[:, None], segment[None, :])
+
+
 def grid_kernel(width, send_ref, out_ref, landed, send_sems, recv_sems):
     me = lax.axis_index("grp")
     core = lax.axis_index("tp") % 2
@@ -424,26 +510,10 @@
     projected = jnp.dot(tokens, both_weights, preferred_element_type=jnp.float32)
     query_rows = projected[:, :head_dim].astype(jnp.bfloat16)
     kv_part = projected[:, head_dim:]
-    key_rows, value_rows = kv_share(kv_part, 3)
-
     position = jnp.arange(seq_total, dtype=jnp.int32)
     bounds = jnp.cumsum(lengths[0])
     segment = jnp.sum((position[:, None] >= bounds[None, :]).astype(jnp.int32), axis=1)
-    allowed = (segment[:, None] == segment[None, :]) & (position[None, :] <= position[:, None])
-    score_scale = head_dim ** (-0.5)
-    scores = (
-        lax.dot_general(
-            query_rows, key_rows, (((1,), (1,)), ((), ())), preferred_element_type=jnp.float32
-        )
-        * score_scale
-    )
-    masked = jnp.where(allowed, scores, -jnp.inf)
-    row_peak = jnp.max(masked, axis=1, keepdims=True)
-    row_exp = jnp.exp(masked - row_peak)
-    attn_probs = (row_exp / jnp.sum(row_exp, axis=1, keepdims=True)).astype(jnp.bfloat16)
-    context = jnp.dot(attn_probs, value_rows, preferred_element_type=jnp.float32)
-    outgoing = context.reshape(tp_count, seq_total // tp_count, head_dim)
-    return exchange(outgoing, "tp", tp_count, True, 1)
+    return tail(kv_part, query_rows, segment, tp_count, 1)
 
 
 def solution(mesh):

time: 133 us -> 131 us (0.985)
  matrix products: 2.73 us -> 1.18 us
    pallas_call x2 -> x1, Pallas kernels: 29.3 us -> 26.9 us  [tail(): pl.pallas_call(functools.partial(tail_kernel, count, width ** (-0.5)), ou...]
    pallas_call x1, Pallas kernels: 35.5 us -> 37.3 us  [gather_hbm(): pl.pallas_call(functools.partial(gather_hbm_kernel, axis, count), out_sha...]
    dot_general x2 -> x0, matrix products: 1.55 us -> none  [the longest x1 1.3 us: on_device(): lax.dot_general(query_rows, key_rows, (((1,), (1,)), ((), ())), preferred...]
    broadcast_in_dim x0 -> x2, local copies, waits for them, and re-layouts: none -> 1.39 us  [the longest x1 0.8 us: tail(): segment[:, None]]
  transfers between devices with their start and end apart: 1 -> 1, of which waited for: 1 -> 0; matrix products, arithmetic and copies ran while one was open for 0% -> 1% of each run, Pallas kernels for 0% -> 0%
where the time goes in v11:
time: 131 us
  Pallas kernels  109 us (83%)
  local copies, waits for them, and re-layouts  8.79 us (7%)
  between operations  6.21 us (5%)
  starting transfers between devices  3.74 us (3%)
  other arithmetic  1.69 us (1%)
    pallas_call x1, Pallas kernels, chip_ring_gather(): pl.pallas_call(functools.partial(chip_ring_kernel, count), out_shape=jax....  44.8 us
    pallas_call x1, Pallas kernels, gather_hbm(): pl.pallas_call(functools.partial(gather_hbm_kernel, axis, count), out_sha...  37.3 us
    pallas_call x1, Pallas kernels, tail(): pl.pallas_call(functools.partial(tail_kernel, count, width ** (-0.5)), ou...  26.9 us
    ppermute x1, starting transfers between devices, on_device(): lax.ppermute(all_halves[panel_home[partner_id]], 'tp', partner_perm)  3.74 us
  transfers between devices with their start and end apart: 1, of which 0 were waited for; matrix products, arithmetic and copies ran while one was open for 1% of the time, Pallas kernels for 0%

profile of v11, /device:TPU:1, one launch (start us, length us, event | category | flops | bytes accessed | tf_op | source)
XLA Modules:
  0.0 130.5 jit_solution(6918766179958231600)
XLA Ops:
  0.0 0.0 copy-start.1
  0.0 1.4 %fusion.8 = (s32[1]{0:T(128)}, s32[1]{0:T(128)}, s32[1]{0:T(128)}) fusion(s32[48]{0:T(128)} %param.6, s32[]{:T(128)S(6)} %select_n.51, s32[]{:T(128)S(6)} %select_n.59, s32[]{:T(128)S(6)} %select_n.53), kind=kLoop, calls=%fused_computation.16 | loop fusion | bytes 36 | tf_op jit(solution)/shard_map/dynamic_slice | solution.py:495
  5.5 44.8 %shard_map.46 = bf16[16,4,160,128]{3,2,1,0:T(8,128)(2,1)} custom-call(bf16[2,320,128]{2,1,0:T(8,128)(2,1)} %panels_ref.1), custom_call_target="tpu_custom_call" | custom-call | tf_op jit(solution)/shard_map/pallas_call | solution.py:152
  52.3 0.8 dynamic-slice_bitcast_fusion.2
  53.1 3.7 %collective-permute-start = (bf16[160,128]{1,0:T(8,128)(2,1)S(1)}, bf16[160,128]{1,0:T(8,128)(2,1)S(1)}, u32[]{:S(2)}, u32[]{:S(2)}) collective-permute-start(bf16[160,128]{1,0:T(8,128)(2,1)S(1)} %get-tuple-element.7), channel_id=1, source_target_pairs={{0,1},{1,0},{2,3},{3,2},{4,5},{5,4},{6,7},{7,6},{8,9},{9,8},{10,11... | collective-permute-start | bytes 122888 | tf_op jit(solution)/shard_map/ppermute | solution.py:496
  56.9 0.0 copy-done.1
  56.9 0.2 reduce-window.8
  57.1 0.1 convert_reduce_fusion
  57.2 0.6 broadcast_in_dim.47.segk_ref
  57.8 0.8 broadcast_in_dim.48.segq_ref
  58.6 0.1 broadcast_in_dim.40
  58.6 0.1 broadcast_in_dim.41
  58.7 0.0 collective-permute-done
  58.8 0.7 pad_maximum_fusion.send_ref
  59.4 37.3 %shard_map.47 = bf16[16,480,128]{2,1,0:T(8,128)(2,1)} custom-call(bf16[480,128]{1,0:T(8,128)(2,1)} %pad_maximum_fusion.send_ref), custom_call_target="tpu_custom_call" | custom-call | tf_op jit(solution)/shard_map/pallas_call | solution.py:412
  96.7 0.0 slice-start
  96.7 0.0 copy-start
  96.8 0.0 slice-start.1
  96.8 1.1 slice-done
  97.8 0.7 bitcast_select_fusion
  98.6 0.5 copy-done
  99.1 0.4 slice-done.1
  99.4 1.2 fusion.4
  100.6 0.7 slice.20.q_ref
  101.3 0.7 slice.17.part_ref
  102.0 26.9 %shard_map.48 = f32[12,4096]{1,0:T(8,128)} custom-call(f32[384,128]{1,0:T(8,128)} %slice.17.part_ref, bf16[384,128]{1,0:T(8,128)(2,1)} %slice.20.q_ref, s32[384,1]{1,0:T(8,128)} %broadcast_in_dim.48.segq_ref, s32[1,384]{1,0:T(1,128)} %broadcast_in_dim.47.segk_ref), custom_call_target="tpu_custom_call" | custom-call | tf_op jit(solution)/shard_map/pallas_call | solution.py:277
  128.8 1.7 %copy.12 = f32[12,4096]{1,0:T(8,128)} copy(f32[12,4096]{1,0:T(8,128)} %shard_map.48) | data formatting | bytes 393216
  (2 shorter events, 0.0 us)
Async XLA Ops:
  0.0 56.9 %copy-start.1 = (s32[1,4]{1,0:T(1,128)S(1)}, s32[1,4]{1,0:T(1,128)}, u32[]{:S(2)}) copy-start(s32[1,4]{1,0:T(1,128)} %param.7) | copy-start | bytes 52
  53.1 5.6 %collective-permute-start = (bf16[160,128]{1,0:T(8,128)(2,1)S(1)}, bf16[160,128]{1,0:T(8,128)(2,1)S(1)}, u32[]{:S(2)}, u32[]{:S(2)}) collective-permute-start(bf16[160,128]{1,0:T(8,128)(2,1)S(1)} %get-tuple-element.7), channel_id=1, source_target_pairs={{0,1},{1,0},{2,3},{3,2},{4,5},{5,4},{6,7},{7,6},{8,9},{9,8},{10,11... | collective-permute-start | bytes 122888 | tf_op jit(solution)/shard_map/ppermute | solution.py:496
  96.7 1.1 slice-start
  96.7 2.3 %copy-start = (bf16[384,5120]{1,0:T(8,128)(2,1)S(1)}, bf16[384,5120]{1,0:T(8,128)(2,1)}, u32[]{:S(2)}) copy-start(bf16[384,5120]{1,0:T(8,128)(2,1)} %param.4) | copy-start | bytes 11796484
  96.8 2.7 %slice-start.1 = ((bf16[16,480,128]{2,1,0:T(8,128)(2,1)}), bf16[16,320,128]{2,1,0:T(8,128)(2,1)S(1)}, s32[]{:S(2)}) async-start(bf16[16,480,128]{2,1,0:T(8,128)(2,1)} %shard_map.47), calls=%async_computation.1 | async-start | bytes 2621440 | tf_op jit(solution)/shard_map/slice | solution.py:502

commit v12 on v11

--- a/solution.py
+++ b/solution.py
@@ -206,8 +206,10 @@
     )(part)
 
 
-def tail_kernel(count, scale, part_ref, q_ref, segq_ref, segk_ref, out_ref,
-                partner_part, mine, theirs, staged, landed, send_sems, recv_sems):
+def tail_kernel(count, scale, projected_ref, segq_ref, segk_ref, out_ref,
+                part_ref, partner_part, mine, theirs, staged, landed, send_sems, recv_sems):
+    width = landed.shape[-1]
+    part_ref[...] = projected_ref[:, width:]
     me = lax.axis_index("tp")
     partner = me + 1 - 2 * (me % 2)
     across = me + 2 - 4 * ((me // 2) % 2)
@@ -234,7 +236,7 @@
     values = jnp.where(holds_k, theirs[...], mine[...])
 
     scores = lax.dot_general(
-        q_ref[...], keys, (((1,), (1,)), ((), ())), preferred_element_type=jnp.float32
+        projected_ref[:, :width].astype(jnp.bfloat16), keys, (((1,), (1,)), ((), ())), preferred_element_type=jnp.float32
     ) * scale
     seq = scores.shape[0]
     row = lax.broadcasted_iota(jnp.int32, (seq, seq), 0)
@@ -265,21 +267,22 @@
     landed[me] = staged[me]
     for copy in copies:
         copy.wait()
-    width = landed.shape[-1]
     for source in range(count):
         out_ref[:, source * width:(source + 1) * width] = landed[source]
 
 
-def tail(part, query, segment, count, collective_id):
-    seq, width = query.shape
+def tail(projected, segment, count, collective_id):
+    seq, width = projected.shape[0], projected.shape[1] // 2
+    part = jax.ShapeDtypeStruct((seq, width), jnp.float32)
     rows = seq // count
     vmem = pl.BlockSpec(memory_space=pltpu.VMEM)
     return pl.pallas_call(
         functools.partial(tail_kernel, count, width ** (-0.5)),
         out_shape=jax.ShapeDtypeStruct((rows, count * width), jnp.float32),
-        in_specs=[vmem] * 4,
+        in_specs=[vmem] * 3,
         out_specs=vmem,
         scratch_shapes=[
+            pltpu.VMEM(part.shape, part.dtype),
             pltpu.VMEM(part.shape, part.dtype),
             pltpu.VMEM(part.shape, jnp.bfloat16),
             pltpu.VMEM(part.shape, jnp.bfloat16),
@@ -289,7 +292,7 @@
             pltpu.SemaphoreType.DMA((count + 1,)),
         ],
         compiler_params=pltpu.CompilerParams(collective_id=collective_id, has_side_effects=True),
-    )(part, query, segment[:, None], segment[None, :])
+    )(projected, segment[:, None], segment[None, :])
 
 
 def grid_kernel(width, send_ref, out_ref, landed, send_sems, recv_sems):
@@ -508,12 +511,10 @@
         [q_weights, kv_rows.reshape(grp_count * block_rows, head_dim)], axis=1
     )
     projected = jnp.dot(tokens, both_weights, preferred_element_type=jnp.float32)
-    query_rows = projected[:, :head_dim].astype(jnp.bfloat16)
-    kv_part = projected[:, head_dim:]
     position = jnp.arange(seq_total, dtype=jnp.int32)
     bounds = jnp.cumsum(lengths[0])
     segment = jnp.sum((position[:, None] >= bounds[None, :]).astype(jnp.int32), axis=1)
-    return tail(kv_part, query_rows, segment, tp_count, 1)
+    return tail(projected, segment, tp_count, 1)
 
 
 def solution(mesh):

time: 131 us -> 131 us (level)
  local copies, waits for them, and re-layouts: 8.79 us -> 7.42 us
    slice x2 -> x0, local copies, waits for them, and re-layouts: 1.34 us -> none  [the longest x1 0.69 us: on_device(): kv_part = projected[:, head_dim:]]
where the time goes in v12:
time: 131 us; the launch traced here: 130 us
  Pallas kernels  109 us (83%)
  local copies, waits for them, and re-layouts  7.42 us (6%)
  between operations  6.2 us (5%)
  starting transfers between devices  3.74 us (3%)
  matrix products  1.94 us (1%)
  other arithmetic  1.68 us (1%)
    pallas_call x1, Pallas kernels, chip_ring_gather(): pl.pallas_call(functools.partial(chip_ring_kernel, count), out_shape=jax....  44.8 us
    pallas_call x1, Pallas kernels, gather_hbm(): pl.pallas_call(functools.partial(gather_hbm_kernel, axis, count), out_sha...  37.3 us
    pallas_call x1, Pallas kernels, tail(): pl.pallas_call(functools.partial(tail_kernel, count, width ** (-0.5)), ou...  27 us
    ppermute x1, starting transfers between devices, on_device(): lax.ppermute(all_halves[panel_home[partner_id]], 'tp', partner_perm)  3.74 us
  transfers between devices with their start and end apart: 1, of which 0 were waited for; matrix products, arithmetic and copies ran while one was open for 1% of the time, Pallas kernels for 0%

profile of v12, /device:TPU:1, one launch (start us, length us, event | category | flops | bytes accessed | tf_op | source)
XLA Modules:
  0.0 130.1 jit_solution(10827433327312929839)
XLA Ops:
  0.0 0.0 copy-start.1
  0.0 1.4 %fusion.8 = (s32[1]{0:T(128)}, s32[1]{0:T(128)}, s32[1]{0:T(128)}) fusion(s32[48]{0:T(128)} %param.6, s32[]{:T(128)S(6)} %select_n.51, s32[]{:T(128)S(6)} %select_n.59, s32[]{:T(128)S(6)} %select_n.53), kind=kLoop, calls=%fused_computation.15 | loop fusion | bytes 36 | tf_op jit(solution)/shard_map/dynamic_slice | solution.py:498
  5.5 44.8 %shard_map.46 = bf16[16,4,160,128]{3,2,1,0:T(8,128)(2,1)} custom-call(bf16[2,320,128]{2,1,0:T(8,128)(2,1)} %panels_ref.1), custom_call_target="tpu_custom_call" | custom-call | tf_op jit(solution)/shard_map/pallas_call | solution.py:152
  52.3 0.8 dynamic-slice_bitcast_fusion.2
  53.1 3.7 %collective-permute-start = (bf16[160,128]{1,0:T(8,128)(2,1)S(1)}, bf16[160,128]{1,0:T(8,128)(2,1)S(1)}, u32[]{:S(2)}, u32[]{:S(2)}) collective-permute-start(bf16[160,128]{1,0:T(8,128)(2,1)S(1)} %get-tuple-element.7), channel_id=1, source_target_pairs={{0,1},{1,0},{2,3},{3,2},{4,5},{5,4},{6,7},{7,6},{8,9},{9,8},{10,11... | collective-permute-start | bytes 122888 | tf_op jit(solution)/shard_map/ppermute | solution.py:499
  56.9 0.0 copy-done.1
  56.9 0.2 reduce-window.8
  57.1 0.1 convert_reduce_fusion
  57.2 0.6 broadcast_in_dim.47.segk_ref
  57.7 0.8 broadcast_in_dim.48.segq_ref
  58.5 0.1 broadcast_in_dim.40
  58.6 0.1 broadcast_in_dim.41
  58.7 0.0 collective-permute-done
  58.8 0.6 pad_maximum_fusion.send_ref
  59.4 37.3 %shard_map.47 = bf16[16,480,128]{2,1,0:T(8,128)(2,1)} custom-call(bf16[480,128]{1,0:T(8,128)(2,1)} %pad_maximum_fusion.send_ref), custom_call_target="tpu_custom_call" | custom-call | tf_op jit(solution)/shard_map/pallas_call | solution.py:415
  96.7 0.0 slice-start
  96.7 0.0 copy-start
  96.7 0.0 slice-start.1
  96.7 1.1 slice-done
  97.8 0.7 bitcast_select_fusion
  98.5 0.5 copy-done
  99.0 0.4 slice-done.1
  99.4 1.9 %fusion.4.projected_ref = f32[384,256]{1,0:T(8,128)} fusion(bf16[384,5120]{1,0:T(8,128)(2,1)S(1)} %copy-done, bf16[5120,128]{1,0:T(8,128)(2,1)S(1)} %bitcast_select_fusion, bf16[5120,128]{1,0:T(8,128)(2,1)S(1)} %bitcast.18), kind=kOutput, calls=%fused_computation.5 | convolution fusion | flops 1011875840 | bytes 6946816 | tf_op jit(solution)/shard_map/dot_general | solution.py:513
  101.3 27.0 %shard_map.48 = f32[12,4096]{1,0:T(8,128)} custom-call(f32[384,256]{1,0:T(8,128)} %fusion.4.projected_ref, s32[384,1]{1,0:T(8,128)} %broadcast_in_dim.48.segq_ref, s32[1,384]{1,0:T(1,128)} %broadcast_in_dim.47.segk_ref), custom_call_target="tpu_custom_call" | custom-call | tf_op jit(solution)/shard_map/pallas_call | solution.py:279
  128.4 1.7 %copy.12 = f32[12,4096]{1,0:T(8,128)} copy(f32[12,4096]{1,0:T(8,128)} %shard_map.48) | data formatting | bytes 393216
  (2 shorter events, 0.0 us)
Async XLA Ops:
  0.0 56.9 %copy-start.1 = (s32[1,4]{1,0:T(1,128)S(1)}, s32[1,4]{1,0:T(1,128)}, u32[]{:S(2)}) copy-start(s32[1,4]{1,0:T(1,128)} %param.7) | copy-start | bytes 52
  53.1 5.6 %collective-permute-start = (bf16[160,128]{1,0:T(8,128)(2,1)S(1)}, bf16[160,128]{1,0:T(8,128)(2,1)S(1)}, u32[]{:S(2)}, u32[]{:S(2)}) collective-permute-start(bf16[160,128]{1,0:T(8,128)(2,1)S(1)} %get-tuple-element.7), channel_id=1, source_target_pairs={{0,1},{1,0},{2,3},{3,2},{4,5},{5,4},{6,7},{7,6},{8,9},{9,8},{10,11... | collective-permute-start | bytes 122888 | tf_op jit(solution)/shard_map/ppermute | solution.py:499
  96.7 1.1 slice-start
  96.7 2.3 %copy-start = (bf16[384,5120]{1,0:T(8,128)(2,1)S(1)}, bf16[384,5120]{1,0:T(8,128)(2,1)}, u32[]{:S(2)}) copy-start(bf16[384,5120]{1,0:T(8,128)(2,1)} %param.4) | copy-start | bytes 11796484
  96.7 2.7 %slice-start.1 = ((bf16[16,480,128]{2,1,0:T(8,128)(2,1)}), bf16[16,320,128]{2,1,0:T(8,128)(2,1)S(1)}, s32[]{:S(2)}) async-start(bf16[16,480,128]{2,1,0:T(8,128)(2,1)} %shard_map.47), calls=%async_computation.1 | async-start | bytes 2621440 | tf_op jit(solution)/shard_map/slice | solution.py:505

commit v13 on v12

--- a/solution.py
+++ b/solution.py
@@ -206,7 +206,7 @@
     )(part)
 
 
-def tail_kernel(count, scale, projected_ref, segq_ref, segk_ref, out_ref,
+def tail_kernel(count, scale, projected_ref, lengths_ref, out_ref,
                 part_ref, partner_part, mine, theirs, staged, landed, send_sems, recv_sems):
     width = landed.shape[-1]
     part_ref[...] = projected_ref[:, width:]
@@ -241,7 +241,14 @@
     seq = scores.shape[0]
     row = lax.broadcasted_iota(jnp.int32, (seq, seq), 0)
     col = lax.broadcasted_iota(jnp.int32, (seq, seq), 1)
-    allowed = (segq_ref[...] == segk_ref[...]) & (col <= row)
+    row_segment = jnp.zeros((seq, seq), jnp.int32)
+    col_segment = jnp.zeros((seq, seq), jnp.int32)
+    bound = lengths_ref[0, 0] * 0
+    for response in range(lengths_ref.shape[1]):
+        bound = bound + lengths_ref[0, response]
+        row_segment = row_segment + (row >= bound).astype(jnp.int32)
+        col_segment = col_segment + (col >= bound).astype(jnp.int32)
+    allowed = (row_segment == col_segment) & (col <= row)
     masked = jnp.where(allowed, scores, -jnp.inf)
     peak = jnp.max(masked, axis=1, keepdims=True)
     weights = jnp.exp(masked - peak)
@@ -271,7 +278,7 @@
         out_ref[:, source * width:(source + 1) * width] = landed[source]
 
 
-def tail(projected, segment, count, collective_id):
+def tail(projected, lengths, count, collective_id):
     seq, width = projected.shape[0], projected.shape[1] // 2
     part = jax.ShapeDtypeStruct((seq, width), jnp.float32)
     rows = seq // count
@@ -279,7 +286,7 @@
     return pl.pallas_call(
         functools.partial(tail_kernel, count, width ** (-0.5)),
         out_shape=jax.ShapeDtypeStruct((rows, count * width), jnp.float32),
-        in_specs=[vmem] * 3,
+        in_specs=[vmem, pl.BlockSpec(memory_space=pltpu.SMEM)],
         out_specs=vmem,
         scratch_shapes=[
             pltpu.VMEM(part.shape, part.dtype),
@@ -292,7 +299,7 @@
             pltpu.SemaphoreType.DMA((count + 1,)),
         ],
         compiler_params=pltpu.CompilerParams(collective_id=collective_id, has_side_effects=True),
-    )(projected, segment[:, None], segment[None, :])
+    )(projected, lengths)
 
 
 def grid_kernel(width, send_ref, out_ref, landed, send_sems, recv_sems):
@@ -511,10 +518,7 @@
         [q_weights, kv_rows.reshape(grp_count * block_rows, head_dim)], axis=1
     )
     projected = jnp.dot(tokens, both_weights, preferred_element_type=jnp.float32)
-    position = jnp.arange(seq_total, dtype=jnp.int32)
-    bounds = jnp.cumsum(lengths[0])
-    segment = jnp.sum((position[:, None] >= bounds[None, :]).astype(jnp.int32), axis=1)
-    return tail(projected, segment, tp_count, 1)
+    return tail(projected, lengths, tp_count, 1)
 
 
 def solution(mesh):

time: 131 us -> 128 us (0.977)
  local copies, waits for them, and re-layouts: 7.42 us -> 6.04 us
    pallas_call x1, Pallas kernels: 37.3 us -> 35.5 us  [gather_hbm(): pl.pallas_call(functools.partial(gather_hbm_kernel, axis, count), out_sha...]
    broadcast_in_dim x2 -> x0, local copies, waits for them, and re-layouts: 1.36 us -> none  [the longest x1 0.79 us: tail(): segment[:, None]]
  transfers between devices with their start and end apart: 1 -> 1, of which waited for: 0 -> 1; matrix products, arithmetic and copies ran while one was open for 1% -> 0% of each run, Pallas kernels for 0% -> 0%
where the time goes in v13:
time: 128 us; the launch traced here: 127 us
  Pallas kernels  108 us (84%)
  local copies, waits for them, and re-layouts  6.04 us (5%)
  between operations  5.8 us (5%)
  starting transfers between devices  3.74 us (3%)
  matrix products  1.93 us (2%)
  other arithmetic  1.42 us (1%)
    pallas_call x1, Pallas kernels, chip_ring_gather(): pl.pallas_call(functools.partial(chip_ring_kernel, count), out_shape=jax....  44.8 us
    pallas_call x1, Pallas kernels, gather_hbm(): pl.pallas_call(functools.partial(gather_hbm_kernel, axis, count), out_sha...  35.5 us
    pallas_call x1, Pallas kernels, tail(): pl.pallas_call(functools.partial(tail_kernel, count, width ** (-0.5)), ou...  27.4 us
    ppermute x1, starting transfers between devices, on_device(): lax.ppermute(all_halves[panel_home[partner_id]], 'tp', partner_perm)  3.74 us
  transfers between devices with their start and end apart: 1, of which 1 were waited for; matrix products, arithmetic and copies ran while one was open for 0% of the time, Pallas kernels for 0%

profile of v13, /device:TPU:1, one launch (start us, length us, event | category | flops | bytes accessed | tf_op | source)
XLA Modules:
  0.0 127.2 jit_solution(8518561513176429997)
XLA Ops:
  0.0 1.4 %fusion.8 = (s32[1]{0:T(128)}, s32[1]{0:T(128)}, s32[1]{0:T(128)}) fusion(s32[48]{0:T(128)} %param.6, s32[]{:T(128)S(6)} %select_n.51, s32[]{:T(128)S(6)} %select_n.59, s32[]{:T(128)S(6)} %select_n.53), kind=kLoop, calls=%fused_computation.13 | loop fusion | bytes 36 | tf_op jit(solution)/shard_map/dynamic_slice | solution.py:505
  5.2 44.8 %shard_map.46 = bf16[16,4,160,128]{3,2,1,0:T(8,128)(2,1)} custom-call(bf16[2,320,128]{2,1,0:T(8,128)(2,1)} %panels_ref.1), custom_call_target="tpu_custom_call" | custom-call | tf_op jit(solution)/shard_map/pallas_call | solution.py:152
  51.9 0.8 dynamic-slice_bitcast_fusion.2
  52.7 3.7 %collective-permute-start = (bf16[160,128]{1,0:T(8,128)(2,1)S(1)}, bf16[160,128]{1,0:T(8,128)(2,1)S(1)}, u32[]{:S(2)}, u32[]{:S(2)}) collective-permute-start(bf16[160,128]{1,0:T(8,128)(2,1)S(1)} %get-tuple-element.7), channel_id=1, source_target_pairs={{0,1},{1,0},{2,3},{3,2},{4,5},{5,4},{6,7},{7,6},{8,9},{9,8},{10,11... | collective-permute-start | bytes 122888 | tf_op jit(solution)/shard_map/ppermute | solution.py:506
  56.5 0.1 broadcast_in_dim.32
  56.6 0.1 broadcast_in_dim.33
  56.7 0.6 collective-permute-done
  57.4 0.7 pad_maximum_fusion.send_ref
  58.0 35.5 %shard_map.47 = bf16[16,480,128]{2,1,0:T(8,128)(2,1)} custom-call(bf16[480,128]{1,0:T(8,128)(2,1)} %pad_maximum_fusion.send_ref), custom_call_target="tpu_custom_call" | custom-call | tf_op jit(solution)/shard_map/pallas_call | solution.py:422
  93.6 0.0 slice-start
  93.6 0.0 copy-start
  93.6 0.0 slice-start.1
  93.6 1.1 slice-done
  94.7 0.7 bitcast_select_fusion
  95.4 0.5 copy-done
  95.9 0.4 slice-done.1
  96.3 1.9 %fusion.4.projected_ref = f32[384,256]{1,0:T(8,128)} fusion(bf16[384,5120]{1,0:T(8,128)(2,1)S(1)} %copy-done, bf16[5120,128]{1,0:T(8,128)(2,1)S(1)} %bitcast_select_fusion, bf16[5120,128]{1,0:T(8,128)(2,1)S(1)} %bitcast.16), kind=kOutput, calls=%fused_computation.5 | convolution fusion | flops 1011875840 | bytes 6946816 | tf_op jit(solution)/shard_map/dot_general | solution.py:520
  98.2 27.4 %shard_map.48 = f32[12,4096]{1,0:T(8,128)} custom-call(f32[384,256]{1,0:T(8,128)} %fusion.4.projected_ref, s32[1,4]{1,0:T(1,128)} %lengths_ref.1), custom_call_target="tpu_custom_call" | custom-call | tf_op jit(solution)/shard_map/pallas_call | solution.py:286
  125.6 1.7 %copy.9 = f32[12,4096]{1,0:T(8,128)} copy(f32[12,4096]{1,0:T(8,128)} %shard_map.48) | data formatting | bytes 393216
  (2 shorter events, 0.0 us)
Async XLA Ops:
  52.7 4.6 %collective-permute-start = (bf16[160,128]{1,0:T(8,128)(2,1)S(1)}, bf16[160,128]{1,0:T(8,128)(2,1)S(1)}, u32[]{:S(2)}, u32[]{:S(2)}) collective-permute-start(bf16[160,128]{1,0:T(8,128)(2,1)S(1)} %get-tuple-element.7), channel_id=1, source_target_pairs={{0,1},{1,0},{2,3},{3,2},{4,5},{5,4},{6,7},{7,6},{8,9},{9,8},{10,11... | collective-permute-start | bytes 122888 | tf_op jit(solution)/shard_map/ppermute | solution.py:506
  93.6 1.1 slice-start
  93.6 2.3 %copy-start = (bf16[384,5120]{1,0:T(8,128)(2,1)S(1)}, bf16[384,5120]{1,0:T(8,128)(2,1)}, u32[]{:S(2)}) copy-start(bf16[384,5120]{1,0:T(8,128)(2,1)} %param.4) | copy-start | bytes 11796484
  93.6 2.7 %slice-start.1 = ((bf16[16,480,128]{2,1,0:T(8,128)(2,1)}), bf16[16,320,128]{2,1,0:T(8,128)(2,1)S(1)}, s32[]{:S(2)}) async-start(bf16[16,480,128]{2,1,0:T(8,128)(2,1)} %shard_map.47), calls=%async_computation.1 | async-start | bytes 2621440 | tf_op jit(solution)/shard_map/slice | solution.py:512

commit v14 on v13

--- a/solution.py
+++ b/solution.py
@@ -433,6 +433,67 @@
     )(x)
 
 
+def weights_gather_kernel(count, own_ref, for_partner_ref, out_ref, partner_rows,
+                          send_sems, recv_sems, partner_sems, local_sems):
+    me = lax.axis_index("grp")
+    member = lax.axis_index("tp")
+    partner = member + 1 - 2 * (member % 2)
+    rows = own_ref.shape[0]
+    barrier = pltpu.get_barrier_semaphore()
+    pl.semaphore_signal(barrier, inc=1, device_id={"tp": partner}, device_id_type=MESH)
+    for step in range(1, count):
+        peer = lax.rem(me + step, count)
+        pl.semaphore_signal(barrier, inc=1, device_id={"grp": peer}, device_id_type=MESH)
+    pl.semaphore_wait(barrier, count)
+    to_partner = pltpu.make_async_remote_copy(
+        src_ref=for_partner_ref, dst_ref=partner_rows, send_sem=partner_sems.at[0],
+        recv_sem=partner_sems.at[1], device_id={"tp": partner}, device_id_type=MESH,
+    )
+    to_partner.start()
+    copies = []
+
+    def spread(part, source, window):
+        for step in range(1, count):
+            peer = lax.rem(me + step, count)
+            copy = pltpu.make_async_remote_copy(
+                src_ref=source,
+                dst_ref=out_ref.at[me, window],
+                send_sem=send_sems.at[part, step],
+                recv_sem=recv_sems.at[part, step],
+                device_id={"grp": peer},
+                device_id_type=MESH,
+            )
+            copy.start()
+            copies.append(copy)
+        local = pltpu.make_async_copy(source, out_ref.at[me, window], local_sems.at[part])
+        local.start()
+        copies.append(local)
+
+    spread(0, own_ref, pl.ds(0, rows))
+    to_partner.wait()
+    spread(1, partner_rows, pl.ds(rows, partner_rows.shape[0]))
+    for copy in copies:
+        copy.wait()
+
+
+def weights_gather(own, for_partner, count, collective_id):
+    rows = own.shape[0] + for_partner.shape[0]
+    return pl.pallas_call(
+        functools.partial(weights_gather_kernel, count),
+        out_shape=jax.ShapeDtypeStruct((count, rows) + own.shape[1:], own.dtype),
+        in_specs=[pl.BlockSpec(memory_space=pltpu.VMEM)] * 2,
+        out_specs=pl.BlockSpec(memory_space=pl.ANY),
+        scratch_shapes=[
+            pltpu.VMEM(for_partner.shape, for_partner.dtype),
+            pltpu.SemaphoreType.DMA((2, count)),
+            pltpu.SemaphoreType.DMA((2, count)),
+            pltpu.SemaphoreType.DMA((2,)),
+            pltpu.SemaphoreType.DMA((2,)),
+        ],
+        compiler_params=pltpu.CompilerParams(collective_id=collective_id, has_side_effects=True),
+    )(own, for_partner)
+
+
 def exchange_kernel(axis, count, scatter, send_ref, out_ref, landed, send_sems, recv_sems):
     me = lax.axis_index(axis)
     barrier = pltpu.get_barrier_semaphore()
@@ -503,14 +564,17 @@
     half = core
     partner_id = member_id ^ 1
     q_mine = all_halves[panel_home[member_id]]
-    q_theirs = lax.ppermute(all_halves[panel_home[partner_id]], "tp", partner_perm)
-    q_block = jnp.where(core == 0, jnp.concatenate([q_mine, q_theirs], axis=0),
-                        jnp.concatenate([q_theirs, q_mine], axis=0))
     kv_half = all_halves[panel_home[kv_panel]]
-    piece = jnp.concatenate([q_block, kv_half], axis=0)
-    gathered = gather_hbm(piece, "grp", grp_count, 0)
-    q_weights = gathered[:, :block_rows].reshape(grp_count * block_rows, head_dim)
-    kv_weights = gathered[:, block_rows:]
+    for_partner = all_halves[panel_home[partner_id]]
+    gathered = weights_gather(jnp.concatenate([q_mine, kv_half], axis=0), for_partner, grp_count, 0)
+    q_here = gathered[:, :half_rows]
+    kv_weights = gathered[:, half_rows:block_rows]
+    q_there = gathered[:, block_rows:]
+    q_weights = jnp.where(
+        core == 0,
+        jnp.concatenate([q_here, q_there], axis=1),
+        jnp.concatenate([q_there, q_here], axis=1),
+    ).reshape(grp_count * block_rows, head_dim)
 
     use_half = lax.broadcasted_iota(jnp.int32, (1, 2, 1, 1), 1) == half
     kv_rows = jnp.where(use_half, kv_weights[:, None], jnp.zeros_like(kv_weights[:, None]))

time: 128 us -> 122 us (0.953)
  Pallas kernels: 108 us -> 104 us
  starting transfers between devices: 3.74 us -> 0 us
  matrix products: 1.93 us -> 4.05 us
    pallas_call x1, Pallas kernels: 35.5 us -> 30 us  [weights_gather(): pl.pallas_call(functools.partial(weights_gather_kernel, count), out_shape...]
    ppermute x1 -> x0, starting transfers between devices: 3.74 us -> none  [on_device(): lax.ppermute(all_halves[panel_home[partner_id]], 'tp', partner_perm)]
    dot_general x1, matrix products: 1.93 us -> 4.05 us  [on_device(): jnp.dot(tokens, both_weights, preferred_element_type=jnp.float32)]
    pallas_call x1, Pallas kernels: 27.4 us -> 28.8 us  [tail(): pl.pallas_call(functools.partial(tail_kernel, count, width ** (-0.5)), ou...]
  transfers between devices with their start and end apart: 1 -> 0, of which waited for: 1 -> 0; matrix products, arithmetic and copies ran while one was open for 0% -> 0% of each run, Pallas kernels for 0% -> 0%
where the time goes in v14:
time: 122 us; the launch traced here: 121 us
  Pallas kernels  104 us (85%)
  local copies, waits for them, and re-layouts  6.33 us (5%)
  between operations  5.74 us (5%)
  matrix products  4.05 us (3%)
  other arithmetic  1.76 us (1%)
    pallas_call x1, Pallas kernels, chip_ring_gather(): pl.pallas_call(functools.partial(chip_ring_kernel, count), out_shape=jax....  44.8 us
    pallas_call x1, Pallas kernels, weights_gather(): pl.pallas_call(functools.partial(weights_gather_kernel, count), out_shape...  30 us
    pallas_call x1, Pallas kernels, tail(): pl.pallas_call(functools.partial(tail_kernel, count, width ** (-0.5)), ou...  28.8 us
    dot_general x1, matrix products, on_device(): jnp.dot(tokens, both_weights, preferred_element_type=jnp.float32)  4.05 us

profile of v14, /device:TPU:1, one launch (start us, length us, event | category | flops | bytes accessed | tf_op | source)
XLA Modules:
  0.0 121.5 jit_solution(11647778138977155302)
XLA Ops:
  0.0 1.4 %fusion.9 = (s32[1]{0:T(128)}, s32[1]{0:T(128)}, s32[1]{0:T(128)}) fusion(s32[48]{0:T(128)} %param.6, s32[]{:T(128)S(6)} %select_n.62, s32[]{:T(128)S(6)} %select_n.55, s32[]{:T(128)S(6)} %select_n.60), kind=kLoop, calls=%fused_computation.14 | loop fusion | bytes 36 | tf_op jit(solution)/shard_map/dynamic_slice | solution.py:568
  7.1 44.8 %shard_map.46 = bf16[16,4,160,128]{3,2,1,0:T(8,128)(2,1)} custom-call(bf16[2,320,128]{2,1,0:T(8,128)(2,1)} %panels_ref.1), custom_call_target="tpu_custom_call" | custom-call | tf_op jit(solution)/shard_map/pallas_call | solution.py:152
  51.9 1.4 %dynamic-slice_bitcast_fusion = (bf16[160,128]{1,0:T(8,128)(2,1)}, bf16[160,128]{1,0:T(8,128)(2,1)S(1)}, bf16[160,128]{1,0:T(8,128)(2,1)S(1)}) fusion(bf16[64,160,128]{2,1,0:T(8,128)(2,1)} %bitcast.16, s32[]{:T(128)S(6)} %select_n.63, s32[]{:T(128)S(6)} %select_n.61, s32[]{:T(128)S(6)} %select_n.56), kind=kLoop, calls=%fused_computation.8 | loop fusion | bytes 245772 | tf_op jit(solution)/shard_map/squeeze | solution.py:568
  53.3 0.6 pad_maximum_fusion.own_ref
  53.9 30.0 %shard_map.47 = bf16[16,480,128]{2,1,0:T(8,128)(2,1)} custom-call(bf16[320,128]{1,0:T(8,128)(2,1)} %pad_maximum_fusion.own_ref, bf16[160,128]{1,0:T(8,128)(2,1)} %get-tuple-element.5.for_partner_ref), custom_call_target="tpu_custom_call" | custom-call | tf_op jit(solution)/shard_map/pallas_call | solution.py:481
  84.0 1.6 %fusion.8 = (bf16[16,160,128]{2,1,0:T(8,128)(2,1)S(1)}, bf16[16,160,128]{2,1,0:T(8,128)(2,1)S(1)}, bf16[16,160,128]{2,1,0:T(8,128)(2,1)S(1)}) fusion(bf16[16,480,128]{2,1,0:T(8,128)(2,1)} %shard_map.47), kind=kLoop, calls=%fused_computation.13 | loop fusion | bytes 3932160 | tf_op jit(solution)/shard_map/slice | solution.py:570
  85.6 0.4 maximum_select_fusion
  86.0 0.1 broadcast_in_dim.32
  86.1 0.1 broadcast_in_dim.33
  86.2 0.7 bitcast_select_fusion
  86.9 4.1 %fusion.4.projected_ref = f32[384,256]{1,0:T(8,128)} fusion(bf16[384,5120]{1,0:T(8,128)(2,1)} %param.4, bf16[5120,128]{1,0:T(8,128)(2,1)S(1)} %bitcast_select_fusion, bf16[5120,128]{1,0:T(8,128)(2,1)S(1)} %bitcast.17), kind=kOutput, calls=%fused_computation.6 | convolution fusion | flops 1011875840 | bytes 6946816 | tf_op jit(solution)/shard_map/dot_general | solution.py:584
  91.0 28.8 %shard_map.48 = f32[12,4096]{1,0:T(8,128)} custom-call(f32[384,256]{1,0:T(8,128)} %fusion.4.projected_ref, s32[1,4]{1,0:T(1,128)} %lengths_ref.1), custom_call_target="tpu_custom_call" | custom-call | tf_op jit(solution)/shard_map/pallas_call | solution.py:286
  119.8 1.7 %copy.9 = f32[12,4096]{1,0:T(8,128)} copy(f32[12,4096]{1,0:T(8,128)} %shard_map.48) | data formatting | bytes 393216
  (1 shorter events, 0.0 us)

commit v15 on v14

--- a/solution.py
+++ b/solution.py
@@ -206,10 +206,9 @@
     )(part)
 
 
-def tail_kernel(count, scale, projected_ref, lengths_ref, out_ref,
+def tail_kernel(count, scale, tokens_ref, weights_ref, lengths_ref, out_ref,
                 part_ref, partner_part, mine, theirs, staged, landed, send_sems, recv_sems):
     width = landed.shape[-1]
-    part_ref[...] = projected_ref[:, width:]
     me = lax.axis_index("tp")
     partner = me + 1 - 2 * (me % 2)
     across = me + 2 - 4 * ((me // 2) % 2)
@@ -217,6 +216,9 @@
     for step in range(1, count):
         peer = lax.rem(me + step, count)
         pl.semaphore_signal(barrier, inc=1, device_id={"tp": peer}, device_id_type=MESH)
+    projected = jnp.dot(tokens_ref[...], weights_ref[...], preferred_element_type=jnp.float32)
+    part_ref[...] = projected[:, width:]
+    query = projected[:, :width].astype(jnp.bfloat16)
     pl.semaphore_wait(barrier, count - 1)
     first = pltpu.make_async_remote_copy(
         src_ref=part_ref, dst_ref=partner_part, send_sem=send_sems.at[0], recv_sem=recv_sems.at[0],
@@ -236,7 +238,7 @@
     values = jnp.where(holds_k, theirs[...], mine[...])
 
     scores = lax.dot_general(
-        projected_ref[:, :width].astype(jnp.bfloat16), keys, (((1,), (1,)), ((), ())), preferred_element_type=jnp.float32
+        query, keys, (((1,), (1,)), ((), ())), preferred_element_type=jnp.float32
     ) * scale
     seq = scores.shape[0]
     row = lax.broadcasted_iota(jnp.int32, (seq, seq), 0)
@@ -278,15 +280,15 @@
         out_ref[:, source * width:(source + 1) * width] = landed[source]
 
 
-def tail(projected, lengths, count, collective_id):
-    seq, width = projected.shape[0], projected.shape[1] // 2
+def tail(tokens, weights, lengths, count, collective_id):
+    seq, width = tokens.shape[0], weights.shape[1] // 2
     part = jax.ShapeDtypeStruct((seq, width), jnp.float32)
     rows = seq // count
     vmem = pl.BlockSpec(memory_space=pltpu.VMEM)
     return pl.pallas_call(
         functools.partial(tail_kernel, count, width ** (-0.5)),
         out_shape=jax.ShapeDtypeStruct((rows, count * width), jnp.float32),
-        in_specs=[vmem, pl.BlockSpec(memory_space=pltpu.SMEM)],
+        in_specs=[vmem, vmem, pl.BlockSpec(memory_space=pltpu.SMEM)],
         out_specs=vmem,
         scratch_shapes=[
             pltpu.VMEM(part.shape, part.dtype),
@@ -299,7 +301,7 @@
             pltpu.SemaphoreType.DMA((count + 1,)),
         ],
         compiler_params=pltpu.CompilerParams(collective_id=collective_id, has_side_effects=True),
-    )(projected, lengths)
+    )(tokens, weights, lengths)
 
 
 def grid_kernel(width, send_ref, out_ref, landed, send_sems, recv_sems):
@@ -581,8 +583,7 @@
     both_weights = jnp.concatenate(
         [q_weights, kv_rows.reshape(grp_count * block_rows, head_dim)], axis=1
     )
-    projected = jnp.dot(tokens, both_weights, preferred_element_type=jnp.float32)
-    return tail(projected, lengths, tp_count, 1)
+    return tail(tokens, both_weights, lengths, tp_count, 1)
 
 
 def solution(mesh):

time: 122 us -> 122 us (level)
  matrix products: 4.05 us -> 0 us
  Pallas kernels: 104 us -> 106 us
  other arithmetic: 1.76 us -> 3.56 us
    dot_general x1 -> x0, matrix products: 4.05 us -> none  [on_device(): jnp.dot(tokens, both_weights, preferred_element_type=jnp.float32)]
    pallas_call x1, Pallas kernels: 28.8 us -> 30.8 us  [tail(): pl.pallas_call(functools.partial(tail_kernel, count, width ** (-0.5)), ou...]
    concatenate x0 -> x1, other arithmetic: none -> 1.79 us  [on_device(): jnp.concatenate([q_weights, kv_rows.reshape(grp_count * block_rows, head_...]
where the time goes in v15:
time: 122 us; the launch traced here: 121 us
  Pallas kernels  106 us (87%)
  local copies, waits for them, and re-layouts  6.33 us (5%)
  between operations  5.72 us (5%)
  other arithmetic  3.56 us (3%)
    pallas_call x1, Pallas kernels, chip_ring_gather(): pl.pallas_call(functools.partial(chip_ring_kernel, count), out_shape=jax....  44.8 us
    pallas_call x1, Pallas kernels, tail(): pl.pallas_call(functools.partial(tail_kernel, count, width ** (-0.5)), ou...  30.8 us
    pallas_call x1, Pallas kernels, weights_gather(): pl.pallas_call(functools.partial(weights_gather_kernel, count), out_shape...  30 us

profile of v15, /device:TPU:1, one launch (start us, length us, event | category | flops | bytes accessed | tf_op | source)
XLA Modules:
  0.0 121.2 jit_solution(15426721434820830675)
XLA Ops:
  0.0 1.4 %fusion.1 = (s32[1]{0:T(128)}, s32[1]{0:T(128)}, s32[1]{0:T(128)}) fusion(s32[48]{0:T(128)} %param.6, s32[]{:T(128)S(6)} %select_n.62, s32[]{:T(128)S(6)} %select_n.55, s32[]{:T(128)S(6)} %select_n.60), kind=kLoop, calls=%fused_computation.9 | loop fusion | bytes 36 | tf_op jit(solution)/shard_map/dynamic_slice | solution.py:570
  7.1 0.1 broadcast_in_dim.32
  7.2 0.1 broadcast_in_dim.33
  7.3 44.8 %shard_map.46 = bf16[16,4,160,128]{3,2,1,0:T(8,128)(2,1)} custom-call(bf16[2,320,128]{2,1,0:T(8,128)(2,1)} %panels_ref.1), custom_call_target="tpu_custom_call" | custom-call | tf_op jit(solution)/shard_map/pallas_call | solution.py:152
  52.0 1.4 %dynamic-slice_bitcast_fusion = (bf16[160,128]{1,0:T(8,128)(2,1)}, bf16[160,128]{1,0:T(8,128)(2,1)S(1)}, bf16[160,128]{1,0:T(8,128)(2,1)S(1)}) fusion(bf16[64,160,128]{2,1,0:T(8,128)(2,1)} %bitcast.14, s32[]{:T(128)S(6)} %select_n.63, s32[]{:T(128)S(6)} %select_n.61, s32[]{:T(128)S(6)} %select_n.56), kind=kLoop, calls=%fused_computation.4 | loop fusion | bytes 245772 | tf_op jit(solution)/shard_map/squeeze | solution.py:570
  53.5 0.6 pad_maximum_fusion.1.own_ref
  54.1 30.0 %shard_map.47 = bf16[16,480,128]{2,1,0:T(8,128)(2,1)} custom-call(bf16[320,128]{1,0:T(8,128)(2,1)} %pad_maximum_fusion.1.own_ref, bf16[160,128]{1,0:T(8,128)(2,1)} %get-tuple-element.5.for_partner_ref), custom_call_target="tpu_custom_call" | custom-call | tf_op jit(solution)/shard_map/pallas_call | solution.py:483
  84.2 1.6 %fusion = (bf16[16,160,128]{2,1,0:T(8,128)(2,1)S(1)}, bf16[16,160,128]{2,1,0:T(8,128)(2,1)S(1)}, bf16[16,160,128]{2,1,0:T(8,128)(2,1)S(1)}) fusion(bf16[16,480,128]{2,1,0:T(8,128)(2,1)} %shard_map.47), kind=kLoop, calls=%fused_computation.8 | loop fusion | bytes 3932160 | tf_op jit(solution)/shard_map/slice | solution.py:572
  85.8 0.4 maximum_select_fusion
  86.2 0.7 bitcast_select_fusion
  86.9 1.8 %pad_maximum_fusion.weights_ref = bf16[5120,256]{1,0:T(8,128)(2,1)} fusion(bf16[5120,128]{1,0:T(8,128)(2,1)S(1)} %bitcast_select_fusion, bf16[5120,128]{1,0:T(8,128)(2,1)S(1)} %bitcast.13), kind=kLoop, calls=%fused_computation | loop fusion | flops 5242880 | bytes 5242880 | tf_op jit(solution)/shard_map/concatenate | solution.py:583
  88.7 30.8 %shard_map.48 = f32[12,4096]{1,0:T(8,128)} custom-call(bf16[384,5120]{1,0:T(8,128)(2,1)} %tokens_ref.1, bf16[5120,256]{1,0:T(8,128)(2,1)} %pad_maximum_fusion.weights_ref, s32[1,4]{1,0:T(1,128)} %lengths_ref.1), custom_call_target="tpu_custom_call" | custom-call | tf_op jit(solution)/shard_map/pallas_call | solution.py:288
  119.5 1.7 %copy.6 = f32[12,4096]{1,0:T(8,128)} copy(f32[12,4096]{1,0:T(8,128)} %shard_map.48) | data formatting | bytes 393216
  (1 shorter events, 0.0 us)

commit v16 on v15

--- a/solution.py
+++ b/solution.py
@@ -206,17 +206,42 @@
     )(part)
 
 
-def tail_kernel(count, scale, tokens_ref, weights_ref, lengths_ref, out_ref,
-                part_ref, partner_part, mine, theirs, staged, landed, send_sems, recv_sems):
+def tail_kernel(count, scale, tokens_ref, gathered_hbm, lengths_ref, out_ref,
+                gathered, load_sem, part_ref, partner_part, mine, theirs, staged, landed, send_sems, recv_sems):
     width = landed.shape[-1]
     me = lax.axis_index("tp")
     partner = me + 1 - 2 * (me % 2)
     across = me + 2 - 4 * ((me // 2) % 2)
+    load = pltpu.make_async_copy(gathered_hbm, gathered, load_sem)
+    load.start()
     barrier = pltpu.get_barrier_semaphore()
     for step in range(1, count):
         peer = lax.rem(me + step, count)
         pl.semaphore_signal(barrier, inc=1, device_id={"tp": peer}, device_id_type=MESH)
-    projected = jnp.dot(tokens_ref[...], weights_ref[...], preferred_element_type=jnp.float32)
+    load.wait()
+    core = me % 2
+    half = gathered.shape[1] // 3
+    sources = gathered.shape[0]
+    first_half = core == 0
+    projected = jnp.zeros((tokens_ref.shape[0], 2 * width), jnp.float32)
+    for pair in range(sources // 2):
+        q_parts, kv_parts = [], []
+        for source in (2 * pair, 2 * pair + 1):
+            here = gathered[source, 0:half]
+            kv = gathered[source, half:2 * half]
+            there = gathered[source, 2 * half:3 * half]
+            zero = jnp.zeros_like(kv)
+            q_parts.append(jnp.where(first_half, jnp.concatenate([here, there], axis=0),
+                                     jnp.concatenate([there, here], axis=0)))
+            kv_parts.append(jnp.where(first_half, jnp.concatenate([kv, zero], axis=0),
+                                      jnp.concatenate([zero, kv], axis=0)))
+        slab = jnp.concatenate(
+            [jnp.concatenate(q_parts, axis=0), jnp.concatenate(kv_parts, axis=0)], axis=1
+        )
+        columns = slab.shape[0]
+        projected = projected + jnp.dot(
+            tokens_ref[:, pair * columns:(pair + 1) * columns], slab, preferred_element_type=jnp.float32
+        )
     part_ref[...] = projected[:, width:]
     query = projected[:, :width].astype(jnp.bfloat16)
     pl.semaphore_wait(barrier, count - 1)
@@ -280,17 +305,19 @@
         out_ref[:, source * width:(source + 1) * width] = landed[source]
 
 
-def tail(tokens, weights, lengths, count, collective_id):
-    seq, width = tokens.shape[0], weights.shape[1] // 2
+def tail(tokens, gathered, lengths, count, collective_id):
+    seq, width = tokens.shape[0], gathered.shape[2]
     part = jax.ShapeDtypeStruct((seq, width), jnp.float32)
     rows = seq // count
     vmem = pl.BlockSpec(memory_space=pltpu.VMEM)
     return pl.pallas_call(
         functools.partial(tail_kernel, count, width ** (-0.5)),
         out_shape=jax.ShapeDtypeStruct((rows, count * width), jnp.float32),
-        in_specs=[vmem, vmem, pl.BlockSpec(memory_space=pltpu.SMEM)],
+        in_specs=[vmem, pl.BlockSpec(memory_space=pl.ANY), pl.BlockSpec(memory_space=pltpu.SMEM)],
         out_specs=vmem,
         scratch_shapes=[
+            pltpu.VMEM(gathered.shape, gathered.dtype),
+            pltpu.SemaphoreType.DMA(()),
             pltpu.VMEM(part.shape, part.dtype),
             pltpu.VMEM(part.shape, part.dtype),
             pltpu.VMEM(part.shape, jnp.bfloat16),
@@ -301,7 +328,7 @@
             pltpu.SemaphoreType.DMA((count + 1,)),
         ],
         compiler_params=pltpu.CompilerParams(collective_id=collective_id, has_side_effects=True),
-    )(tokens, weights, lengths)
+    )(tokens, gathered, lengths)
 
 
 def grid_kernel(width, send_ref, out_ref, landed, send_sems, recv_sems):
@@ -569,21 +596,7 @@
     kv_half = all_halves[panel_home[kv_panel]]
     for_partner = all_halves[panel_home[partner_id]]
     gathered = weights_gather(jnp.concatenate([q_mine, kv_half], axis=0), for_partner, grp_count, 0)
-    q_here = gathered[:, :half_rows]
-    kv_weights = gathered[:, half_rows:block_rows]
-    q_there = gathered[:, block_rows:]
-    q_weights = jnp.where(
-        core == 0,
-        jnp.concatenate([q_here, q_there], axis=1),
-        jnp.concatenate([q_there, q_here], axis=1),
-    ).reshape(grp_count * block_rows, head_dim)
-
-    use_half = lax.broadcasted_iota(jnp.int32, (1, 2, 1, 1), 1) == half
-    kv_rows = jnp.where(use_half, kv_weights[:, None], jnp.zeros_like(kv_weights[:, None]))
-    both_weights = jnp.concatenate(
-        [q_weights, kv_rows.reshape(grp_count * block_rows, head_dim)], axis=1
-    )
-    return tail(tokens, both_weights, lengths, tp_count, 1)
+    return tail(tokens, gathered, lengths, tp_count, 1)
 
 
 def solution(mesh):

time: 122 us -> 116 us (0.951)
  other arithmetic: 3.56 us -> 0.64 us
  local copies, waits for them, and re-layouts: 6.33 us -> 4.53 us
    concatenate x1 -> x0, other arithmetic: 1.79 us -> none  [on_device(): jnp.concatenate([q_weights, kv_rows.reshape(grp_count * block_rows, head_...]
    slice x1 -> x0, local copies, waits for them, and re-layouts: 1.62 us -> none  [on_device(): q_here = gathered[:, :half_rows]]
where the time goes in v16:
time: 116 us
  Pallas kernels  105 us (91%)
  between operations  5.77 us (5%)
  local copies, waits for them, and re-layouts  4.53 us (4%)
    pallas_call x1, Pallas kernels, chip_ring_gather(): pl.pallas_call(functools.partial(chip_ring_kernel, count), out_shape=jax....  44.8 us
    pallas_call x1, Pallas kernels, weights_gather(): pl.pallas_call(functools.partial(weights_gather_kernel, count), out_shape...  30 us
    pallas_call x1, Pallas kernels, tail(): pl.pallas_call(functools.partial(tail_kernel, count, width ** (-0.5)), ou...  30 us

profile of v16, /device:TPU:1, one launch (start us, length us, event | category | flops | bytes accessed | tf_op | source)
XLA Modules:
  0.0 115.8 jit_solution(8530255759142736739)
XLA Ops:
  0.0 1.4 %fusion = (s32[1]{0:T(128)}, s32[1]{0:T(128)}, s32[1]{0:T(128)}) fusion(s32[48]{0:T(128)} %param.6, s32[]{:T(128)S(6)} %select_n.39, s32[]{:T(128)S(6)} %select_n.32, s32[]{:T(128)S(6)} %select_n.37), kind=kLoop, calls=%fused_computation.4 | loop fusion | bytes 36 | tf_op jit(solution)/shard_map/dynamic_slice | solution.py:597
  7.2 44.8 %shard_map.46 = bf16[16,4,160,128]{3,2,1,0:T(8,128)(2,1)} custom-call(bf16[2,320,128]{2,1,0:T(8,128)(2,1)} %panels_ref.1), custom_call_target="tpu_custom_call" | custom-call | tf_op jit(solution)/shard_map/pallas_call | solution.py:152
  51.9 1.4 %dynamic-slice_bitcast_fusion = (bf16[160,128]{1,0:T(8,128)(2,1)}, bf16[160,128]{1,0:T(8,128)(2,1)S(1)}, bf16[160,128]{1,0:T(8,128)(2,1)S(1)}) fusion(bf16[64,160,128]{2,1,0:T(8,128)(2,1)} %bitcast.10, s32[]{:T(128)S(6)} %select_n.40, s32[]{:T(128)S(6)} %select_n.38, s32[]{:T(128)S(6)} %select_n.33), kind=kLoop, calls=%fused_computation.1 | loop fusion | bytes 245772 | tf_op jit(solution)/shard_map/squeeze | solution.py:597
  53.4 0.6 pad_maximum_fusion.own_ref
  54.0 30.0 %shard_map.47.gathered_hbm = bf16[16,480,128]{2,1,0:T(8,128)(2,1)} custom-call(bf16[320,128]{1,0:T(8,128)(2,1)} %pad_maximum_fusion.own_ref, bf16[160,128]{1,0:T(8,128)(2,1)} %get-tuple-element.5.for_partner_ref), custom_call_target="tpu_custom_call" | custom-call | tf_op jit(solution)/shard_map/pallas_call | solution.py:510
  84.1 30.0 %shard_map.48 = f32[12,4096]{1,0:T(8,128)} custom-call(bf16[384,5120]{1,0:T(8,128)(2,1)} %tokens_ref.1, bf16[16,480,128]{2,1,0:T(8,128)(2,1)} %shard_map.47.gathered_hbm, s32[1,4]{1,0:T(1,128)} %lengths_ref.1), custom_call_target="tpu_custom_call" | custom-call | tf_op jit(solution)/shard_map/pallas_call | solution.py:313
  114.1 1.7 %copy.6 = f32[12,4096]{1,0:T(8,128)} copy(f32[12,4096]{1,0:T(8,128)} %shard_map.48) | data formatting | bytes 393216

commit v17 on v16

--- a/solution.py
+++ b/solution.py
@@ -77,7 +77,7 @@
     return gathered.reshape((count * x.shape[0] * x.shape[1],) + x.shape[2:])
 
 
-def chip_ring_kernel(count, panels_ref, out_ref, landed, send_sems, recv_sems):
+def chip_ring_kernel(count, panels_ref, home_ref, own_ref, partner_ref, landed, send_sems, recv_sems):
     me = lax.axis_index("tp")
     total = 2 * count
     core = me % 2
@@ -144,23 +144,39 @@
         incoming(lax.rem(spot + far_left, count), chunk).wait_recv()
     for copy in sends:
         copy.wait_send()
-    out_ref[...] = landed[...]
-
-
-def chip_ring_gather(panels, count, collective_id):
+    heads = total
+    kv_heads = (home_ref.shape[0] - heads) // 2
+    group = heads // kv_heads
+    quarter = me % group
+    kv_panel = heads + me // group + kv_heads * (quarter // 2)
+    chip_slots = landed.shape[1]
+
+    def block(panel):
+        slot = home_ref[panel]
+        return landed[slot // chip_slots, slot % chip_slots]
+
+    own_ref[0:half] = block(me)
+    own_ref[half:2 * half] = block(kv_panel)
+    partner_ref[...] = block(partner)
+
+
+def chip_ring_gather(panels, home, count, collective_id):
     slots, rows, width = panels.shape
     return pl.pallas_call(
         functools.partial(chip_ring_kernel, count),
-        out_shape=jax.ShapeDtypeStruct((count, 2 * slots, rows // 2, width), panels.dtype),
-        in_specs=[pl.BlockSpec(memory_space=pltpu.VMEM)],
-        out_specs=pl.BlockSpec(memory_space=pltpu.VMEM),
+        out_shape=(
+            jax.ShapeDtypeStruct((rows, width), panels.dtype),
+            jax.ShapeDtypeStruct((rows // 2, width), panels.dtype),
+        ),
+        in_specs=[pl.BlockSpec(memory_space=pltpu.VMEM), pl.BlockSpec(memory_space=pltpu.SMEM)],
+        out_specs=(pl.BlockSpec(memory_space=pltpu.VMEM), pl.BlockSpec(memory_space=pltpu.VMEM)),
         scratch_shapes=[
             pltpu.VMEM((count, 2 * slots, rows // 2, width), panels.dtype),
             pltpu.SemaphoreType.DMA((2, count // 2 + 1, 2 * slots)),
             pltpu.SemaphoreType.DMA((count, 2 * slots)),
         ],
         compiler_params=pltpu.CompilerParams(collective_id=collective_id, has_side_effects=True),
-    )(panels)
+    )(panels, home)
 
 
 def kv_share_kernel(part_ref, out_ref, partner_part, mine, theirs, send_sems, recv_sems):
@@ -583,19 +599,8 @@
     half_rows = block_rows // 2
     seq_total = tokens.shape[0]
 
-    core = member_id % 2
-    partner_perm = [(i, i ^ 1) for i in range(tp_count)]
-    all_halves = chip_ring_gather(trainer_panels, tp_count // 2, 2)
-    all_halves = all_halves.reshape((-1,) + all_halves.shape[2:])
-    kv_id = member_id // group_size
-    quarter = member_id % group_size
-    kv_panel = tp_count + kv_id + kv_count * (quarter // 2)
-    half = core
-    partner_id = member_id ^ 1
-    q_mine = all_halves[panel_home[member_id]]
-    kv_half = all_halves[panel_home[kv_panel]]
-    for_partner = all_halves[panel_home[partner_id]]
-    gathered = weights_gather(jnp.concatenate([q_mine, kv_half], axis=0), for_partner, grp_count, 0)
+    own, for_partner = chip_ring_gather(trainer_panels, panel_home, tp_count // 2, 2)
+    gathered = weights_gather(own, for_partner, grp_count, 0)
     return tail(tokens, gathered, lengths, tp_count, 1)
 
 

time: 116 us -> 106 us (0.914)
  between operations: 5.77 us -> 0.02 us
  local copies, waits for them, and re-layouts: 4.53 us -> 1.67 us
    squeeze x1 -> x0, local copies, waits for them, and re-layouts: 1.44 us -> none  [on_device(): for_partner = all_halves[panel_home[partner_id]]]
    dynamic_slice x1 -> x0, local copies, waits for them, and re-layouts: 1.42 us -> none  [on_device(): for_partner = all_halves[panel_home[partner_id]]]
where the time goes in v17:
time: 106 us
  Pallas kernels  104 us (98%)
  local copies, waits for them, and re-layouts  1.67 us (2%)
    pallas_call x1, Pallas kernels, chip_ring_gather(): pl.pallas_call(functools.partial(chip_ring_kernel, count), out_shape=(jax...  43.8 us
    pallas_call x1, Pallas kernels, weights_gather(): pl.pallas_call(functools.partial(weights_gather_kernel, count), out_shape...  30 us
    pallas_call x1, Pallas kernels, tail(): pl.pallas_call(functools.partial(tail_kernel, count, width ** (-0.5)), ou...  30 us

profile of v17, /device:TPU:1, one launch (start us, length us, event | category | flops | bytes accessed | tf_op | source)
XLA Modules:
  0.0 105.5 jit_solution(8176062770294700262)
XLA Ops:
  0.0 43.8 %shard_map.46 = (bf16[320,128]{1,0:T(8,128)(2,1)}, bf16[160,128]{1,0:T(8,128)(2,1)}) custom-call(bf16[2,320,128]{2,1,0:T(8,128)(2,1)} %panels_ref.1, s32[48]{0:T(128)} %home_ref.1), custom_call_target="tpu_custom_call" | custom-call | tf_op jit(solution)/shard_map/pallas_call | solution.py:165
  43.8 30.0 %shard_map.47.gathered_hbm = bf16[16,480,128]{2,1,0:T(8,128)(2,1)} custom-call(bf16[320,128]{1,0:T(8,128)(2,1)} %get-tuple-element.7.own_ref, bf16[160,128]{1,0:T(8,128)(2,1)} %get-tuple-element.8.for_partner_ref), custom_call_target="tpu_custom_call" | custom-call | tf_op jit(solution)/shard_map/pallas_call | solution.py:526
  73.9 30.0 %shard_map.48 = f32[12,4096]{1,0:T(8,128)} custom-call(bf16[384,5120]{1,0:T(8,128)(2,1)} %tokens_ref.1, bf16[16,480,128]{2,1,0:T(8,128)(2,1)} %shard_map.47.gathered_hbm, s32[1,4]{1,0:T(1,128)} %lengths_ref.1), custom_call_target="tpu_custom_call" | custom-call | tf_op jit(solution)/shard_map/pallas_call | solution.py:329
  103.9 1.7 %copy.6 = f32[12,4096]{1,0:T(8,128)} copy(f32[12,4096]{1,0:T(8,128)} %shard_map.48) | data formatting | bytes 393216

commit v18 on v17

--- a/solution.py
+++ b/solution.py
@@ -239,33 +239,36 @@
     half = gathered.shape[1] // 3
     sources = gathered.shape[0]
     first_half = core == 0
-    projected = jnp.zeros((tokens_ref.shape[0], 2 * width), jnp.float32)
-    for pair in range(sources // 2):
-        q_parts, kv_parts = [], []
-        for source in (2 * pair, 2 * pair + 1):
-            here = gathered[source, 0:half]
-            kv = gathered[source, half:2 * half]
-            there = gathered[source, 2 * half:3 * half]
-            zero = jnp.zeros_like(kv)
-            q_parts.append(jnp.where(first_half, jnp.concatenate([here, there], axis=0),
-                                     jnp.concatenate([there, here], axis=0)))
-            kv_parts.append(jnp.where(first_half, jnp.concatenate([kv, zero], axis=0),
-                                      jnp.concatenate([zero, kv], axis=0)))
-        slab = jnp.concatenate(
-            [jnp.concatenate(q_parts, axis=0), jnp.concatenate(kv_parts, axis=0)], axis=1
-        )
-        columns = slab.shape[0]
-        projected = projected + jnp.dot(
-            tokens_ref[:, pair * columns:(pair + 1) * columns], slab, preferred_element_type=jnp.float32
-        )
-    part_ref[...] = projected[:, width:]
-    query = projected[:, :width].astype(jnp.bfloat16)
+    def project(which):
+        total = jnp.zeros((tokens_ref.shape[0], width), jnp.float32)
+        for pair in range(sources // 2):
+            parts = []
+            for source in (2 * pair, 2 * pair + 1):
+                here = gathered[source, 0:half]
+                kv = gathered[source, half:2 * half]
+                there = gathered[source, 2 * half:3 * half]
+                if which == "q":
+                    parts.append(jnp.where(first_half, jnp.concatenate([here, there], axis=0),
+                                           jnp.concatenate([there, here], axis=0)))
+                else:
+                    zero = jnp.zeros_like(kv)
+                    parts.append(jnp.where(first_half, jnp.concatenate([kv, zero], axis=0),
+                                           jnp.concatenate([zero, kv], axis=0)))
+            slab = jnp.concatenate(parts, axis=0)
+            columns = slab.shape[0]
+            total = total + jnp.dot(
+                tokens_ref[:, pair * columns:(pair + 1) * columns], slab, preferred_element_type=jnp.float32
+            )
+        return total
+
+    part_ref[...] = project("kv")
     pl.semaphore_wait(barrier, count - 1)
     first = pltpu.make_async_remote_copy(
         src_ref=part_ref, dst_ref=partner_part, send_sem=send_sems.at[0], recv_sem=recv_sems.at[0],
         device_id={"tp": partner}, device_id_type=MESH,
     )
     first.start()
+    query = project("q").astype(jnp.bfloat16)
     first.wait()
     mine[...] = (part_ref[...] + partner_part[...]).astype(mine.dtype)
     second = pltpu.make_async_remote_copy(

time: 106 us -> 106 us (level)
  no operation moved by 1% of the time
where the time goes in v18:
time: 106 us; the launch traced here: 105 us
  Pallas kernels  104 us (98%)
  local copies, waits for them, and re-layouts  1.67 us (2%)
    pallas_call x1, Pallas kernels, chip_ring_gather(): pl.pallas_call(functools.partial(chip_ring_kernel, count), out_shape=(jax...  43.8 us
    pallas_call x1, Pallas kernels, weights_gather(): pl.pallas_call(functools.partial(weights_gather_kernel, count), out_shape...  30 us
    pallas_call x1, Pallas kernels, tail(): pl.pallas_call(functools.partial(tail_kernel, count, width ** (-0.5)), ou...  29.9 us

profile of v18, /device:TPU:1, one launch (start us, length us, event | category | flops | bytes accessed | tf_op | source)
XLA Modules:
  0.0 105.5 jit_solution(7331635647115409302)
XLA Ops:
  0.0 43.8 %shard_map.46 = (bf16[320,128]{1,0:T(8,128)(2,1)}, bf16[160,128]{1,0:T(8,128)(2,1)}) custom-call(bf16[2,320,128]{2,1,0:T(8,128)(2,1)} %panels_ref.1, s32[48]{0:T(128)} %home_ref.1), custom_call_target="tpu_custom_call" | custom-call | tf_op jit(solution)/shard_map/pallas_call | solution.py:165
  43.8 30.0 %shard_map.47.gathered_hbm = bf16[16,480,128]{2,1,0:T(8,128)(2,1)} custom-call(bf16[320,128]{1,0:T(8,128)(2,1)} %get-tuple-element.7.own_ref, bf16[160,128]{1,0:T(8,128)(2,1)} %get-tuple-element.8.for_partner_ref), custom_call_target="tpu_custom_call" | custom-call | tf_op jit(solution)/shard_map/pallas_call | solution.py:529
  73.9 29.9 %shard_map.48 = f32[12,4096]{1,0:T(8,128)} custom-call(bf16[384,5120]{1,0:T(8,128)(2,1)} %tokens_ref.1, bf16[16,480,128]{2,1,0:T(8,128)(2,1)} %shard_map.47.gathered_hbm, s32[1,4]{1,0:T(1,128)} %lengths_ref.1), custom_call_target="tpu_custom_call" | custom-call | tf_op jit(solution)/shard_map/pallas_call | solution.py:332
  103.8 1.7 %copy.6 = f32[12,4096]{1,0:T(8,128)} copy(f32[12,4096]{1,0:T(8,128)} %shard_map.48) | data formatting | bytes 393216

commit v19 on v17

--- a/solution.py
+++ b/solution.py
@@ -317,8 +317,7 @@
     landed[me] = staged[me]
     for copy in copies:
         copy.wait()
-    for source in range(count):
-        out_ref[:, source * width:(source + 1) * width] = landed[source]
+    out_ref[...] = landed[...]
 
 
 def tail(tokens, gathered, lengths, count, collective_id):
@@ -328,7 +327,7 @@
     vmem = pl.BlockSpec(memory_space=pltpu.VMEM)
     return pl.pallas_call(
         functools.partial(tail_kernel, count, width ** (-0.5)),
-        out_shape=jax.ShapeDtypeStruct((rows, count * width), jnp.float32),
+        out_shape=jax.ShapeDtypeStruct((count, rows, width), jnp.float32),
         in_specs=[vmem, pl.BlockSpec(memory_space=pl.ANY), pl.BlockSpec(memory_space=pltpu.SMEM)],
         out_specs=vmem,
         scratch_shapes=[
@@ -601,7 +600,8 @@
 
     own, for_partner = chip_ring_gather(trainer_panels, panel_home, tp_count // 2, 2)
     gathered = weights_gather(own, for_partner, grp_count, 0)
-    return tail(tokens, gathered, lengths, tp_count, 1)
+    arrived = tail(tokens, gathered, lengths, tp_count, 1)
+    return jnp.transpose(arrived, (1, 0, 2)).reshape(arrived.shape[1], tp_count * head_dim)
 
 
 def solution(mesh):

time: 106 us -> 106 us (level)
  no operation moved by 1% of the time
where the time goes in v19:
time: 106 us
  Pallas kernels  104 us (98%)
  local copies, waits for them, and re-layouts  1.89 us (2%)
    pallas_call x1, Pallas kernels, chip_ring_gather(): pl.pallas_call(functools.partial(chip_ring_kernel, count), out_shape=(jax...  43.8 us
    pallas_call x1, Pallas kernels, weights_gather(): pl.pallas_call(functools.partial(weights_gather_kernel, count), out_shape...  30 us
    pallas_call x1, Pallas kernels, tail(): pl.pallas_call(functools.partial(tail_kernel, count, width ** (-0.5)), ou...  30 us

profile of v19, /device:TPU:1, one launch (start us, length us, event | category | flops | bytes accessed | tf_op | source)
XLA Modules:
  0.0 105.8 jit_solution(11095923972222808947)
XLA Ops:
  0.0 43.8 %shard_map.46 = (bf16[320,128]{1,0:T(8,128)(2,1)}, bf16[160,128]{1,0:T(8,128)(2,1)}) custom-call(bf16[2,320,128]{2,1,0:T(8,128)(2,1)} %panels_ref.1, s32[48]{0:T(128)} %home_ref.1), custom_call_target="tpu_custom_call" | custom-call | tf_op jit(solution)/shard_map/pallas_call | solution.py:165
  43.8 30.0 %shard_map.47.gathered_hbm = bf16[16,480,128]{2,1,0:T(8,128)(2,1)} custom-call(bf16[320,128]{1,0:T(8,128)(2,1)} %get-tuple-element.7.own_ref, bf16[160,128]{1,0:T(8,128)(2,1)} %get-tuple-element.8.for_partner_ref), custom_call_target="tpu_custom_call" | custom-call | tf_op jit(solution)/shard_map/pallas_call | solution.py:525
  73.9 30.0 %shard_map.48 = f32[32,12,128]{2,1,0:T(8,128)} custom-call(bf16[384,5120]{1,0:T(8,128)(2,1)} %tokens_ref.1, bf16[16,480,128]{2,1,0:T(8,128)(2,1)} %shard_map.47.gathered_hbm, s32[1,4]{1,0:T(1,128)} %lengths_ref.1), custom_call_target="tpu_custom_call" | custom-call | tf_op jit(solution)/shard_map/pallas_call | solution.py:328
  103.9 1.0 copy.5
  104.9 0.9 copy.6
  (1 shorter events, 0.0 us)

commit v20 on v17

--- a/solution.py
+++ b/solution.py
@@ -77,8 +77,10 @@
     return gathered.reshape((count * x.shape[0] * x.shape[1],) + x.shape[2:])
 
 
-def chip_ring_kernel(count, panels_ref, home_ref, own_ref, partner_ref, landed, send_sems, recv_sems):
+def chip_ring_kernel(count, groups, panels_ref, home_ref, out_ref, landed, send_sems, recv_sems,
+                     own_ref, partner_ref, partner_rows, grp_send_sems, grp_recv_sems, partner_sems, local_sems):
     me = lax.axis_index("tp")
+    here = lax.axis_index("grp")
     total = 2 * count
     core = me % 2
     partner = me + 1 - 2 * core
@@ -88,7 +90,10 @@
     barrier = pltpu.get_barrier_semaphore()
     for neighbour in (left, right, partner):
         pl.semaphore_signal(barrier, inc=1, device_id={"tp": neighbour}, device_id_type=MESH)
-    pl.semaphore_wait(barrier, 3)
+    for step in range(1, groups):
+        peer = lax.rem(here + step, groups)
+        pl.semaphore_signal(barrier, inc=1, device_id={"grp": peer}, device_id_type=MESH)
+    pl.semaphore_wait(barrier, 2 + groups)
 
     def rows_of(slot, which):
         return panels_ref.at[slot, pl.ds(pl.multiple_of(which * half, 16), half)]
@@ -159,21 +164,55 @@
     own_ref[half:2 * half] = block(kv_panel)
     partner_ref[...] = block(partner)
 
-
-def chip_ring_gather(panels, home, count, collective_id):
+    to_partner = pltpu.make_async_remote_copy(
+        src_ref=partner_ref, dst_ref=partner_rows, send_sem=partner_sems.at[0],
+        recv_sem=partner_sems.at[1], device_id={"tp": partner}, device_id_type=MESH,
+    )
+    to_partner.start()
+    copies = []
+
+    def spread(part, source, window):
+        for step in range(1, groups):
+            peer = lax.rem(here + step, groups)
+            copy = pltpu.make_async_remote_copy(
+                src_ref=source,
+                dst_ref=out_ref.at[here, window],
+                send_sem=grp_send_sems.at[part, step],
+                recv_sem=grp_recv_sems.at[part, step],
+                device_id={"grp": peer},
+                device_id_type=MESH,
+            )
+            copy.start()
+            copies.append(copy)
+        local = pltpu.make_async_copy(source, out_ref.at[here, window], local_sems.at[part])
+        local.start()
+        copies.append(local)
+
+    spread(0, own_ref, pl.ds(0, 2 * half))
+    to_partner.wait()
+    spread(1, partner_rows, pl.ds(2 * half, half))
+    for copy in copies:
+        copy.wait()
+
+
+def chip_ring_gather(panels, home, count, groups, collective_id):
     slots, rows, width = panels.shape
     return pl.pallas_call(
-        functools.partial(chip_ring_kernel, count),
-        out_shape=(
-            jax.ShapeDtypeStruct((rows, width), panels.dtype),
-            jax.ShapeDtypeStruct((rows // 2, width), panels.dtype),
-        ),
+        functools.partial(chip_ring_kernel, count, groups),
+        out_shape=jax.ShapeDtypeStruct((groups, rows + rows // 2, width), panels.dtype),
         in_specs=[pl.BlockSpec(memory_space=pltpu.VMEM), pl.BlockSpec(memory_space=pltpu.SMEM)],
-        out_specs=(pl.BlockSpec(memory_space=pltpu.VMEM), pl.BlockSpec(memory_space=pltpu.VMEM)),
+        out_specs=pl.BlockSpec(memory_space=pl.ANY),
         scratch_shapes=[
             pltpu.VMEM((count, 2 * slots, rows // 2, width), panels.dtype),
             pltpu.SemaphoreType.DMA((2, count // 2 + 1, 2 * slots)),
             pltpu.SemaphoreType.DMA((count, 2 * slots)),
+            pltpu.VMEM((rows, width), panels.dtype),
+            pltpu.VMEM((rows // 2, width), panels.dtype),
+            pltpu.VMEM((rows // 2, width), panels.dtype),
+            pltpu.SemaphoreType.DMA((2, groups)),
+            pltpu.SemaphoreType.DMA((2, groups)),
+            pltpu.SemaphoreType.DMA((2,)),
+            pltpu.SemaphoreType.DMA((2,)),
         ],
         compiler_params=pltpu.CompilerParams(collective_id=collective_id, has_side_effects=True),
     )(panels, home)
@@ -599,8 +638,7 @@
     half_rows = block_rows // 2
     seq_total = tokens.shape[0]
 
-    own, for_partner = chip_ring_gather(trainer_panels, panel_home, tp_count // 2, 2)
-    gathered = weights_gather(own, for_partner, grp_count, 0)
+    gathered = chip_ring_gather(trainer_panels, panel_home, tp_count // 2, grp_count, 2)
     return tail(tokens, gathered, lengths, tp_count, 1)
 
 

time: 106 us -> 103 us (0.972)
  Pallas kernels: 104 us -> 101 us
    pallas_call x2 -> x1, Pallas kernels: 73.8 us -> 71.6 us  [chip_ring_gather(): pl.pallas_call(functools.partial(chip_ring_kernel, count, groups), out_sh...]
where the time goes in v20:
time: 103 us
  Pallas kernels  101 us (98%)
  local copies, waits for them, and re-layouts  1.67 us (2%)
    pallas_call x1, Pallas kernels, chip_ring_gather(): pl.pallas_call(functools.partial(chip_ring_kernel, count, groups), out_sh...  71.6 us
    pallas_call x1, Pallas kernels, tail(): pl.pallas_call(functools.partial(tail_kernel, count, width ** (-0.5)), ou...  29.3 us

profile of v20, /device:TPU:1, one launch (start us, length us, event | category | flops | bytes accessed | tf_op | source)
XLA Modules:
  0.0 102.6 jit_solution(8507586251010512462)
XLA Ops:
  0.0 71.6 %shard_map.46.gathered_hbm = bf16[16,480,128]{2,1,0:T(8,128)(2,1)} custom-call(bf16[2,320,128]{2,1,0:T(8,128)(2,1)} %panels_ref.1, s32[48]{0:T(128)} %home_ref.1), custom_call_target="tpu_custom_call" | custom-call | tf_op jit(solution)/shard_map/pallas_call | solution.py:200
  71.6 29.3 %shard_map.47 = f32[12,4096]{1,0:T(8,128)} custom-call(bf16[384,5120]{1,0:T(8,128)(2,1)} %tokens_ref.1, bf16[16,480,128]{2,1,0:T(8,128)(2,1)} %shard_map.46.gathered_hbm, s32[1,4]{1,0:T(1,128)} %lengths_ref.1), custom_call_target="tpu_custom_call" | custom-call | tf_op jit(solution)/shard_map/pallas_call | solution.py:368
  100.9 1.7 %copy.6 = f32[12,4096]{1,0:T(8,128)} copy(f32[12,4096]{1,0:T(8,128)} %shard_map.47) | data formatting | bytes 393216

commit v21 on v20

--- a/solution.py
+++ b/solution.py
@@ -78,7 +78,8 @@
 
 
 def chip_ring_kernel(count, groups, panels_ref, home_ref, out_ref, landed, send_sems, recv_sems,
-                     own_ref, partner_ref, partner_rows, grp_send_sems, grp_recv_sems, partner_sems, local_sems):
+                     own_ref, partner_ref, partner_rows, grp_send_sems, grp_recv_sems, partner_sems, local_sems,
+                     greet=True):
     me = lax.axis_index("tp")
     here = lax.axis_index("grp")
     total = 2 * count
@@ -87,13 +88,14 @@
     right, left = lax.rem(me + 2, total), lax.rem(me + total - 2, total)
     spot = me // 2
     half = panels_ref.shape[1] // 2
-    barrier = pltpu.get_barrier_semaphore()
-    for neighbour in (left, right, partner):
-        pl.semaphore_signal(barrier, inc=1, device_id={"tp": neighbour}, device_id_type=MESH)
-    for step in range(1, groups):
-        peer = lax.rem(here + step, groups)
-        pl.semaphore_signal(barrier, inc=1, device_id={"grp": peer}, device_id_type=MESH)
-    pl.semaphore_wait(barrier, 2 + groups)
+    if greet:
+        barrier = pltpu.get_barrier_semaphore()
+        for neighbour in (left, right, partner):
+            pl.semaphore_signal(barrier, inc=1, device_id={"tp": neighbour}, device_id_type=MESH)
+        for step in range(1, groups):
+            peer = lax.rem(here + step, groups)
+            pl.semaphore_signal(barrier, inc=1, device_id={"grp": peer}, device_id_type=MESH)
+        pl.semaphore_wait(barrier, 2 + groups)
 
     def rows_of(slot, which):
         return panels_ref.at[slot, pl.ds(pl.multiple_of(which * half, 16), half)]
@@ -262,18 +264,20 @@
 
 
 def tail_kernel(count, scale, tokens_ref, gathered_hbm, lengths_ref, out_ref,
-                gathered, load_sem, part_ref, partner_part, mine, theirs, staged, landed, send_sems, recv_sems):
+                gathered, load_sem, part_ref, partner_part, mine, theirs, staged, landed, send_sems, recv_sems,
+                greet=True):
     width = landed.shape[-1]
     me = lax.axis_index("tp")
     partner = me + 1 - 2 * (me % 2)
     across = me + 2 - 4 * ((me // 2) % 2)
-    load = pltpu.make_async_copy(gathered_hbm, gathered, load_sem)
-    load.start()
-    barrier = pltpu.get_barrier_semaphore()
-    for step in range(1, count):
-        peer = lax.rem(me + step, count)
-        pl.semaphore_signal(barrier, inc=1, device_id={"tp": peer}, device_id_type=MESH)
-    load.wait()
+    if greet:
+        load = pltpu.make_async_copy(gathered_hbm, gathered, load_sem)
+        load.start()
+        barrier = pltpu.get_barrier_semaphore()
+        for step in range(1, count):
+            peer = lax.rem(me + step, count)
+            pl.semaphore_signal(barrier, inc=1, device_id={"tp": peer}, device_id_type=MESH)
+        load.wait()
     core = me % 2
     half = gathered.shape[1] // 3
     sources = gathered.shape[0]
@@ -299,7 +303,8 @@
         )
     part_ref[...] = projected[:, width:]
     query = projected[:, :width].astype(jnp.bfloat16)
-    pl.semaphore_wait(barrier, count - 1)
+    if greet:
+        pl.semaphore_wait(barrier, count - 1)
     first = pltpu.make_async_remote_copy(
         src_ref=part_ref, dst_ref=partner_part, send_sem=send_sems.at[0], recv_sem=recv_sems.at[0],
         device_id={"tp": partner}, device_id_type=MESH,
@@ -386,6 +391,61 @@
     )(tokens, gathered, lengths)
 
 
+def whole_kernel(count, groups, scale, panels_ref, home_ref, tokens_ref, lengths_ref, out_ref, *scratch):
+    ring_scratch, gathered, tail_scratch = scratch[:10], scratch[10], scratch[11:]
+    me = lax.axis_index("tp")
+    here = lax.axis_index("grp")
+    total = 2 * count
+    barrier = pltpu.get_barrier_semaphore()
+    for step in range(1, total):
+        peer = lax.rem(me + step, total)
+        pl.semaphore_signal(barrier, inc=1, device_id={"tp": peer}, device_id_type=MESH)
+    for step in range(1, groups):
+        peer = lax.rem(here + step, groups)
+        pl.semaphore_signal(barrier, inc=1, device_id={"grp": peer}, device_id_type=MESH)
+    pl.semaphore_wait(barrier, total + groups - 2)
+    chip_ring_kernel(count, groups, panels_ref, home_ref, gathered, *ring_scratch, greet=False)
+    tail_kernel(total, scale, tokens_ref, None, lengths_ref, out_ref, gathered, None, *tail_scratch, greet=False)
+
+
+def whole(panels, home, tokens, lengths, count, groups, collective_id):
+    slots, rows, width = panels.shape
+    seq = tokens.shape[0]
+    total = 2 * count
+    out_rows = seq // total
+    part = (seq, width)
+    vmem = pl.BlockSpec(memory_space=pltpu.VMEM)
+    smem = pl.BlockSpec(memory_space=pltpu.SMEM)
+    return pl.pallas_call(
+        functools.partial(whole_kernel, count, groups, width ** (-0.5)),
+        out_shape=jax.ShapeDtypeStruct((out_rows, total * width), jnp.float32),
+        in_specs=[vmem, smem, vmem, smem],
+        out_specs=vmem,
+        scratch_shapes=[
+            pltpu.VMEM((count, 2 * slots, rows // 2, width), panels.dtype),
+            pltpu.SemaphoreType.DMA((2, count // 2 + 1, 2 * slots)),
+            pltpu.SemaphoreType.DMA((count, 2 * slots)),
+            pltpu.VMEM((rows, width), panels.dtype),
+            pltpu.VMEM((rows // 2, width), panels.dtype),
+            pltpu.VMEM((rows // 2, width), panels.dtype),
+            pltpu.SemaphoreType.DMA((2, groups)),
+            pltpu.SemaphoreType.DMA((2, groups)),
+            pltpu.SemaphoreType.DMA((2,)),
+            pltpu.SemaphoreType.DMA((2,)),
+            pltpu.VMEM((groups, rows + rows // 2, width), panels.dtype),
+            pltpu.VMEM(part, jnp.float32),
+            pltpu.VMEM(part, jnp.float32),
+            pltpu.VMEM(part, jnp.bfloat16),
+            pltpu.VMEM(part, jnp.bfloat16),
+            pltpu.VMEM((total, out_rows, width), jnp.float32),
+            pltpu.VMEM((total, out_rows, width), jnp.float32),
+            pltpu.SemaphoreType.DMA((total + 1,)),
+            pltpu.SemaphoreType.DMA((total + 1,)),
+        ],
+        compiler_params=pltpu.CompilerParams(collective_id=collective_id, has_side_effects=True),
+    )(panels, home, tokens, lengths)
+
+
 def grid_kernel(width, send_ref, out_ref, landed, send_sems, recv_sems):
     me = lax.axis_index("grp")
     core = lax.axis_index("tp") % 2
@@ -638,8 +698,7 @@
     half_rows = block_rows // 2
     seq_total = tokens.shape[0]
 
-    gathered = chip_ring_gather(trainer_panels, panel_home, tp_count // 2, grp_count, 2)
-    return tail(tokens, gathered, lengths, tp_count, 1)
+    return whole(trainer_panels, panel_home, tokens, lengths, tp_count // 2, grp_count, 4)
 
 
 def solution(mesh):

time: 103 us -> 100 us (0.971)
  Pallas kernels: 101 us -> 98.4 us
    pallas_call x2 -> x1, Pallas kernels: 101 us -> 98.4 us  [whole(): pl.pallas_call(functools.partial(whole_kernel, count, groups, width ** (-...]
where the time goes in v21:
time: 100 us
  Pallas kernels  98.4 us (98%)
  local copies, waits for them, and re-layouts  1.67 us (2%)
    pallas_call x1, Pallas kernels, whole(): pl.pallas_call(functools.partial(whole_kernel, count, groups, width ** (-...  98.4 us

profile of v21, /device:TPU:1, one launch (start us, length us, event | category | flops | bytes accessed | tf_op | source)
XLA Modules:
  0.0 100.1 jit_solution(834850805040894296)
XLA Ops:
  0.0 98.4 %shard_map.46 = f32[12,4096]{1,0:T(8,128)} custom-call(bf16[2,320,128]{2,1,0:T(8,128)(2,1)} %panels_ref.1, s32[48]{0:T(128)} %home_ref.1, bf16[384,5120]{1,0:T(8,128)(2,1)} %tokens_ref.1, s32[1,4]{1,0:T(1,128)} %lengths_ref.1), custom_call_target="tpu_custom_call" | custom-call | tf_op jit(solution)/shard_map/pallas_call | solution.py:419
  98.4 1.7 %copy.6 = f32[12,4096]{1,0:T(8,128)} copy(f32[12,4096]{1,0:T(8,128)} %shard_map.46) | data formatting | bytes 393216

commit v22 on v21

--- a/solution.py
+++ b/solution.py
@@ -171,7 +171,7 @@
         recv_sem=partner_sems.at[1], device_id={"tp": partner}, device_id_type=MESH,
     )
     to_partner.start()
-    copies = []
+    copies, local_copies = [], []
 
     def spread(part, source, window):
         for step in range(1, groups):
@@ -188,13 +188,39 @@
             copies.append(copy)
         local = pltpu.make_async_copy(source, out_ref.at[here, window], local_sems.at[part])
         local.start()
-        copies.append(local)
+        local_copies.append(local)
 
     spread(0, own_ref, pl.ds(0, 2 * half))
     to_partner.wait()
     spread(1, partner_rows, pl.ds(2 * half, half))
-    for copy in copies:
+    for copy in local_copies:
         copy.wait()
+    if greet:
+        for copy in copies:
+            copy.wait()
+        return None
+    windows = [(own_ref, pl.ds(0, 2 * half)), (partner_rows, pl.ds(2 * half, half))]
+
+    def arrive(source):
+        step = lax.rem(here + groups - source, groups)
+
+        @pl.when(step != 0)
+        def _():
+            for part, (shape_ref, window) in enumerate(windows):
+                pltpu.make_async_remote_copy(
+                    src_ref=shape_ref,
+                    dst_ref=out_ref.at[here, window],
+                    send_sem=grp_send_sems.at[part, 0],
+                    recv_sem=grp_recv_sems.at[part, step],
+                    device_id={"grp": lax.rem(here + 1, groups)},
+                    device_id_type=MESH,
+                ).wait_recv()
+
+    def finish():
+        for copy in copies:
+            copy.wait_send()
+
+    return arrive, finish
 
 
 def chip_ring_gather(panels, home, count, groups, collective_id):
@@ -265,7 +291,7 @@
 
 def tail_kernel(count, scale, tokens_ref, gathered_hbm, lengths_ref, out_ref,
                 gathered, load_sem, part_ref, partner_part, mine, theirs, staged, landed, send_sems, recv_sems,
-                greet=True):
+                greet=True, arrive=None):
     width = landed.shape[-1]
     me = lax.axis_index("tp")
     partner = me + 1 - 2 * (me % 2)
@@ -284,6 +310,9 @@
     first_half = core == 0
     projected = jnp.zeros((tokens_ref.shape[0], 2 * width), jnp.float32)
     for pair in range(sources // 2):
+        if arrive is not None:
+            arrive(2 * pair)
+            arrive(2 * pair + 1)
         q_parts, kv_parts = [], []
         for source in (2 * pair, 2 * pair + 1):
             here = gathered[source, 0:half]
@@ -404,8 +433,10 @@
         peer = lax.rem(here + step, groups)
         pl.semaphore_signal(barrier, inc=1, device_id={"grp": peer}, device_id_type=MESH)
     pl.semaphore_wait(barrier, total + groups - 2)
-    chip_ring_kernel(count, groups, panels_ref, home_ref, gathered, *ring_scratch, greet=False)
-    tail_kernel(total, scale, tokens_ref, None, lengths_ref, out_ref, gathered, None, *tail_scratch, greet=False)
+    arrive, finish = chip_ring_kernel(count, groups, panels_ref, home_ref, gathered, *ring_scratch, greet=False)
+    tail_kernel(total, scale, tokens_ref, None, lengths_ref, out_ref, gathered, None, *tail_scratch, greet=False,
+                arrive=arrive)
+    finish()
 
 
 def whole(panels, home, tokens, lengths, count, groups, collective_id):

time: 100 us -> 100 us (level)
  no operation moved by 1% of the time
where the time goes in v22:
time: 100 us
  Pallas kernels  98.4 us (98%)
  local copies, waits for them, and re-layouts  1.67 us (2%)
    pallas_call x1, Pallas kernels, whole(): pl.pallas_call(functools.partial(whole_kernel, count, groups, width ** (-...  98.4 us

profile of v22, /device:TPU:1, one launch (start us, length us, event | category | flops | bytes accessed | tf_op | source)
XLA Modules:
  0.0 100.0 jit_solution(5349210213985926859)
XLA Ops:
  0.0 98.4 %shard_map.46 = f32[12,4096]{1,0:T(8,128)} custom-call(bf16[2,320,128]{2,1,0:T(8,128)(2,1)} %panels_ref.1, s32[48]{0:T(128)} %home_ref.1, bf16[384,5120]{1,0:T(8,128)(2,1)} %tokens_ref.1, s32[1,4]{1,0:T(1,128)} %lengths_ref.1), custom_call_target="tpu_custom_call" | custom-call | tf_op jit(solution)/shard_map/pallas_call | solution.py:450
  98.4 1.7 %copy.6 = f32[12,4096]{1,0:T(8,128)} copy(f32[12,4096]{1,0:T(8,128)} %shard_map.46) | data formatting | bytes 393216

commit v23 on v22

--- a/solution.py
+++ b/solution.py
@@ -351,45 +351,73 @@
     keys = jnp.where(holds_k, mine[...], theirs[...])
     values = jnp.where(holds_k, theirs[...], mine[...])
 
-    scores = lax.dot_general(
-        query, keys, (((1,), (1,)), ((), ())), preferred_element_type=jnp.float32
-    ) * scale
-    seq = scores.shape[0]
-    row = lax.broadcasted_iota(jnp.int32, (seq, seq), 0)
-    col = lax.broadcasted_iota(jnp.int32, (seq, seq), 1)
-    row_segment = jnp.zeros((seq, seq), jnp.int32)
-    col_segment = jnp.zeros((seq, seq), jnp.int32)
+    seq = query.shape[0]
+    rows = seq // count
+    blocks = 4
+    block_rows = seq // blocks
+    col = lax.broadcasted_iota(jnp.int32, (block_rows, seq), 1)
+    col_segment = jnp.zeros((block_rows, seq), jnp.int32)
+    bounds = []
     bound = lengths_ref[0, 0] * 0
     for response in range(lengths_ref.shape[1]):
         bound = bound + lengths_ref[0, response]
-        row_segment = row_segment + (row >= bound).astype(jnp.int32)
+        bounds.append(bound)
         col_segment = col_segment + (col >= bound).astype(jnp.int32)
-    allowed = (row_segment == col_segment) & (col <= row)
-    masked = jnp.where(allowed, scores, -jnp.inf)
-    peak = jnp.max(masked, axis=1, keepdims=True)
-    weights = jnp.exp(masked - peak)
-    probs = (weights / jnp.sum(weights, axis=1, keepdims=True)).astype(jnp.bfloat16)
-    context = jnp.dot(probs, values, preferred_element_type=jnp.float32)
-    rows = seq // count
-    for target in range(count):
-        staged[target] = context[target * rows:(target + 1) * rows]
-
     copies = []
-    for step in range(1, count):
-        peer = lax.rem(me + step, count)
-        copy = pltpu.make_async_remote_copy(
-            src_ref=staged.at[peer],
-            dst_ref=landed.at[me],
-            send_sem=send_sems.at[1 + step],
-            recv_sem=recv_sems.at[1 + step],
-            device_id={"tp": peer},
+    for block in range(blocks):
+        first_row = block * block_rows
+        scores = lax.dot_general(
+            query[first_row:first_row + block_rows], keys, (((1,), (1,)), ((), ())),
+            preferred_element_type=jnp.float32,
+        ) * scale
+        row = lax.broadcasted_iota(jnp.int32, (block_rows, seq), 0) + first_row
+        row_segment = jnp.zeros((block_rows, seq), jnp.int32)
+        for bound in bounds:
+            row_segment = row_segment + (row >= bound).astype(jnp.int32)
+        allowed = (row_segment == col_segment) & (col <= row)
+        masked = jnp.where(allowed, scores, -jnp.inf)
+        peak = jnp.max(masked, axis=1, keepdims=True)
+        weights = jnp.exp(masked - peak)
+        probs = (weights / jnp.sum(weights, axis=1, keepdims=True)).astype(jnp.bfloat16)
+        context = jnp.dot(probs, values, preferred_element_type=jnp.float32)
+        per_block = block_rows // rows
+        for i in range(per_block):
+            target = block * per_block + i
+            staged[target] = context[i * rows:(i + 1) * rows]
+        for i in range(per_block):
+            target = block * per_block + i
+            copy = pltpu.make_async_remote_copy(
+                src_ref=staged.at[target],
+                dst_ref=landed.at[me],
+                send_sem=send_sems.at[2 + target],
+                recv_sem=recv_sems.at[2 + me],
+                device_id={"tp": target},
+                device_id_type=MESH,
+            )
+
+            @pl.when(target != me)
+            def _():
+                copy.start()
+
+            copies.append((target, copy))
+    landed[me] = staged[me]
+    for target, copy in copies:
+        @pl.when(target != me)
+        def _():
+            copy.wait_send()
+    for source in range(count):
+        incoming = pltpu.make_async_remote_copy(
+            src_ref=staged.at[source],
+            dst_ref=landed.at[source],
+            send_sem=send_sems.at[0],
+            recv_sem=recv_sems.at[2 + source],
+            device_id={"tp": partner},
             device_id_type=MESH,
         )
-        copy.start()
-        copies.append(copy)
-    landed[me] = staged[me]
-    for copy in copies:
-        copy.wait()
+
+        @pl.when(source != me)
+        def _():
+            incoming.wait_recv()
     for source in range(count):
         out_ref[:, source * width:(source + 1) * width] = landed[source]
 
@@ -470,8 +498,8 @@
             pltpu.VMEM(part, jnp.bfloat16),
             pltpu.VMEM((total, out_rows, width), jnp.float32),
             pltpu.VMEM((total, out_rows, width), jnp.float32),
-            pltpu.SemaphoreType.DMA((total + 1,)),
-            pltpu.SemaphoreType.DMA((total + 1,)),
+            pltpu.SemaphoreType.DMA((total + 2,)),
+            pltpu.SemaphoreType.DMA((total + 2,)),
         ],
         compiler_params=pltpu.CompilerParams(collective_id=collective_id, has_side_effects=True),
     )(panels, home, tokens, lengths)

time: 100 us -> 95 us (0.950)
  Pallas kernels: 98.4 us -> 93.2 us
    pallas_call x1, Pallas kernels: 98.4 us -> 93.2 us  [whole(): pl.pallas_call(functools.partial(whole_kernel, count, groups, width ** (-...]
where the time goes in v23:
time: 95 us; the launch traced here: 94.9 us
  Pallas kernels  93.2 us (98%)
  local copies, waits for them, and re-layouts  1.67 us (2%)
    pallas_call x1, Pallas kernels, whole(): pl.pallas_call(functools.partial(whole_kernel, count, groups, width ** (-...  93.2 us

profile of v23, /device:TPU:1, one launch (start us, length us, event | category | flops | bytes accessed | tf_op | source)
XLA Modules:
  0.0 94.9 jit_solution(1630974999207510055)
XLA Ops:
  0.0 93.2 %shard_map.46 = f32[12,4096]{1,0:T(8,128)} custom-call(bf16[2,320,128]{2,1,0:T(8,128)(2,1)} %panels_ref.1, s32[48]{0:T(128)} %home_ref.1, bf16[384,5120]{1,0:T(8,128)(2,1)} %tokens_ref.1, s32[1,4]{1,0:T(1,128)} %lengths_ref.1), custom_call_target="tpu_custom_call" | custom-call | tf_op jit(solution)/shard_map/pallas_call | solution.py:478
  93.2 1.7 %copy.6 = f32[12,4096]{1,0:T(8,128)} copy(f32[12,4096]{1,0:T(8,128)} %shard_map.46) | data formatting | bytes 393216

commit v24 on v23

--- a/solution.py
+++ b/solution.py
@@ -353,7 +353,7 @@
 
     seq = query.shape[0]
     rows = seq // count
-    blocks = 4
+    blocks = 8
     block_rows = seq // blocks
     col = lax.broadcasted_iota(jnp.int32, (block_rows, seq), 1)
     col_segment = jnp.zeros((block_rows, seq), jnp.int32)

time: 95 us -> 95.4 us (level)
  no operation moved by 1% of the time
where the time goes in v24:
time: 95.4 us; the launch traced here: 94.8 us
  Pallas kernels  93.1 us (98%)
  local copies, waits for them, and re-layouts  1.67 us (2%)
    pallas_call x1, Pallas kernels, whole(): pl.pallas_call(functools.partial(whole_kernel, count, groups, width ** (-...  93.1 us

profile of v24, /device:TPU:1, one launch (start us, length us, event | category | flops | bytes accessed | tf_op | source)
XLA Modules:
  0.0 94.8 jit_solution(7886391826397060124)
XLA Ops:
  0.0 93.1 %shard_map.46 = f32[12,4096]{1,0:T(8,128)} custom-call(bf16[2,320,128]{2,1,0:T(8,128)(2,1)} %panels_ref.1, s32[48]{0:T(128)} %home_ref.1, bf16[384,5120]{1,0:T(8,128)(2,1)} %tokens_ref.1, s32[1,4]{1,0:T(1,128)} %lengths_ref.1), custom_call_target="tpu_custom_call" | custom-call | tf_op jit(solution)/shard_map/pallas_call | solution.py:478
  93.1 1.7 %copy.6 = f32[12,4096]{1,0:T(8,128)} copy(f32[12,4096]{1,0:T(8,128)} %shard_map.46) | data formatting | bytes 393216

commit v25 on v23

--- a/solution.py
+++ b/solution.py
@@ -355,31 +355,32 @@
     rows = seq // count
     blocks = 4
     block_rows = seq // blocks
-    col = lax.broadcasted_iota(jnp.int32, (block_rows, seq), 1)
-    col_segment = jnp.zeros((block_rows, seq), jnp.int32)
     bounds = []
     bound = lengths_ref[0, 0] * 0
     for response in range(lengths_ref.shape[1]):
         bound = bound + lengths_ref[0, response]
         bounds.append(bound)
-        col_segment = col_segment + (col >= bound).astype(jnp.int32)
     copies = []
     for block in range(blocks):
         first_row = block * block_rows
+        seen = first_row + block_rows
         scores = lax.dot_general(
-            query[first_row:first_row + block_rows], keys, (((1,), (1,)), ((), ())),
+            query[first_row:seen], keys[0:seen], (((1,), (1,)), ((), ())),
             preferred_element_type=jnp.float32,
         ) * scale
-        row = lax.broadcasted_iota(jnp.int32, (block_rows, seq), 0) + first_row
-        row_segment = jnp.zeros((block_rows, seq), jnp.int32)
+        row = lax.broadcasted_iota(jnp.int32, (block_rows, seen), 0) + first_row
+        col = lax.broadcasted_iota(jnp.int32, (block_rows, seen), 1)
+        row_segment = jnp.zeros((block_rows, seen), jnp.int32)
+        col_segment = jnp.zeros((block_rows, seen), jnp.int32)
         for bound in bounds:
             row_segment = row_segment + (row >= bound).astype(jnp.int32)
+            col_segment = col_segment + (col >= bound).astype(jnp.int32)
         allowed = (row_segment == col_segment) & (col <= row)
         masked = jnp.where(allowed, scores, -jnp.inf)
         peak = jnp.max(masked, axis=1, keepdims=True)
         weights = jnp.exp(masked - peak)
         probs = (weights / jnp.sum(weights, axis=1, keepdims=True)).astype(jnp.bfloat16)
-        context = jnp.dot(probs, values, preferred_element_type=jnp.float32)
+        context = jnp.dot(probs, values[0:seen], preferred_element_type=jnp.float32)
         per_block = block_rows // rows
         for i in range(per_block):
             target = block * per_block + i

time: 95 us -> 95.5 us (level)
  no operation moved by 1% of the time
where the time goes in v25:
time: 95.5 us; the launch traced here: 95.4 us
  Pallas kernels  93.7 us (98%)
  local copies, waits for them, and re-layouts  1.67 us (2%)
    pallas_call x1, Pallas kernels, whole(): pl.pallas_call(functools.partial(whole_kernel, count, groups, width ** (-...  93.7 us

profile of v25, /device:TPU:1, one launch (start us, length us, event | category | flops | bytes accessed | tf_op | source)
XLA Modules:
  0.0 95.4 jit_solution(4385993159780069407)
XLA Ops:
  0.0 93.7 %shard_map.46 = f32[12,4096]{1,0:T(8,128)} custom-call(bf16[2,320,128]{2,1,0:T(8,128)(2,1)} %panels_ref.1, s32[48]{0:T(128)} %home_ref.1, bf16[384,5120]{1,0:T(8,128)(2,1)} %tokens_ref.1, s32[1,4]{1,0:T(1,128)} %lengths_ref.1), custom_call_target="tpu_custom_call" | custom-call | tf_op jit(solution)/shard_map/pallas_call | solution.py:479
  93.7 1.7 %copy.6 = f32[12,4096]{1,0:T(8,128)} copy(f32[12,4096]{1,0:T(8,128)} %shard_map.46) | data formatting | bytes 393216

commit v26 on v23

--- a/solution.py
+++ b/solution.py
@@ -149,8 +149,9 @@
     for chunk in range(4):
         incoming(lax.rem(spot + count - far_right, count), chunk).wait_recv()
         incoming(lax.rem(spot + far_left, count), chunk).wait_recv()
-    for copy in sends:
-        copy.wait_send()
+    if greet:
+        for copy in sends:
+            copy.wait_send()
     heads = total
     kv_heads = (home_ref.shape[0] - heads) // 2
     group = heads // kv_heads
@@ -217,7 +218,7 @@
                 ).wait_recv()
 
     def finish():
-        for copy in copies:
+        for copy in sends + copies:
             copy.wait_send()
 
     return arrive, finish

time: 95 us -> 95 us (level)
  no operation moved by 1% of the time
where the time goes in v26:
time: 95 us; the launch traced here: 94.8 us
  Pallas kernels  93.2 us (98%)
  local copies, waits for them, and re-layouts  1.67 us (2%)
    pallas_call x1, Pallas kernels, whole(): pl.pallas_call(functools.partial(whole_kernel, count, groups, width ** (-...  93.2 us

profile of v26, /device:TPU:1, one launch (start us, length us, event | category | flops | bytes accessed | tf_op | source)
XLA Modules:
  0.0 94.8 jit_solution(10933457341925486923)
XLA Ops:
  0.0 93.2 %shard_map.46 = f32[12,4096]{1,0:T(8,128)} custom-call(bf16[2,320,128]{2,1,0:T(8,128)(2,1)} %panels_ref.1, s32[48]{0:T(128)} %home_ref.1, bf16[384,5120]{1,0:T(8,128)(2,1)} %tokens_ref.1, s32[1,4]{1,0:T(1,128)} %lengths_ref.1), custom_call_target="tpu_custom_call" | custom-call | tf_op jit(solution)/shard_map/pallas_call | solution.py:479
  93.2 1.7 %copy.6 = f32[12,4096]{1,0:T(8,128)} copy(f32[12,4096]{1,0:T(8,128)} %shard_map.46) | data formatting | bytes 393216
